TPU v7x, 32 devices: a whole 2x2x4 slice. The times are simulated.
32 devices in a mesh: lon: 32 (over z, y, x, core).
Axes of the slice: x: 2, y: 2, z: 4, core: 2. Of those that a mesh axis runs over, the one named last changes fastest.
Arguments:
- field: float32 [16, 1664, 200], P(None, 'lon'), may hold values from -6 to 6
- south_rows: float32 [8, 1664, 200], P(None, 'lon'), may hold values from -6 to 6
- sign_mask: int32 [200], replicated, may hold values from -1 to 1, as said below
- weights: float32 [4, 9, 200, 200], replicated, may hold values from -0.125 to 0.125
- biases: float32 [4, 200], replicated, may hold values from -3 to 3
Outputs:
- result: float32 [16, 1664, 200], P(None, 'lon')
Inputs may be any that keep to these rules, and one draw needn't show every extreme that they name: `sign_mask`: every entry is +1 or -1.
All inputs are finite; a program needn't handle non-finite values.
Results may differ from a plain program's by a relative error of at most 0.0001.
Values sent between devices are 32-bit elements; how exact they have to be, the bound alone decides.
No kernel may reach another device: no remote copies, remote signals or barrier semaphores. Data moves between devices by JAX's collectives and lax.ppermute only.
A program may use at most 64 MiB of HBM per device.

v0:
```python
import jax
import jax.numpy as jnp
from jax import lax
from jax.sharding import PartitionSpec as P


def swapped(block, axis, distance):
    count = lax.axis_size(axis)
    route = []
    for low in range(count):
        high = low | 1 << distance
        if high != low and high < count:
            route += [(low, high), (high, low)]
    return lax.ppermute(block, axis, route)


def padded_2(cells, sides, width):
    for axis, dim in sides:
        count = lax.axis_size(axis)
        head = lax.slice_in_dim(cells, 0, width, axis=dim)
        tail = lax.slice_in_dim(cells, cells.shape[dim] - width, cells.shape[dim], axis=dim)
        cells = jnp.concatenate(
            [
                lax.ppermute(tail, axis, [(i, (i + 1) % count) for i in range(count)]),
                cells,
                lax.ppermute(head, axis, [((i + 1) % count, i) for i in range(count)]),
            ],
            axis=dim,
        )
    return cells


def convolve(padded, kernel, offset, dilate, row_count, col_count):
    summed = jnp.zeros((row_count, col_count, kernel.shape[-1]), jnp.float32)
    for tap_row in range(3):
        for tap_col in range(3):
            window = padded[
                tap_row * dilate : tap_row * dilate + row_count,
                tap_col * dilate : tap_col * dilate + col_count,
            ]
            summed = summed + jnp.einsum(
                "rlc,cd->rld",
                window,
                kernel[3 * tap_row + tap_col],
                precision=lax.Precision.HIGHEST,
            )
    return summed + offset


def local(field, south_rows, sign_mask, weights, biases):
    row_count, col_count = (field.shape[0], field.shape[1])
    channel_signs = sign_mask.astype(jnp.float32)
    hop_count = lax.axis_size("lon").bit_length() - 1
    bit_list = list(range(hop_count))
    for layer_index in range(weights.shape[0]):
        dilate = 2**layer_index
        south_part = south_rows[south_rows.shape[0] - dilate :]
        north_rows = (field[row_count - dilate :][::-1] * channel_signs)[:, ::-1]
        for bit_number in bit_list:
            north_rows = swapped(north_rows, "lon", bit_number)
        stacked = jnp.concatenate([south_part, field, north_rows], 0)
        padded = padded_2(stacked, (("lon", 1),), dilate)
        field = field + jax.nn.gelu(
            convolve(
                padded, weights[layer_index], biases[layer_index], dilate, row_count, col_count
            )
        )
    return field


def solution(mesh):
    in_specs = (P(None, "lon", None), P(None, "lon", None), P(), P(), P())
    out_specs = P(None, "lon", None)
    return jax.shard_map(local, mesh=mesh, in_specs=in_specs, out_specs=out_specs, check_vma=False)
```

profile of v0, /device:TPU:0, one launch (start us, length us, event | category | flops | bytes accessed | tf_op | source)
XLA Modules:
  0.0 225.1 jit_solution(17179112630037606763)
XLA Ops:
  4.0 2.8 %collective-permute-start.1 = (f32[1,52,200]{2,1,0:T(8,128)S(1)}, f32[1,52,200]{2,1,0:T(8,128)S(1)}, u32[]{:S(2)}, u32[]{:S(2)}) collective-permute-start(f32[1,52,200]{2,1,0:T(8,128)S(1)} %collective-permute-done), channel_id=1, source_target_pairs={{0,2},{2,0},{1,3},{3,1},{4,6},{6,4},{5,7},{7,5},{8,10},{10,8},{9,1... | collective-permute-start | bytes 124808 | tf_op jit(solution)/shard_map/ppermute | solution.py:14
  6.8 2.2 collective-permute-done.1
  17.7 3.2 %collective-permute-start.4 = (f32[1,52,200]{2,1,0:T(8,128)S(1)}, f32[1,52,200]{2,1,0:T(8,128)S(1)}, u32[]{:S(2)}, u32[]{:S(2)}) collective-permute-start(f32[1,52,200]{2,1,0:T(8,128)S(1)} %collective-permute-done.3), channel_id=1, source_target_pairs={{0,16},{16,0},{1,17},{17,1},{2,18},{18,2},{3,19},{19,3},{4,20},{20... | collective-permute-start | bytes 124808 | tf_op jit(solution)/shard_map/ppermute | solution.py:14
  23.1 5.6 %collective-permute-start.6 = (f32[18,1,200]{2,1,0:T(1,128)S(1)}, f32[18,1,200]{2,1,0:T(1,128)S(1)}, u32[]{:S(2)}, u32[]{:S(2)}) collective-permute-start(f32[18,1,200]{2,1,0:T(1,128)S(1)} %get-tuple-element.20), channel_id=1, source_target_pairs={{1,0},{2,1},{3,2},{4,3},{5,4},{6,5},{7,6},{8,7},{9,8},{10,9},{11,1... | collective-permute-start | bytes 43208 | tf_op jit(solution)/shard_map/ppermute | solution.py:26
  45.1 5.2 %collective-permute-done.8 = f32[2,52,200]{2,1,0:T(8,128)S(1)} collective-permute-done((f32[2,52,200]{2,1,0:T(8,128)S(1)}, f32[2,52,200]{2,1,0:T(8,128)S(1)}, u32[]{:S(2)}, u32[]{:S(2)}) %collective-permute-start.8) | collective-permute-done | bytes 83232 | tf_op jit(solution)/shard_map/ppermute | solution.py:14
  51.1 4.0 %collective-permute-done.9 = f32[2,52,200]{2,1,0:T(8,128)S(1)} collective-permute-done((f32[2,52,200]{2,1,0:T(8,128)S(1)}, f32[2,52,200]{2,1,0:T(8,128)S(1)}, u32[]{:S(2)}, u32[]{:S(2)}) %collective-permute-start.9) | collective-permute-done | bytes 83232 | tf_op jit(solution)/shard_map/ppermute | solution.py:14
  56.3 3.6 %collective-permute-done.10 = f32[2,52,200]{2,1,0:T(8,128)S(1)} collective-permute-done((f32[2,52,200]{2,1,0:T(8,128)S(1)}, f32[2,52,200]{2,1,0:T(8,128)S(1)}, u32[]{:S(2)}, u32[]{:S(2)}) %collective-permute-start.10) | collective-permute-done | bytes 83232 | tf_op jit(solution)/shard_map/ppermute | solution.py:14
  59.9 2.3 %collective-permute-start.11 = (f32[2,52,200]{2,1,0:T(8,128)S(1)}, f32[2,52,200]{2,1,0:T(8,128)S(1)}, u32[]{:S(2)}, u32[]{:S(2)}) collective-permute-start(f32[2,52,200]{2,1,0:T(8,128)S(1)} %collective-permute-done.10), channel_id=1, source_target_pairs={{0,16},{16,0},{1,17},{17,1},{2,18},{18,2},{3,19},{19,3},{4,20},{20... | collective-permute-start | bytes 249608 | tf_op jit(solution)/shard_map/ppermute | solution.py:14
  64.0 2.8 %collective-permute-done.11 = f32[2,52,200]{2,1,0:T(8,128)S(1)} collective-permute-done((f32[2,52,200]{2,1,0:T(8,128)S(1)}, f32[2,52,200]{2,1,0:T(8,128)S(1)}, u32[]{:S(2)}, u32[]{:S(2)}) %collective-permute-start.11) | collective-permute-done | bytes 83232 | tf_op jit(solution)/shard_map/ppermute | solution.py:14
  66.9 5.8 %collective-permute-start.13 = (f32[20,2,200]{2,1,0:T(2,128)S(1)}, f32[20,2,200]{2,1,0:T(2,128)S(1)}, u32[]{:S(2)}, u32[]{:S(2)}) collective-permute-start(f32[20,2,200]{2,1,0:T(2,128)S(1)} %get-tuple-element.16), channel_id=1, source_target_pairs={{1,0},{2,1},{3,2},{4,3},{5,4},{6,5},{7,6},{8,7},{9,8},{10,9},{11,1... | collective-permute-start | bytes 96008 | tf_op jit(solution)/shard_map/ppermute | solution.py:26
  89.9 7.6 %collective-permute-done.15 = f32[4,52,200]{2,1,0:T(8,128)S(1)} collective-permute-done((f32[4,52,200]{2,1,0:T(8,128)S(1)}, f32[4,52,200]{2,1,0:T(8,128)S(1)}, u32[]{:S(2)}, u32[]{:S(2)}) %collective-permute-start.15) | collective-permute-done | bytes 166432 | tf_op jit(solution)/shard_map/ppermute | solution.py:14
  97.5 6.8 %collective-permute-done.16 = f32[4,52,200]{2,1,0:T(8,128)S(1)} collective-permute-done((f32[4,52,200]{2,1,0:T(8,128)S(1)}, f32[4,52,200]{2,1,0:T(8,128)S(1)}, u32[]{:S(2)}, u32[]{:S(2)}) %collective-permute-start.16) | collective-permute-done | bytes 166432 | tf_op jit(solution)/shard_map/ppermute | solution.py:14
  106.1 4.2 %collective-permute-done.17 = f32[4,52,200]{2,1,0:T(8,128)S(1)} collective-permute-done((f32[4,52,200]{2,1,0:T(8,128)S(1)}, f32[4,52,200]{2,1,0:T(8,128)S(1)}, u32[]{:S(2)}, u32[]{:S(2)}) %collective-permute-start.17) | collective-permute-done | bytes 166432 | tf_op jit(solution)/shard_map/ppermute | solution.py:14
  110.3 3.1 %collective-permute-start.18 = (f32[4,52,200]{2,1,0:T(8,128)S(1)}, f32[4,52,200]{2,1,0:T(8,128)S(1)}, u32[]{:S(2)}, u32[]{:S(2)}) collective-permute-start(f32[4,52,200]{2,1,0:T(8,128)S(1)} %collective-permute-done.17), channel_id=1, source_target_pairs={{0,16},{16,0},{1,17},{17,1},{2,18},{18,2},{3,19},{19,3},{4,20},{20... | collective-permute-start | bytes 499208 | tf_op jit(solution)/shard_map/ppermute | solution.py:14
  115.3 7.5 %collective-permute-done.18 = f32[4,52,200]{2,1,0:T(8,128)S(1)} collective-permute-done((f32[4,52,200]{2,1,0:T(8,128)S(1)}, f32[4,52,200]{2,1,0:T(8,128)S(1)}, u32[]{:S(2)}, u32[]{:S(2)}) %collective-permute-start.18) | collective-permute-done | bytes 166432 | tf_op jit(solution)/shard_map/ppermute | solution.py:14
  122.9 5.5 %collective-permute-start.20 = (f32[24,4,200]{2,1,0:T(4,128)S(1)}, f32[24,4,200]{2,1,0:T(4,128)S(1)}, u32[]{:S(2)}, u32[]{:S(2)}) collective-permute-start(f32[24,4,200]{2,1,0:T(4,128)S(1)} %get-tuple-element.12), channel_id=1, source_target_pairs={{1,0},{2,1},{3,2},{4,3},{5,4},{6,5},{7,6},{8,7},{9,8},{10,9},{11,1... | collective-permute-start | bytes 230408 | tf_op jit(solution)/shard_map/ppermute | solution.py:26
  140.0 2.2 fusion.87
  144.5 12.6 %collective-permute-done.22 = f32[8,52,200]{2,1,0:T(8,128)S(1)} collective-permute-done((f32[8,52,200]{2,1,0:T(8,128)S(1)}, f32[8,52,200]{2,1,0:T(8,128)S(1)}, u32[]{:S(2)}, u32[]{:S(2)}) %collective-permute-start.22) | collective-permute-done | bytes 332832 | tf_op jit(solution)/shard_map/ppermute | solution.py:14
  157.2 11.5 %collective-permute-done.23 = f32[8,52,200]{2,1,0:T(8,128)S(1)} collective-permute-done((f32[8,52,200]{2,1,0:T(8,128)S(1)}, f32[8,52,200]{2,1,0:T(8,128)S(1)}, u32[]{:S(2)}, u32[]{:S(2)}) %collective-permute-start.23) | collective-permute-done | bytes 332832 | tf_op jit(solution)/shard_map/ppermute | solution.py:14
  168.7 10.8 %collective-permute-done.24 = f32[8,52,200]{2,1,0:T(8,128)S(1)} collective-permute-done((f32[8,52,200]{2,1,0:T(8,128)S(1)}, f32[8,52,200]{2,1,0:T(8,128)S(1)}, u32[]{:S(2)}, u32[]{:S(2)}) %collective-permute-start.24) | collective-permute-done | bytes 332832 | tf_op jit(solution)/shard_map/ppermute | solution.py:14
  179.6 3.5 %collective-permute-start.25 = (f32[8,52,200]{2,1,0:T(8,128)S(1)}, f32[8,52,200]{2,1,0:T(8,128)S(1)}, u32[]{:S(2)}, u32[]{:S(2)}) collective-permute-start(f32[8,52,200]{2,1,0:T(8,128)S(1)} %collective-permute-done.24), channel_id=1, source_target_pairs={{0,16},{16,0},{1,17},{17,1},{2,18},{18,2},{3,19},{19,3},{4,20},{20... | collective-permute-start | bytes 998408 | tf_op jit(solution)/shard_map/ppermute | solution.py:14
  186.7 15.5 %collective-permute-done.25 = f32[8,52,200]{2,1,0:T(8,128)S(1)} collective-permute-done((f32[8,52,200]{2,1,0:T(8,128)S(1)}, f32[8,52,200]{2,1,0:T(8,128)S(1)}, u32[]{:S(2)}, u32[]{:S(2)}) %collective-permute-start.25) | collective-permute-done | bytes 332832 | tf_op jit(solution)/shard_map/ppermute | solution.py:14
  202.3 5.5 %collective-permute-start.27 = (f32[32,8,200]{2,1,0:T(8,128)S(1)}, f32[32,8,200]{2,1,0:T(8,128)S(1)}, u32[]{:S(2)}, u32[]{:S(2)}) collective-permute-start(f32[32,8,200]{2,1,0:T(8,128)S(1)} %get-tuple-element.8), channel_id=1, source_target_pairs={{1,0},{2,1},{3,2},{4,3},{5,4},{6,5},{7,6},{8,7},{9,8},{10,9},{11,1... | collective-permute-start | bytes 614408 | tf_op jit(solution)/shard_map/ppermute | solution.py:26
  221.5 2.2 fusion.95
  (101 shorter events, 88.2 us)
Async XLA Ops:
  4.0 5.1 %collective-permute-start.1 = (f32[1,52,200]{2,1,0:T(8,128)S(1)}, f32[1,52,200]{2,1,0:T(8,128)S(1)}, u32[]{:S(2)}, u32[]{:S(2)}) collective-permute-start(f32[1,52,200]{2,1,0:T(8,128)S(1)} %collective-permute-done), channel_id=1, source_target_pairs={{0,2},{2,0},{1,3},{3,1},{4,6},{6,4},{5,7},{7,5},{8,10},{10,8},{9,1... | collective-permute-start | bytes 124808 | tf_op jit(solution)/shard_map/ppermute | solution.py:14
  9.1 4.2 %collective-permute-start.2 = (f32[1,52,200]{2,1,0:T(8,128)S(1)}, f32[1,52,200]{2,1,0:T(8,128)S(1)}, u32[]{:S(2)}, u32[]{:S(2)}) collective-permute-start(f32[1,52,200]{2,1,0:T(8,128)S(1)} %collective-permute-done.1), channel_id=1, source_target_pairs={{0,4},{4,0},{1,5},{5,1},{2,6},{6,2},{3,7},{7,3},{8,12},{12,8},{9,1... | collective-permute-start | bytes 124808 | tf_op jit(solution)/shard_map/ppermute | solution.py:14
  13.2 4.4 %collective-permute-start.3 = (f32[1,52,200]{2,1,0:T(8,128)S(1)}, f32[1,52,200]{2,1,0:T(8,128)S(1)}, u32[]{:S(2)}, u32[]{:S(2)}) collective-permute-start(f32[1,52,200]{2,1,0:T(8,128)S(1)} %collective-permute-done.2), channel_id=1, source_target_pairs={{0,8},{8,0},{1,9},{9,1},{2,10},{10,2},{3,11},{11,3},{4,12},{12,4},... | collective-permute-start | bytes 124808 | tf_op jit(solution)/shard_map/ppermute | solution.py:14
  17.7 5.3 %collective-permute-start.4 = (f32[1,52,200]{2,1,0:T(8,128)S(1)}, f32[1,52,200]{2,1,0:T(8,128)S(1)}, u32[]{:S(2)}, u32[]{:S(2)}) collective-permute-start(f32[1,52,200]{2,1,0:T(8,128)S(1)} %collective-permute-done.3), channel_id=1, source_target_pairs={{0,16},{16,0},{1,17},{17,1},{2,18},{18,2},{3,19},{19,3},{4,20},{20... | collective-permute-start | bytes 124808 | tf_op jit(solution)/shard_map/ppermute | solution.py:14
  23.1 6.8 %collective-permute-start.5 = (f32[18,1,200]{2,1,0:T(1,128)S(1)}, f32[18,1,200]{2,1,0:T(1,128)S(1)}, u32[]{:S(2)}, u32[]{:S(2)}) collective-permute-start(f32[18,1,200]{2,1,0:T(1,128)S(1)} %get-tuple-element.19), channel_id=1, source_target_pairs={{0,1},{1,2},{2,3},{3,4},{4,5},{5,6},{6,7},{7,8},{8,9},{9,10},{10,1... | collective-permute-start | bytes 43208 | tf_op jit(solution)/shard_map/ppermute | solution.py:24
  23.1 7.1 %collective-permute-start.6 = (f32[18,1,200]{2,1,0:T(1,128)S(1)}, f32[18,1,200]{2,1,0:T(1,128)S(1)}, u32[]{:S(2)}, u32[]{:S(2)}) collective-permute-start(f32[18,1,200]{2,1,0:T(1,128)S(1)} %get-tuple-element.20), channel_id=1, source_target_pairs={{1,0},{2,1},{3,2},{4,3},{5,4},{6,5},{7,6},{8,7},{9,8},{10,9},{11,1... | collective-permute-start | bytes 43208 | tf_op jit(solution)/shard_map/ppermute | solution.py:26
  45.1 5.2 %collective-permute-start.8 = (f32[2,52,200]{2,1,0:T(8,128)S(1)}, f32[2,52,200]{2,1,0:T(8,128)S(1)}, u32[]{:S(2)}, u32[]{:S(2)}) collective-permute-start(f32[2,52,200]{2,1,0:T(8,128)S(1)} %collective-permute-done.7), channel_id=1, source_target_pairs={{0,2},{2,0},{1,3},{3,1},{4,6},{6,4},{5,7},{7,5},{8,10},{10,8},{9,1... | collective-permute-start | bytes 249608 | tf_op jit(solution)/shard_map/ppermute | solution.py:14
  50.3 4.8 %collective-permute-start.9 = (f32[2,52,200]{2,1,0:T(8,128)S(1)}, f32[2,52,200]{2,1,0:T(8,128)S(1)}, u32[]{:S(2)}, u32[]{:S(2)}) collective-permute-start(f32[2,52,200]{2,1,0:T(8,128)S(1)} %collective-permute-done.8), channel_id=1, source_target_pairs={{0,4},{4,0},{1,5},{5,1},{2,6},{6,2},{3,7},{7,3},{8,12},{12,8},{9,1... | collective-permute-start | bytes 249608 | tf_op jit(solution)/shard_map/ppermute | solution.py:14
  55.1 4.8 %collective-permute-start.10 = (f32[2,52,200]{2,1,0:T(8,128)S(1)}, f32[2,52,200]{2,1,0:T(8,128)S(1)}, u32[]{:S(2)}, u32[]{:S(2)}) collective-permute-start(f32[2,52,200]{2,1,0:T(8,128)S(1)} %collective-permute-done.9), channel_id=1, source_target_pairs={{0,8},{8,0},{1,9},{9,1},{2,10},{10,2},{3,11},{11,3},{4,12},{12,4},... | collective-permute-start | bytes 249608 | tf_op jit(solution)/shard_map/ppermute | solution.py:14
  59.9 6.9 %collective-permute-start.11 = (f32[2,52,200]{2,1,0:T(8,128)S(1)}, f32[2,52,200]{2,1,0:T(8,128)S(1)}, u32[]{:S(2)}, u32[]{:S(2)}) collective-permute-start(f32[2,52,200]{2,1,0:T(8,128)S(1)} %collective-permute-done.10), channel_id=1, source_target_pairs={{0,16},{16,0},{1,17},{17,1},{2,18},{18,2},{3,19},{19,3},{4,20},{20... | collective-permute-start | bytes 249608 | tf_op jit(solution)/shard_map/ppermute | solution.py:14
  66.8 7.7 %collective-permute-start.12 = (f32[20,2,200]{2,1,0:T(2,128)S(1)}, f32[20,2,200]{2,1,0:T(2,128)S(1)}, u32[]{:S(2)}, u32[]{:S(2)}) collective-permute-start(f32[20,2,200]{2,1,0:T(2,128)S(1)} %get-tuple-element.15), channel_id=1, source_target_pairs={{0,1},{1,2},{2,3},{3,4},{4,5},{5,6},{6,7},{7,8},{8,9},{9,10},{10,1... | collective-permute-start | bytes 96008 | tf_op jit(solution)/shard_map/ppermute | solution.py:24
  66.9 7.7 %collective-permute-start.13 = (f32[20,2,200]{2,1,0:T(2,128)S(1)}, f32[20,2,200]{2,1,0:T(2,128)S(1)}, u32[]{:S(2)}, u32[]{:S(2)}) collective-permute-start(f32[20,2,200]{2,1,0:T(2,128)S(1)} %get-tuple-element.16), channel_id=1, source_target_pairs={{1,0},{2,1},{3,2},{4,3},{5,4},{6,5},{7,6},{8,7},{9,8},{10,9},{11,1... | collective-permute-start | bytes 96008 | tf_op jit(solution)/shard_map/ppermute | solution.py:26
  89.9 7.6 %collective-permute-start.15 = (f32[4,52,200]{2,1,0:T(8,128)S(1)}, f32[4,52,200]{2,1,0:T(8,128)S(1)}, u32[]{:S(2)}, u32[]{:S(2)}) collective-permute-start(f32[4,52,200]{2,1,0:T(8,128)S(1)} %collective-permute-done.14), channel_id=1, source_target_pairs={{0,2},{2,0},{1,3},{3,1},{4,6},{6,4},{5,7},{7,5},{8,10},{10,8},{9,1... | collective-permute-start | bytes 499208 | tf_op jit(solution)/shard_map/ppermute | solution.py:14
  97.5 6.8 %collective-permute-start.16 = (f32[4,52,200]{2,1,0:T(8,128)S(1)}, f32[4,52,200]{2,1,0:T(8,128)S(1)}, u32[]{:S(2)}, u32[]{:S(2)}) collective-permute-start(f32[4,52,200]{2,1,0:T(8,128)S(1)} %collective-permute-done.15), channel_id=1, source_target_pairs={{0,4},{4,0},{1,5},{5,1},{2,6},{6,2},{3,7},{7,3},{8,12},{12,8},{9,1... | collective-permute-start | bytes 499208 | tf_op jit(solution)/shard_map/ppermute | solution.py:14
  104.3 6.0 %collective-permute-start.17 = (f32[4,52,200]{2,1,0:T(8,128)S(1)}, f32[4,52,200]{2,1,0:T(8,128)S(1)}, u32[]{:S(2)}, u32[]{:S(2)}) collective-permute-start(f32[4,52,200]{2,1,0:T(8,128)S(1)} %collective-permute-done.16), channel_id=1, source_target_pairs={{0,8},{8,0},{1,9},{9,1},{2,10},{10,2},{3,11},{11,3},{4,12},{12,4},... | collective-permute-start | bytes 499208 | tf_op jit(solution)/shard_map/ppermute | solution.py:14
  110.3 12.5 %collective-permute-start.18 = (f32[4,52,200]{2,1,0:T(8,128)S(1)}, f32[4,52,200]{2,1,0:T(8,128)S(1)}, u32[]{:S(2)}, u32[]{:S(2)}) collective-permute-start(f32[4,52,200]{2,1,0:T(8,128)S(1)} %collective-permute-done.17), channel_id=1, source_target_pairs={{0,16},{16,0},{1,17},{17,1},{2,18},{18,2},{3,19},{19,3},{4,20},{20... | collective-permute-start | bytes 499208 | tf_op jit(solution)/shard_map/ppermute | solution.py:14
  122.8 7.7 %collective-permute-start.19 = (f32[24,4,200]{2,1,0:T(4,128)S(1)}, f32[24,4,200]{2,1,0:T(4,128)S(1)}, u32[]{:S(2)}, u32[]{:S(2)}) collective-permute-start(f32[24,4,200]{2,1,0:T(4,128)S(1)} %get-tuple-element.11), channel_id=1, source_target_pairs={{0,1},{1,2},{2,3},{3,4},{4,5},{5,6},{6,7},{7,8},{8,9},{9,10},{10,1... | collective-permute-start | bytes 230408 | tf_op jit(solution)/shard_map/ppermute | solution.py:24
  122.9 7.7 %collective-permute-start.20 = (f32[24,4,200]{2,1,0:T(4,128)S(1)}, f32[24,4,200]{2,1,0:T(4,128)S(1)}, u32[]{:S(2)}, u32[]{:S(2)}) collective-permute-start(f32[24,4,200]{2,1,0:T(4,128)S(1)} %get-tuple-element.12), channel_id=1, source_target_pairs={{1,0},{2,1},{3,2},{4,3},{5,4},{6,5},{7,6},{8,7},{9,8},{10,9},{11,1... | collective-permute-start | bytes 230408 | tf_op jit(solution)/shard_map/ppermute | solution.py:26
  144.5 12.6 %collective-permute-start.22 = (f32[8,52,200]{2,1,0:T(8,128)S(1)}, f32[8,52,200]{2,1,0:T(8,128)S(1)}, u32[]{:S(2)}, u32[]{:S(2)}) collective-permute-start(f32[8,52,200]{2,1,0:T(8,128)S(1)} %collective-permute-done.21), channel_id=1, source_target_pairs={{0,2},{2,0},{1,3},{3,1},{4,6},{6,4},{5,7},{7,5},{8,10},{10,8},{9,1... | collective-permute-start | bytes 998408 | tf_op jit(solution)/shard_map/ppermute | solution.py:14
  157.0 11.7 %collective-permute-start.23 = (f32[8,52,200]{2,1,0:T(8,128)S(1)}, f32[8,52,200]{2,1,0:T(8,128)S(1)}, u32[]{:S(2)}, u32[]{:S(2)}) collective-permute-start(f32[8,52,200]{2,1,0:T(8,128)S(1)} %collective-permute-done.22), channel_id=1, source_target_pairs={{0,4},{4,0},{1,5},{5,1},{2,6},{6,2},{3,7},{7,3},{8,12},{12,8},{9,1... | collective-permute-start | bytes 998408 | tf_op jit(solution)/shard_map/ppermute | solution.py:14
  168.7 10.8 %collective-permute-start.24 = (f32[8,52,200]{2,1,0:T(8,128)S(1)}, f32[8,52,200]{2,1,0:T(8,128)S(1)}, u32[]{:S(2)}, u32[]{:S(2)}) collective-permute-start(f32[8,52,200]{2,1,0:T(8,128)S(1)} %collective-permute-done.23), channel_id=1, source_target_pairs={{0,8},{8,0},{1,9},{9,1},{2,10},{10,2},{3,11},{11,3},{4,12},{12,4},... | collective-permute-start | bytes 998408 | tf_op jit(solution)/shard_map/ppermute | solution.py:14
  179.6 22.6 %collective-permute-start.25 = (f32[8,52,200]{2,1,0:T(8,128)S(1)}, f32[8,52,200]{2,1,0:T(8,128)S(1)}, u32[]{:S(2)}, u32[]{:S(2)}) collective-permute-start(f32[8,52,200]{2,1,0:T(8,128)S(1)} %collective-permute-done.24), channel_id=1, source_target_pairs={{0,16},{16,0},{1,17},{17,1},{2,18},{18,2},{3,19},{19,3},{4,20},{20... | collective-permute-start | bytes 998408 | tf_op jit(solution)/shard_map/ppermute | solution.py:14
  202.3 9.5 %collective-permute-start.26 = (f32[32,8,200]{2,1,0:T(8,128)S(1)}, f32[32,8,200]{2,1,0:T(8,128)S(1)}, u32[]{:S(2)}, u32[]{:S(2)}) collective-permute-start(f32[32,8,200]{2,1,0:T(8,128)S(1)} %get-tuple-element.7), channel_id=1, source_target_pairs={{0,1},{1,2},{2,3},{3,4},{4,5},{5,6},{6,7},{7,8},{8,9},{9,10},{10,1... | collective-permute-start | bytes 614408 | tf_op jit(solution)/shard_map/ppermute | solution.py:24
  202.3 9.5 %collective-permute-start.27 = (f32[32,8,200]{2,1,0:T(8,128)S(1)}, f32[32,8,200]{2,1,0:T(8,128)S(1)}, u32[]{:S(2)}, u32[]{:S(2)}) collective-permute-start(f32[32,8,200]{2,1,0:T(8,128)S(1)} %get-tuple-element.8), channel_id=1, source_target_pairs={{1,0},{2,1},{3,2},{4,3},{5,4},{6,5},{7,6},{8,7},{9,8},{10,9},{11,1... | collective-permute-start | bytes 614408 | tf_op jit(solution)/shard_map/ppermute | solution.py:26
  (7 other events, 50.3 us)
where the time goes:
time: 229 us; the launch traced here: 225 us
  waiting for transfers between devices  106 us (46%)
  matrix products  67.7 us (30%)
  starting transfers between devices  44.6 us (19%)
  local copies, waits for them, and re-layouts  3.7 us (2%)
    ppermute x20, waiting for transfers between devices, swapped(): return lax.ppermute(block, axis, route)  102 us
    dot_general x36, matrix products, convolve(): jnp.einsum('rlc,cd->rld', window, kernel[3 * tap_row + tap_col], precisio...  67.7 us
    ppermute x4, starting transfers between devices, padded_2(): lax.ppermute(head, axis, [((i + 1) % count, i) for i in range(count)])  22.4 us
    ppermute x20, starting transfers between devices, swapped(): return lax.ppermute(block, axis, route)  21.9 us
  transfers between devices with their start and end apart: 28, of which 24 were waited for; matrix products, arithmetic and copies ran while one was open for 8% of the time, Pallas kernels for 0%

commit v1 on v0

v1 whole, which is shorter than its diff:
```python
import functools

import jax
import jax.numpy as jnp
from jax import lax
from jax.experimental import pallas as pl
from jax.experimental.pallas import tpu as pltpu
from jax.sharding import PartitionSpec as P

F32 = jnp.float32
BF16 = jnp.bfloat16
LANES = 128
HALF = 64
MW = 64
HALO = 8


def slot_count(rows):
    halves = (rows + 1) // 2
    merged = rows % 2 == 1 and rows <= 8
    return rows + halves + (0 if merged else -(-rows // 16))


def lane_of(width):
    return lax.broadcasted_iota(jnp.int32, (width, LANES), 1)


def roll(x, shift):
    shift = shift % LANES
    return x if shift == 0 else pltpu.roll(x, shift, 1)


def pack(get, put, rows, width, rem):
    lane = lane_of(width)
    halves = (rows + 1) // 2
    merged = rows % 2 == 1 and rows <= 8
    for k in range(rows):
        put(k, get(k, 0))
    second = [get(k, 1) for k in range(rows)]
    for p in range(halves):
        other = roll(second[2 * p + 1], HALF) if 2 * p + 1 < rows else jnp.zeros((width, LANES), F32)
        tile = jnp.where(lane < HALF, second[2 * p], other)
        if merged and p == halves - 1:
            for k in range(rows):
                at = HALF + rem * k
                tile = jnp.where((lane >= at) & (lane < at + rem), roll(second[k], rem * k), tile)
        put(rows + p, tile)
    if not merged:
        for c in range(-(-rows // 16)):
            tile = jnp.zeros((width, LANES), F32)
            for k in range(16 * c, min(rows, 16 * c + 16)):
                at = rem * (k % 16)
                tile = jnp.where((lane >= at) & (lane < at + rem), roll(second[k], at - HALF), tile)
            put(rows + halves + c, tile)


def unpack(slot, k, rows, width, rem):
    lane = lane_of(width)
    halves = (rows + 1) // 2
    merged = rows % 2 == 1 and rows <= 8
    half = roll(slot(rows + k // 2), HALF * (k % 2))
    if merged:
        rest = roll(slot(rows + halves - 1), -rem * k)
    else:
        rest = roll(slot(rows + halves + k // 16), HALF - rem * (k % 16))
    tile = jnp.where(lane < HALF, half, jnp.where(lane < HALF + rem, rest, 0.0))
    return slot(k), tile


def slots_of(ref, width):
    return lambda k: ref[k * width : (k + 1) * width, :]


def putter(ref, width):
    def put(k, tile):
        ref[k * width : (k + 1) * width, :] = tile

    return put


def fill(hi, lo, dst, ref, src, count, offs):
    def body(i, carry):
        for b in range(3):
            for t in range(2):
                x = ref[src + i, t, offs[b] : offs[b] + MW, :]
                h = x.astype(BF16)
                at = b * 2 * LANES + t * LANES
                hi[dst + i, :, at : at + LANES] = h
                lo[dst + i, :, at : at + LANES] = (x - h.astype(F32)).astype(BF16)
        return carry

    lax.fori_loop(0, count, body, 0)


def products(hi, lo, wh, wl, taps, row, chunk, dilate, turn=False):
    total = None
    for a in taps:
        at = pl.ds(row + a * dilate, chunk)
        lh = hi[at].reshape(chunk * MW, hi.shape[-1])
        ll = lo[at].reshape(chunk * MW, hi.shape[-1])
        for left, right in ((lh, wh), (ll, wh), (lh, wl)):
            term = jnp.dot(left, right[2 - a if turn else a], preferred_element_type=F32)
            total = term if total is None else total + term
    return total


def conv(hi, lo, wh, wl, bias, dilate, base, count, chunk, emit, turn=False):
    def body(i, carry):
        row = i * chunk
        total = products(hi, lo, wh, wl, (0, 1, 2), base + row, chunk, dilate, turn)
        emit(row, jax.nn.gelu(total + bias[...]))
        return carry

    if count == chunk:
        body(0, 0)
    else:
        lax.fori_loop(0, count // chunk, body, 0)


def add_rows(out, out_row, res, res_row, off, chunk):
    def emit(row, grown):
        for q in range(chunk):
            for t in range(2):
                out[out_row + row + q, t, 0:MW, :] = (
                    res[res_row + row + q, t, off : off + MW, :]
                    + grown[q * MW : (q + 1) * MW, t * LANES : (t + 1) * LANES]
                )

    return emit


def put_row(dst, row, at, tiles):
    for t in range(2):
        dst[row, t, at : at + tiles[t].shape[0], :] = tiles[t]


def tile_of(ref, row, lo, hi, channels):
    part = ref[row, lo:hi, LANES:channels]
    return jnp.concatenate([part, jnp.zeros((hi - lo, 2 * LANES - channels), F32)], axis=1)


def k_first(par, field, south, main, ewi, ewc, *, top):
    rows, cols, channels = field.shape
    rem = channels - LANES - HALF

    def get(k, t):
        row = rows - 1 - k
        return field[row, :, 0:LANES] if t == 0 else tile_of(field, row, 0, cols, channels)

    pack(get, putter(main, cols), top, cols, rem)
    even = par[0] == 0

    def edge(flip):
        def get(k, t):
            ref, row = (field, k) if k < rows else (south, k - rows)
            if t == 0:
                west, east = ref[row, 0:HALO, 0:LANES], ref[row, cols - HALO : cols, 0:LANES]
            else:
                west = tile_of(ref, row, 0, HALO, channels)
                east = tile_of(ref, row, cols - HALO, cols, channels)
            return jnp.where(even != flip, east, west)

        return get

    count = rows + south.shape[0]
    pack(edge(False), putter(ewi, HALO), count, HALO, rem)
    pack(edge(True), putter(ewc, HALO), count, HALO, rem)


def k_weights(w, wh, wl):
    channels = w.shape[-1]
    wh[...] = jnp.zeros(wh.shape, BF16)
    wl[...] = jnp.zeros(wl.shape, BF16)
    for a in range(3):
        for b in range(3):
            x = w[0, 3 * a + b]
            h = x.astype(BF16)
            at = b * 2 * LANES
            wh[0, a, at : at + channels, 0:channels] = h
            wl[0, a, at : at + channels, 0:channels] = (x - h.astype(F32)).astype(BF16)


def sided(par, ewi, ewc):
    even = par[0] == 0
    west = lambda k: jnp.where(even, slots_of(ewc, HALO)(k), slots_of(ewi, HALO)(k))
    east = lambda k: jnp.where(even, slots_of(ewi, HALO)(k), slots_of(ewc, HALO)(k))
    return west, east


def k_corner(par, ewi, ewc, out, *, count, total, last, rem):
    west, east = sided(par, ewi, ewc)
    tiles = []
    for k in range(count):
        w = unpack(west, last - k, total, HALO, rem)
        e = unpack(east, last - k, total, HALO, rem)
        tiles.append([jnp.concatenate([w[t], e[t]], axis=0) for t in range(2)])
    pack(lambda k, t: tiles[k][t], putter(out, 2 * HALO), count, 2 * HALO, rem)


def k_a(par, field, south, ewi, ewc, wh, wl, bias, st1, se, edge0, x0, hi, lo):
    rows, cols, channels = field.shape
    rem = channels - LANES - HALF
    total = rows + south.shape[0]
    west, east = sided(par, ewi, ewc)
    for k in range(total):
        ref, row, dst = (field, k, x0) if k < rows else (south, k - rows, se)
        put_row(dst, row, 0, unpack(west, k, total, HALO, rem))
        put_row(dst, row, HALO, (ref[row, :, 0:LANES], tile_of(ref, row, 0, cols, channels)))
        put_row(dst, row, HALO + cols, unpack(east, k, total, HALO, rem))
    edge0[...] = x0[rows - 2 :]
    offs = (1, 2, 3)
    fill(hi, lo, 0, se, south.shape[0] - 1, 1, offs)
    fill(hi, lo, 1, x0, 0, rows, offs)
    count = rows - 1
    conv(hi, lo, wh.at[0], wl.at[0], bias, 1, 0, count, 5, add_rows(st1, 0, x0, 0, 2, 5))


def signed(tiles, sign):
    return tiles if sign is None else [tiles[t] * sign[t] for t in range(2)]


def north_rows(dst, dst_row, main, sign, count, cols, width, left, rem):
    n = slot_count(count)
    for k in range(count):
        t = unpack(lambda q: main[(n - 1 - q) * width : (n - q) * width, :], k, count, width, rem)
        put_row(dst, dst_row + k, left, signed(t, sign))


def north_corners(dst, dst_row, corner, sign, ks, total, cols, left, rem):
    n = slot_count(total)
    width = 2 * HALO
    for i, k in enumerate(ks):
        t = unpack(lambda q: corner[(n - 1 - q) * width : (n - q) * width, :], k, total, width, rem)
        t = signed(t, sign)
        put_row(dst, dst_row + i, left - HALO, [x[0:HALO] for x in t])
        put_row(dst, dst_row + i, left + cols, [x[HALO:] for x in t])


def k_b(edge0, main, corner, st1, sign, wh, wl, bias, st2, out, x0, xr, x1, hi, lo, *, cols, rem):
    rows = st1.shape[0] + 1
    north_rows(xr, 1, main, None, 3, cols, cols, HALO, rem)
    north_corners(xr, 1, corner, None, range(3), 3, cols, HALO, rem)
    x0[0:2] = edge0[...]
    for t in range(2):
        x0[2, t] = xr[1, t] * sign[t]
        xr[0, t] = edge0[1, t] * sign[t]
    x1[0:5] = st1[rows - 6 : rows - 1]
    offs = (1, 2, 3)
    fill(hi, lo, 0, x0, 0, 3, offs)
    conv(hi, lo, wh.at[0], wl.at[0], bias.at[0], 1, 0, 1, 1, add_rows(x1, 5, x0, 1, 2, 1))
    fill(hi, lo, 3, xr, 0, 4, offs[::-1])

    def emit(row, grown):
        for q in range(2):
            for t in range(2):
                x1[6 + q, t, 0:MW, :] = sign[t] * (
                    xr[1 + q, t, 2 : 2 + MW, :] + grown[q * MW : (q + 1) * MW, t * LANES : (t + 1) * LANES]
                )

    conv(hi, lo, wh.at[0], wl.at[0], bias.at[0], 1, 3, 2, 2, emit, turn=True)
    fill(hi, lo, 0, x1, 0, 8, (0, 2, 4))
    conv(hi, lo, wh.at[1], wl.at[1], bias.at[1], 2, 0, 4, 4, add_rows(st2, 0, x1, 2, 2, 4))
    wide = cols + 8
    pack(lambda k, t: st2[3 - k, t, 0:wide, :], putter(out, wide), 4, wide, rem)


def k_c(st1, st2b, se, wh, wl, bias, st2, st3, out, hi, lo, *, cols, rem):
    south = se.shape[0]
    rows = st2.shape[0]
    low = rows - 4
    fill(hi, lo, 0, se, south - 2, 2, (2, 4, 6))
    fill(hi, lo, 2, st1, 0, low + 2, (0, 2, 4))
    conv(hi, lo, wh.at[0], wl.at[0], bias.at[0], 2, 0, low, 4, add_rows(st2, 0, st1, 0, 2, 4))
    st2[low:rows] = st2b[...]
    fill(hi, lo, 0, se, south - 4, 4, (4, 8, 12))
    fill(hi, lo, 4, st2, 0, rows, (0, 4, 8))
    conv(hi, lo, wh.at[1], wl.at[1], bias.at[1], 4, 0, low, 4, add_rows(st3, 0, st2, 0, 4, 4))
    pack(lambda k, t: st3[low - 1 - k, t, 0:cols, :], putter(out, cols), 4, cols, rem)


def k_d(par, st2, north, st3a, sign, wh, wl, bias, st3b, out, ewi, ewc, x2, hi, lo, *, cols, rem):
    rows = st2.shape[0]
    wide = cols + 8
    north_rows(x2, 0, north, sign, 4, cols, wide, 0, rem)
    fill(hi, lo, 0, st2, rows - 8, 8, (0, 4, 8))
    fill(hi, lo, 8, x2, 0, 4, (0, 4, 8))
    conv(hi, lo, wh, wl, bias, 4, 0, 4, 4, add_rows(st3b, 0, st2, rows - 4, 4, 4))
    pack(lambda k, t: st3b[3 - k, t, 0:cols, :], putter(out, cols), 4, cols, rem)
    even = par[0] == 0

    def edge(flip):
        def get(k, t):
            ref, row = (st3a, k) if k < rows - 4 else (st3b, k - rows + 4)
            west, east = ref[row, t, 0:HALO, :], ref[row, t, cols - HALO : cols, :]
            return jnp.where(even != flip, east, west)

        return get

    pack(edge(False), putter(ewi, HALO), rows, HALO, rem)
    pack(edge(True), putter(ewc, HALO), rows, HALO, rem)


def k_f(par, st3a, st3b, ewi, ewc, se, wh, wl, bias, outlo, acc, x3, hi, lo, *, cols, channels):
    rem = channels - LANES - HALF
    rows = x3.shape[0]
    south = se.shape[0]
    west, east = sided(par, ewi, ewc)
    for k in range(rows):
        ref, row = (st3a, k) if k < rows - 4 else (st3b, k - rows + 4)
        put_row(x3, k, 0, unpack(west, k, rows, HALO, rem))
        put_row(x3, k, HALO, [ref[row, t, 0:cols, :] for t in range(2)])
        put_row(x3, k, HALO + cols, unpack(east, k, rows, HALO, rem))
    offs = (0, 8, 16)
    fill(hi, lo, 0, se, 0, south, offs)
    fill(hi, lo, south, x3, 0, rows, offs)

    def emit(row, grown):
        for q in range(4):
            g = grown[q * MW : q * MW + cols]
            outlo[row + q, :, 0:LANES] = x3[row + q, 0, HALO : HALO + cols, :] + g[:, 0:LANES]
            outlo[row + q, :, LANES:channels] = (x3[row + q, 1, HALO : HALO + cols, :] + g[:, LANES:])[
                :, 0 : channels - LANES
            ]

    conv(hi, lo, wh, wl, bias, 8, 0, rows - 8, 4, emit)

    def body(i, carry):
        total = products(hi, lo, wh, wl, (0, 1), rows - 8 + 4 * i, 4, 8)
        acc[pl.ds(4 * i, 4)] = (total + bias[...]).reshape(4, MW, 2 * LANES)
        return carry

    lax.fori_loop(0, 2, body, 0)


def k_g(outlo, acc, st3a, st3b, na, nb, nc, sign, wh, wl, out, xn, hi, lo, *, rem):
    rows, cols, channels = out.shape
    north_rows(xn, 0, nb, sign, 4, cols, cols, HALO, rem)
    north_rows(xn, 4, na, sign, 4, cols, cols, HALO, rem)
    north_corners(xn, 0, nc, sign, range(8), 8, cols, HALO, rem)
    fill(hi, lo, 0, xn, 0, 8, (0, 8, 16))
    for r in range(rows - 8):
        out[r] = outlo[r]
    for i in range(2):
        total = None
        at = pl.ds(4 * i, 4)
        lh = hi[at].reshape(4 * MW, hi.shape[-1])
        ll = lo[at].reshape(4 * MW, hi.shape[-1])
        total = acc[at].reshape(4 * MW, 2 * LANES)
        for left, right in ((lh, wh), (ll, wh), (lh, wl)):
            total = total + jnp.dot(left, right[2], preferred_element_type=F32)
        grown = jax.nn.gelu(total)
        for q in range(4):
            r = rows - 8 + 4 * i + q
            ref, row = (st3a, r) if r < rows - 4 else (st3b, r - rows + 4)
            g = grown[q * MW : q * MW + cols]
            out[r, :, 0:LANES] = ref[row, 0, 0:cols, :] + g[:, 0:LANES]
            out[r, :, LANES:channels] = (ref[row, 1, 0:cols, :] + g[:, LANES:])[:, 0 : channels - LANES]


VM = pl.BlockSpec(memory_space=pltpu.VMEM)
SM = pl.BlockSpec(memory_space=pltpu.SMEM)


def lhs(rows):
    return [pltpu.VMEM((rows, MW, 6 * LANES), BF16)] * 2


def call(kernel, outs, scratch, args, smem=0, flops=0, limit=30, name=None, layers=None):
    specs = [SM] * smem + [VM] * (len(args) - smem)
    for at, (first, count) in (layers or {}).items():
        shape = (count,) + args[at].shape[1:]
        assert first % count == 0
        if count == 1:
            shape = (None,) + args[at].shape[1:]
        specs[at] = pl.BlockSpec(
            shape,
            functools.partial(lambda f, nd, i: (f,) + (0,) * (nd - 1), first // count, args[at].ndim),
            pipeline_mode=pl.Buffered(1),
        )
    moved = sum(a.size * a.dtype.itemsize for a in args[smem:])
    return pl.pallas_call(
        kernel,
        grid=(1,),
        out_shape=[jax.ShapeDtypeStruct(s, F32) for s in outs],
        in_specs=specs,
        out_specs=[VM] * len(outs),
        scratch_shapes=scratch,
        compiler_params=pltpu.CompilerParams(vmem_limit_bytes=limit * 2**20),
        cost_estimate=pl.CostEstimate(flops=flops, bytes_accessed=moved, transcendentals=0),
        name=name,
    )(*args)


def local(field, south_rows, sign_mask, weights, biases):
    rows, cols, channels = field.shape
    south = south_rows.shape[0]
    layers = weights.shape[0]
    rem = channels - LANES - HALF
    devices = lax.axis_size("lon")
    mirror = [(i, devices - 1 - i) for i in range(devices)]
    intra = [(i, i ^ 1) for i in range(devices)]
    cross = [(i, (i + 1) % devices if i % 2 else (i - 1) % devices) for i in range(devices)]
    send = lambda x, route: lax.ppermute(x, "lon", route)
    par = (lax.axis_index("lon") % 2).astype(jnp.int32).reshape(1)
    pad = 2 * LANES - channels
    sign = jnp.pad(sign_mask.astype(F32), (0, pad)).reshape(2, 1, LANES)
    bias = jnp.pad(biases, ((0, 0), (0, pad))).reshape(layers, 1, 2 * LANES)
    row_flops = MW * 6 * LANES * 2 * LANES * 2 * 9

    total = rows + south
    ew_rows = slot_count(total) * HALO
    main, ewi, ewc = call(
        functools.partial(k_first, top=3),
        [(slot_count(3) * cols, LANES), (ew_rows, LANES), (ew_rows, LANES)],
        [], [par, field, south_rows], smem=1, name="first",
    )
    ewi, ewc, main = send(ewi, intra), send(ewc, cross), send(main, mirror)

    wshape = jax.ShapeDtypeStruct((layers, 3, 6 * LANES, 2 * LANES), BF16)
    wspec = pl.BlockSpec((1, 3, 6 * LANES, 2 * LANES), lambda i: (i, 0, 0, 0))
    wh, wl = pl.pallas_call(
        k_weights,
        grid=(layers,),
        out_shape=[wshape, wshape],
        in_specs=[pl.BlockSpec((1,) + weights.shape[1:], lambda i: (i, 0, 0, 0))],
        out_specs=[wspec, wspec],
        compiler_params=pltpu.CompilerParams(vmem_limit_bytes=30 * 2**20),
        cost_estimate=pl.CostEstimate(flops=0, bytes_accessed=16 * 2**20, transcendentals=0),
        name="weights",
    )(weights)

    (corner,) = call(
        functools.partial(k_corner, count=3, total=total, last=rows - 1, rem=rem),
        [(slot_count(3) * 2 * HALO, LANES)], [], [par, ewi, ewc], smem=1, name="corner",
    )
    corner = send(corner, mirror)

    def state(n, width):
        return (n, 2, width, LANES)

    st1, se, edge0 = call(
        k_a,
        [state(rows - 1, 72), state(south, 80), state(2, 72)],
        [pltpu.VMEM(state(rows, 72), F32)] + lhs(rows + 1),
        [par, field, south_rows, ewi, ewc, wh[0:1], wl[0:1], bias[0]],
        smem=1, flops=(rows - 1) * row_flops, name="a",
    )
    st2b, north = call(
        functools.partial(k_b, cols=cols, rem=rem),
        [state(4, 72), (slot_count(4) * (cols + 8), LANES)],
        [pltpu.VMEM(state(3, 72), F32), pltpu.VMEM(state(4, 72), F32), pltpu.VMEM(state(8, 72), F32)] + lhs(8),
        [edge0, main[::-1], corner[::-1], st1, sign, wh[0:2], wl[0:2], bias[0:2]],
        flops=7 * row_flops, name="b",
    )
    north = send(north, mirror)
    st2, st3a, na = call(
        functools.partial(k_c, cols=cols, rem=rem),
        [state(rows, 72), state(rows - 4, MW), (slot_count(4) * cols, LANES)],
        lhs(rows + 4),
        [st1, st2b, se, wh[1:3], wl[1:3], bias[1:3]],
        flops=(2 * rows - 8) * row_flops, name="c",
    )
    na = send(na, mirror)
    ew_rows = slot_count(rows) * HALO
    st3b, nb, ewi, ewc = call(
        functools.partial(k_d, cols=cols, rem=rem),
        [state(4, MW), (slot_count(4) * cols, LANES), (ew_rows, LANES), (ew_rows, LANES)],
        [pltpu.VMEM(state(4, 72), F32)] + lhs(12),
        [par, st2, north[::-1], st3a, sign, wh[2], wl[2], bias[2]],
        smem=1, flops=4 * row_flops, name="d",
    )
    nb = send(nb, mirror)
    ewi, ewc = send(ewi, intra), send(ewc, cross)
    (nc,) = call(
        functools.partial(k_corner, count=8, total=rows, last=rows - 1, rem=rem),
        [(slot_count(8) * 2 * HALO, LANES)], [], [par, ewi, ewc], smem=1, name="corner2",
    )
    nc = send(nc, mirror)
    outlo, acc = call(
        functools.partial(k_f, cols=cols, channels=channels),
        [(rows - 8, cols, channels), (8, MW, 2 * LANES)],
        [pltpu.VMEM(state(rows, 80), F32)] + lhs(rows + south),
        [par, st3a, st3b, ewi, ewc, se, wh[3], wl[3], bias[3]],
        smem=1, flops=(rows - 3) * row_flops, name="f",
    )
    (out,) = call(
        functools.partial(k_g, rem=rem),
        [(rows, cols, channels)],
        [pltpu.VMEM(state(8, 80), F32)] + lhs(8),
        [outlo, acc, st3a, st3b, na[::-1], nb[::-1], nc[::-1], sign, wh[3], wl[3]],
        flops=3 * row_flops, name="g",
    )
    return out


def solution(mesh):
    in_specs = (P(None, "lon", None), P(None, "lon", None), P(), P(), P())
    out_specs = P(None, "lon", None)
    return jax.shard_map(local, mesh=mesh, in_specs=in_specs, out_specs=out_specs, check_vma=False)
```

time: 229 us -> 112 us (0.49); the launches traced: 225 us -> 110 us
  waiting for transfers between devices: 106 us -> 0.74 us
  matrix products: 67.7 us -> 0 us
  local copies, waits for them, and re-layouts: 3.7 us -> 53.8 us
  Pallas kernels: 0 us -> 31.8 us
  starting transfers between devices: 44.6 us -> 23.9 us
    ppermute x28 -> x10, waiting for transfers between devices: 106 us -> 0.74 us  [local(): send = lambda x, route: lax.ppermute(x, 'lon', route)]
    dot_general x36 -> x0, matrix products: 67.7 us -> none  [convolve(): jnp.einsum('rlc,cd->rld', window, kernel[3 * tap_row + tap_col], precisio...]
    unnamed x8 -> x88, local copies, waits for them, and re-layouts: 1.91 us -> 36.3 us
    pallas_call x0 -> x10, Pallas kernels: none -> 31.8 us  [the longest x9 30.1 us: call(): pl.pallas_call(kernel, grid=(1,), out_shape=[jax.ShapeDtypeStruct(s, F32)...]
    ppermute x28 -> x10, starting transfers between devices: 44.6 us -> 23.9 us  [local(): send = lambda x, route: lax.ppermute(x, 'lon', route)]
    rev x4 -> x6, local copies, waits for them, and re-layouts: 0.54 us -> 10.2 us  [the longest x1 2.21 us: local(): main[::-1]]
    slice x7 -> x5, local copies, waits for them, and re-layouts: 0.09 us -> 3.51 us  [the longest x1 2.93 us: local(): wl[1:3]]
    squeeze x0 -> x1, local copies, waits for them, and re-layouts: none -> 2.61 us  [local(): wl[3]]
  transfers between devices with their start and end apart: 28 -> 10, of which waited for: 24 -> 1; matrix products, arithmetic and copies ran while one was open for 8% -> 12% of each run, Pallas kernels for 0% -> 22%
where the time goes in v1:
time: 112 us; the launch traced here: 110 us
  local copies, waits for them, and re-layouts  53.8 us (48%)
  Pallas kernels  31.8 us (28%)
  starting transfers between devices  23.9 us (21%)
    unnamed x88, local copies, waits for them, and re-layouts  36.3 us
    pallas_call x9, Pallas kernels, call(): pl.pallas_call(kernel, grid=(1,), out_shape=[jax.ShapeDtypeStruct(s, F32)...  30.1 us
    ppermute x10, starting transfers between devices, local(): send = lambda x, route: lax.ppermute(x, 'lon', route)  23.9 us
    slice x1, local copies, waits for them, and re-layouts, local(): wl[1:3]  2.93 us
    squeeze x1, local copies, waits for them, and re-layouts, local(): wl[3]  2.61 us
  transfers between devices with their start and end apart: 10, of which 1 were waited for; matrix products, arithmetic and copies ran while one was open for 12% of the time, Pallas kernels for 22%

profile of v1, /device:TPU:0, one launch (start us, length us, event | category | flops | bytes accessed | tf_op | source)
XLA Modules:
  0.0 110.4 jit_solution(9666964970361940036)
XLA Ops:
  0.0 1.7 %copy.8.field = f32[16,52,200]{2,1,0:T(8,128)S(1)} copy(f32[16,52,200]{2,0,1:T(8,128)} %param.5) | data formatting | bytes 1331200 | tf_op args[0]
  1.7 1.5 %copy.9.south = f32[8,52,200]{2,1,0:T(8,128)S(1)} copy(f32[8,52,200]{2,0,1:T(8,128)} %param.6) | data formatting | bytes 665600 | tf_op args[1]
  4.5 6.6 %collective-permute-start.1 = (f32[304,128]{1,0:T(8,128)}, f32[304,128]{1,0:T(8,128)}, u32[]{:S(2)}, u32[]{:S(2)}) collective-permute-start(f32[304,128]{1,0:T(8,128)} %get-tuple-element.25), channel_id=1, source_target_pairs={{0,31},{1,2},{2,1},{3,4},{4,3},{5,6},{6,5},{7,8},{8,7},{9,10},{10,... | collective-permute-start | bytes 466952 | tf_op jit(solution)/shard_map/ppermute | solution.py:403
  11.2 3.1 %copy-done.1 = f32[4,9,200,200]{3,2,1,0:T(8,128)S(1)} copy-done((f32[4,9,200,200]{3,2,1,0:T(8,128)S(1)}, f32[4,9,200,200]{3,2,1,0:T(8,128)}, u32[]{:S(2)}) %copy-start.1) | copy-done | bytes 5760024
  14.2 1.7 %weights.1 = (bf16[4,3,768,256]{3,2,1,0:T(8,128)(2,1)S(1)}, bf16[4,3,768,256]{3,2,1,0:T(8,128)(2,1)S(1)}) custom-call(f32[4,9,200,200]{3,2,1,0:T(8,128)S(1)} %copy-done.1), custom_call_target="tpu_custom_call" | custom-call | bytes 16777216 | tf_op jit(solution)/shard_map/weights/pallas_call | solution.py:421
  16.0 2.6 %slice_bitcast_fusion = (bf16[3,768,256]{2,1,0:T(8,128)(2,1)}, bf16[3,768,256]{2,1,0:T(8,128)(2,1)S(1)}, bf16[1,3,768,256]{3,2,1,0:T(8,128)(2,1)}, bf16[1,3,768,...) fusion(bf16[4,3,768,256]{3,2,1,0:T(8,128)(2,1)S(1)} %get-tuple-element.27, ...), kind=kLoop, calls=%fused_computation | loop fusion | bytes 14155776 | tf_op jit(solution)/shard_map/squeeze | solution.py:483
  18.6 2.9 %fusion.2 = (bf16[2,3,768,256]{3,2,1,0:T(8,128)(2,1)}, bf16[2,3,768,256]{3,2,1,0:T(8,128)(2,1)S(1)}, bf16[2,3,768,256]{3,2,1,0:T(8,128)(2,1)}, bf16[2,3,768,256]{3,2,1,0:T(8,128)(2,1)}) fusion(bf16[4,3,768,256]{3,2,1,0:T(8,128)(2,1)S(1)} %get-tuple-element.27, bf16[4,3,768,256]{3,2,1,0:T(8,128)(2,1)S(1)} %get-tuple-element.26), kind=kLoop, calls=%fused_computation.11 | loop fusion | bytes 18874368 | tf_op jit(solution)/shard_map/slice | solution.py:460
  22.2 2.2 %rev.18.main = f32[260,128]{1,0:T(8,128)} reverse(f32[260,128]{1,0:T(8,128)} %collective-permute-done.2), dimensions={0} | reverse | bytes 266240 | tf_op jit(solution)/shard_map/rev | solution.py:452
  25.5 5.3 %collective-permute-start.3 = (f32[80,128]{1,0:T(8,128)S(1)}, f32[80,128]{1,0:T(8,128)}, u32[]{:S(2)}, u32[]{:S(2)}) collective-permute-start(f32[80,128]{1,0:T(8,128)S(1)} %corner.1), channel_id=1, source_target_pairs={{0,31},{1,30},{2,29},{3,28},{4,27},{5,26},{6,25},{7,24},{8,23},{9,... | collective-permute-start | bytes 122888 | tf_op jit(solution)/shard_map/ppermute | solution.py:403
  36.2 5.9 %a.1 = (f32[15,2,72,128]{3,2,1,0:T(8,128)S(1)}, f32[8,2,80,128]{3,2,1,0:T(8,128)S(1)}, f32[2,2,72,128]{3,2,1,0:T(8,128)S(1)}) custom-call(s32[1]{0:T(128)} %bitcast.par, f32[16,52,200]{2,1,0:T(8,128)S(1)} %copy-done.7, f32[8,52,200]{2,1,0:T(8,128)S(1)} %copy-done.15, f32[304,128]{1,0:T(8,128)} %collective-permute-done.ewi, ...), custom_call_target="tpu_custom_call" | custom-call | flops 3397386240 | bytes 3670016 | tf_op jit(solution)/shard_map/a/pallas_call | solution.py:381
  44.7 1.4 %rev.19.corner = f32[80,128]{1,0:T(8,128)} reverse(f32[80,128]{1,0:T(8,128)} %collective-permute-done.3), dimensions={0} | reverse | bytes 81920 | tf_op jit(solution)/shard_map/rev | solution.py:452
  46.1 1.7 %copy-done = bf16[2,3,768,256]{3,2,1,0:T(8,128)(2,1)S(1)} copy-done((bf16[2,3,768,256]{3,2,1,0:T(8,128)(2,1)S(1)}, bf16[2,3,768,256]{3,2,1,0:T(8,128)(2,1)}, u32[]{:S(2)}) %copy-start) | copy-done | bytes 2359320
  51.6 4.1 %b.1 = (f32[4,2,72,128]{3,2,1,0:T(8,128)S(1)}, f32[420,128]{1,0:T(8,128)S(1)}) custom-call(f32[2,2,72,128]{3,2,1,0:T(8,128)S(1)} %copy-done.34, f32[260,128]{1,0:T(8,128)S(1)} %copy-done.23, f32[80,128]{1,0:T(8,128)S(1)} %copy-done.32, f32[15,2,72,128]{3,2,1,0:T(8,128)S(1)} %copy-done.21, f32[2,1,128]{2,1,0:T(1,128)S(1)} %bitcast.14, ...), custom_call_target="tpu_custom_call" | custom-call | flops 1585446912 | bytes 6149120 | tf_op jit(solution)/shard_map/b/pallas_call | solution.py:381
  55.8 8.9 %c.1 = (f32[16,2,72,128]{3,2,1,0:T(8,128)S(1)}, f32[12,2,64,128]{3,2,1,0:T(8,128)S(1)}, f32[364,128]{1,0:T(8,128)}) custom-call(f32[15,2,72,128]{3,2,1,0:T(8,128)S(1)} %copy-done.21, f32[4,2,72,128]{3,2,1,0:T(8,128)S(1)} %get-tuple-element.31.st2b, f32[8,2,80,128]{3,2,1,0:T(8,128)S(1)} %copy-done.39, bf16[2,3,768,256]{3,2,1,0:T(8,128)(2,1)S(1)} %copy-done.13, ...), custom_call_target="tpu_custom_call" | custom-call | flops 5435817984 | bytes 6776832 | tf_op jit(solution)/shard_map/c/pallas_call | solution.py:381
  66.7 5.3 %collective-permute-start.7 = (f32[364,128]{1,0:T(8,128)}, f32[364,128]{1,0:T(8,128)}, u32[]{:S(2)}, u32[]{:S(2)}) collective-permute-start(f32[364,128]{1,0:T(8,128)} %get-tuple-element.41), channel_id=1, source_target_pairs={{0,31},{1,30},{2,29},{3,28},{4,27},{5,26},{6,25},{7,24},{8,23},{9,... | collective-permute-start | bytes 559112 | tf_op jit(solution)/shard_map/ppermute | solution.py:403
  72.0 1.4 %rev.20.north = f32[420,128]{1,0:T(8,128)} reverse(f32[420,128]{1,0:T(8,128)S(1)} %collective-permute-done.4), dimensions={0} | reverse | bytes 430080 | tf_op jit(solution)/shard_map/rev | solution.py:469
  76.7 2.4 %d.1 = (f32[4,2,64,128]{3,2,1,0:T(8,128)S(1)}, f32[364,128]{1,0:T(8,128)S(1)}, f32[200,128]{1,0:T(8,128)}, f32[200,128]{1,0:T(8,128)}) custom-call(s32[1]{0:T(128)} %bitcast.par, f32[16,2,72,128]{3,2,1,0:T(8,128)S(1)} %copy-done.19, f32[420,128]{1,0:T(8,128)S(1)} %copy-done.22, f32[12,2,64,128]{3,2,1,0:T(8,128)S(1)} %copy-done.9, f32[2,1,128]{2,1,0:T(1,128)S(1)} %bitcast.15, ...), custom_call_target="tpu_custom_call" | custom-call | flops 905969664 | bytes 4542464 | tf_op jit(solution)/shard_map/d/pallas_call | solution.py:381
  81.1 1.9 %rev.21.na = f32[364,128]{1,0:T(8,128)S(1)} reverse(f32[364,128]{1,0:T(8,128)} %collective-permute-done.7), dimensions={0} | reverse | bytes 372736 | tf_op jit(solution)/shard_map/rev | solution.py:490
  83.0 4.8 %collective-permute-start.8 = (f32[364,128]{1,0:T(8,128)}, f32[364,128]{1,0:T(8,128)}, u32[]{:S(2)}, u32[]{:S(2)}) collective-permute-start(f32[364,128]{1,0:T(8,128)} %copy-done.37), channel_id=1, source_target_pairs={{0,31},{1,30},{2,29},{3,28},{4,27},{5,26},{6,25},{7,24},{8,23},{9,... | collective-permute-start | bytes 559112 | tf_op jit(solution)/shard_map/ppermute | solution.py:403
  90.0 1.3 %copy-done.4 = bf16[3,768,256]{2,1,0:T(8,128)(2,1)S(1)} copy-done((bf16[3,768,256]{2,1,0:T(8,128)(2,1)S(1)}, bf16[3,768,256]{2,1,0:T(8,128)(2,1)}, u32[]{:S(2)}) %copy-start.4) | copy-done | bytes 1179672
  94.4 4.7 %f.1 = (f32[8,52,200]{2,1,0:T(8,128)S(1)}, f32[8,64,256]{2,1,0:T(8,128)S(1)}) custom-call(s32[1]{0:T(128)} %bitcast.par, f32[12,2,64,128]{3,2,1,0:T(8,128)S(1)} %copy-done.10, f32[4,2,64,128]{3,2,1,0:T(8,128)S(1)} %copy-done.30, f32[200,128]{1,0:T(8,128)S(1)} %collective-permute-done.5.ewi, f32[200,128]{1,0:T(8,128)S(1)} %collective-permute-done.6.ewc, ...), custom_call_target="tpu_custom_call" | custom-call | flops 2944401408 | bytes 4269056 | tf_op jit(solution)/shard_map/f/pallas_call | solution.py:381
  100.7 1.9 %rev.22.nb = f32[364,128]{1,0:T(8,128)S(1)} reverse(f32[364,128]{1,0:T(8,128)} %collective-permute-done.8), dimensions={0} | reverse | bytes 372736 | tf_op jit(solution)/shard_map/rev | solution.py:490
  102.5 1.5 %rev.23.nc = f32[208,128]{1,0:T(8,128)} reverse(f32[208,128]{1,0:T(8,128)} %collective-permute-done.9), dimensions={0} | reverse | bytes 212992 | tf_op jit(solution)/shard_map/rev | solution.py:490
  107.9 1.3 %g.1 = f32[16,52,200]{2,1,0:T(8,128)S(1)} custom-call(f32[8,52,200]{2,1,0:T(8,128)S(1)} %copy-done.27, f32[8,64,256]{2,1,0:T(8,128)S(1)} %copy-done.25, f32[12,2,64,128]{3,2,1,0:T(8,128)S(1)} %copy-done.11, f32[4,2,64,128]{3,2,1,0:T(8,128)S(1)} %copy-done.31, f32[364,128]{1,0:T(8,128)S(1)} %rev.21.na, f32[364,128]{1,0:T(8,128)S(1)} %rev.22.nb, ...), custom_call_target="tpu_custom_call" | custom-call | flops 679477248 | bytes 4745216 | tf_op jit(solution)/shard_map/g/pallas_call | solution.py:381
  (109 shorter events, 34.4 us)
Async XLA Ops:
  1.7 14.3 %copy-start.6 = (f32[16,52,200]{2,1,0:T(8,128)}, f32[16,52,200]{2,1,0:T(8,128)S(1)}, u32[]{:S(2)}) copy-start(f32[16,52,200]{2,1,0:T(8,128)S(1)} %copy.8.field) | copy-start | bytes 1996804
  3.1 12.8 %copy-start.14 = (f32[8,52,200]{2,1,0:T(8,128)}, f32[8,52,200]{2,1,0:T(8,128)S(1)}, u32[]{:S(2)}) copy-start(f32[8,52,200]{2,1,0:T(8,128)S(1)} %copy.9.south) | copy-start | bytes 998404
  4.0 20.3 %collective-permute-start = (f32[304,128]{1,0:T(8,128)}, f32[304,128]{1,0:T(8,128)}, u32[]{:S(2)}, u32[]{:S(2)}) collective-permute-start(f32[304,128]{1,0:T(8,128)} %get-tuple-element.24), channel_id=1, source_target_pairs={{0,1},{1,0},{2,3},{3,2},{4,5},{5,4},{6,7},{7,6},{8,9},{9,8},{10,11... | collective-permute-start | bytes 466952 | tf_op jit(solution)/shard_map/ppermute | solution.py:403
  4.5 19.8 %collective-permute-start.1 = (f32[304,128]{1,0:T(8,128)}, f32[304,128]{1,0:T(8,128)}, u32[]{:S(2)}, u32[]{:S(2)}) collective-permute-start(f32[304,128]{1,0:T(8,128)} %get-tuple-element.25), channel_id=1, source_target_pairs={{0,31},{1,2},{2,1},{3,4},{4,3},{5,6},{6,5},{7,8},{8,7},{9,10},{10,... | collective-permute-start | bytes 466952 | tf_op jit(solution)/shard_map/ppermute | solution.py:403
  11.1 11.0 %collective-permute-start.2 = (f32[260,128]{1,0:T(8,128)S(1)}, f32[260,128]{1,0:T(8,128)}, u32[]{:S(2)}, u32[]{:S(2)}) collective-permute-start(f32[260,128]{1,0:T(8,128)S(1)} %get-tuple-element.30), channel_id=1, source_target_pairs={{0,31},{1,30},{2,29},{3,28},{4,27},{5,26},{6,25},{7,24},{8,23},{9,... | collective-permute-start | bytes 399368 | tf_op jit(solution)/shard_map/ppermute | solution.py:403
  11.2 3.1 %copy-start.1 = (f32[4,9,200,200]{3,2,1,0:T(8,128)S(1)}, f32[4,9,200,200]{3,2,1,0:T(8,128)}, u32[]{:S(2)}) copy-start(f32[4,9,200,200]{3,2,1,0:T(8,128)} %w.1) | copy-start | bytes 17280004
  18.6 2.9 %copy-start.41 = (f32[4,200]{1,0:T(4,128)S(1)}, f32[4,200]{1,0:T(4,128)}, u32[]{:S(2)}) copy-start(f32[4,200]{1,0:T(4,128)} %param.9) | copy-start | bytes 9604
  18.6 2.9 %copy-start.42 = (s32[200]{0:T(256)S(1)}, s32[200]{0:T(256)}, u32[]{:S(2)}) copy-start(s32[200]{0:T(256)} %param.7) | copy-start | bytes 2404
  25.5 19.2 %collective-permute-start.3 = (f32[80,128]{1,0:T(8,128)S(1)}, f32[80,128]{1,0:T(8,128)}, u32[]{:S(2)}, u32[]{:S(2)}) collective-permute-start(f32[80,128]{1,0:T(8,128)S(1)} %corner.1), channel_id=1, source_target_pairs={{0,31},{1,30},{2,29},{3,28},{4,27},{5,26},{6,25},{7,24},{8,23},{9,... | collective-permute-start | bytes 122888 | tf_op jit(solution)/shard_map/ppermute | solution.py:403
  46.1 1.7 %copy-start = (bf16[2,3,768,256]{3,2,1,0:T(8,128)(2,1)S(1)}, bf16[2,3,768,256]{3,2,1,0:T(8,128)(2,1)}, u32[]{:S(2)}) copy-start(bf16[2,3,768,256]{3,2,1,0:T(8,128)(2,1)} %get-tuple-element.61.wh) | copy-start | bytes 7077892
  51.6 4.2 %copy-start.12 = (bf16[2,3,768,256]{3,2,1,0:T(8,128)(2,1)S(1)}, bf16[2,3,768,256]{3,2,1,0:T(8,128)(2,1)}, u32[]{:S(2)}) copy-start(bf16[2,3,768,256]{3,2,1,0:T(8,128)(2,1)} %get-tuple-element.49.wl) | copy-start | bytes 7077892
  51.6 4.2 %copy-start.13 = (bf16[2,3,768,256]{3,2,1,0:T(8,128)(2,1)S(1)}, bf16[2,3,768,256]{3,2,1,0:T(8,128)(2,1)}, u32[]{:S(2)}) copy-start(bf16[2,3,768,256]{3,2,1,0:T(8,128)(2,1)} %get-tuple-element.62.wh) | copy-start | bytes 7077892
  51.6 4.2 %copy-start.39 = (f32[8,2,80,128]{3,2,1,0:T(8,128)S(1)}, f32[8,2,80,128]{3,2,1,0:T(8,128)}, u32[]{:S(2)}) copy-start(f32[8,2,80,128]{3,2,1,0:T(8,128)} %copy-done.38) | copy-start | bytes 1966084
  55.7 16.3 %collective-permute-start.4 = (f32[420,128]{1,0:T(8,128)S(1)}, f32[420,128]{1,0:T(8,128)S(1)}, u32[]{:S(2)}, u32[]{:S(2)}) collective-permute-start(f32[420,128]{1,0:T(8,128)S(1)} %get-tuple-element.35), channel_id=1, source_target_pairs={{0,31},{1,30},{2,29},{3,28},{4,27},{5,26},{6,25},{7,24},{8,23},{9,... | collective-permute-start | bytes 645128 | tf_op jit(solution)/shard_map/ppermute | solution.py:403
  55.8 17.5 %copy-start.2 = (bf16[3,768,256]{2,1,0:T(8,128)(2,1)S(1)}, bf16[3,768,256]{2,1,0:T(8,128)(2,1)}, u32[]{:S(2)}) copy-start(bf16[3,768,256]{2,1,0:T(8,128)(2,1)} %get-tuple-element.59.wh) | copy-start | bytes 3538948
  66.7 14.5 %collective-permute-start.7 = (f32[364,128]{1,0:T(8,128)}, f32[364,128]{1,0:T(8,128)}, u32[]{:S(2)}, u32[]{:S(2)}) collective-permute-start(f32[364,128]{1,0:T(8,128)} %get-tuple-element.41), channel_id=1, source_target_pairs={{0,31},{1,30},{2,29},{3,28},{4,27},{5,26},{6,25},{7,24},{8,23},{9,... | collective-permute-start | bytes 559112 | tf_op jit(solution)/shard_map/ppermute | solution.py:403
  76.7 13.3 %copy-start.3 = (bf16[3,768,256]{2,1,0:T(8,128)(2,1)S(1)}, bf16[3,768,256]{2,1,0:T(8,128)(2,1)}, u32[]{:S(2)}) copy-start(bf16[3,768,256]{2,1,0:T(8,128)(2,1)} %get-tuple-element.43.wl) | copy-start | bytes 3538948
  76.7 13.3 %copy-start.35 = (f32[1,256]{1,0:T(1,128)S(1)}, f32[1,256]{1,0:T(1,128)}, u32[]{:S(2)}) copy-start(f32[1,256]{1,0:T(1,128)} %get-tuple-element.53.bias) | copy-start | bytes 3076
  80.5 7.3 %collective-permute-start.5 = (f32[200,128]{1,0:T(8,128)}, f32[200,128]{1,0:T(8,128)S(1)}, u32[]{:S(2)}, u32[]{:S(2)}) collective-permute-start(f32[200,128]{1,0:T(8,128)} %get-tuple-element.37), channel_id=1, source_target_pairs={{0,1},{1,0},{2,3},{3,2},{4,5},{5,4},{6,7},{7,6},{8,9},{9,8},{10,11... | collective-permute-start | bytes 307208 | tf_op jit(solution)/shard_map/ppermute | solution.py:403
  80.5 8.0 %collective-permute-start.6 = (f32[200,128]{1,0:T(8,128)}, f32[200,128]{1,0:T(8,128)S(1)}, u32[]{:S(2)}, u32[]{:S(2)}) collective-permute-start(f32[200,128]{1,0:T(8,128)} %get-tuple-element.38), channel_id=1, source_target_pairs={{0,31},{1,2},{2,1},{3,4},{4,3},{5,6},{6,5},{7,8},{8,7},{9,10},{10,... | collective-permute-start | bytes 307208 | tf_op jit(solution)/shard_map/ppermute | solution.py:403
  83.0 17.6 %collective-permute-start.8 = (f32[364,128]{1,0:T(8,128)}, f32[364,128]{1,0:T(8,128)}, u32[]{:S(2)}, u32[]{:S(2)}) collective-permute-start(f32[364,128]{1,0:T(8,128)} %copy-done.37), channel_id=1, source_target_pairs={{0,31},{1,30},{2,29},{3,28},{4,27},{5,26},{6,25},{7,24},{8,23},{9,... | collective-permute-start | bytes 559112 | tf_op jit(solution)/shard_map/ppermute | solution.py:403
  89.3 13.2 %collective-permute-start.9 = (f32[208,128]{1,0:T(8,128)}, f32[208,128]{1,0:T(8,128)}, u32[]{:S(2)}, u32[]{:S(2)}) collective-permute-start(f32[208,128]{1,0:T(8,128)} %corner2.1), channel_id=1, source_target_pairs={{0,31},{1,30},{2,29},{3,28},{4,27},{5,26},{6,25},{7,24},{8,23},{9,... | collective-permute-start | bytes 319496 | tf_op jit(solution)/shard_map/ppermute | solution.py:403
  94.4 9.6 %copy-start.5 = (bf16[3,768,256]{2,1,0:T(8,128)(2,1)S(1)}, bf16[3,768,256]{2,1,0:T(8,128)(2,1)}, u32[]{:S(2)}) copy-start(bf16[3,768,256]{2,1,0:T(8,128)(2,1)} %get-tuple-element.60.wh) | copy-start | bytes 3538948
  94.4 9.6 %copy-start.11 = (f32[12,2,64,128]{3,2,1,0:T(8,128)S(1)}, f32[12,2,64,128]{3,2,1,0:T(8,128)}, u32[]{:S(2)}) copy-start(f32[12,2,64,128]{3,2,1,0:T(8,128)} %copy-done.8) | copy-start | bytes 2359300
  (29 other events, 28.4 us)

commit v2 on v1

v2 whole, which is shorter than its diff:
```python
import functools

import jax
import jax.numpy as jnp
from jax import lax
from jax.experimental import pallas as pl
from jax.experimental.pallas import tpu as pltpu
from jax.sharding import PartitionSpec as P

F32 = jnp.float32
BF16 = jnp.bfloat16
LANES = 128
HALF = 64
MW = 64
HALO = 8


def slot_count(rows):
    halves = (rows + 1) // 2
    merged = rows % 2 == 1 and rows <= 8
    return rows + halves + (0 if merged else -(-rows // 16))


def lane_of(width):
    return lax.broadcasted_iota(jnp.int32, (width, LANES), 1)


def roll(x, shift):
    shift = shift % LANES
    return x if shift == 0 else pltpu.roll(x, shift, 1)


def pack(get, put, rows, width, rem):
    lane = lane_of(width)
    halves = (rows + 1) // 2
    merged = rows % 2 == 1 and rows <= 8
    for k in range(rows):
        put(k, get(k, 0))
    second = [get(k, 1) for k in range(rows)]
    for p in range(halves):
        other = roll(second[2 * p + 1], HALF) if 2 * p + 1 < rows else jnp.zeros((width, LANES), F32)
        tile = jnp.where(lane < HALF, second[2 * p], other)
        if merged and p == halves - 1:
            for k in range(rows):
                at = HALF + rem * k
                tile = jnp.where((lane >= at) & (lane < at + rem), roll(second[k], rem * k), tile)
        put(rows + p, tile)
    if not merged:
        for c in range(-(-rows // 16)):
            tile = jnp.zeros((width, LANES), F32)
            for k in range(16 * c, min(rows, 16 * c + 16)):
                at = rem * (k % 16)
                tile = jnp.where((lane >= at) & (lane < at + rem), roll(second[k], at - HALF), tile)
            put(rows + halves + c, tile)


def unpack(slot, k, rows, width, rem):
    lane = lane_of(width)
    halves = (rows + 1) // 2
    merged = rows % 2 == 1 and rows <= 8
    half = roll(slot(rows + k // 2), HALF * (k % 2))
    if merged:
        rest = roll(slot(rows + halves - 1), -rem * k)
    else:
        rest = roll(slot(rows + halves + k // 16), HALF - rem * (k % 16))
    tile = jnp.where(lane < HALF, half, jnp.where(lane < HALF + rem, rest, 0.0))
    return slot(k), tile


def slots_of(ref, width):
    return lambda k: ref[k * width : (k + 1) * width, :]


def putter(ref, width):
    def put(k, tile):
        ref[k * width : (k + 1) * width, :] = tile

    return put


def turned(ref, width, count):
    order = 7 - lax.broadcasted_iota(jnp.int32, (8, LANES), 0)
    flip = lambda x: jnp.take_along_axis(x, order, axis=0)

    def one(k):
        parts, left = [], width
        while left >= 8:
            parts.append(flip(ref[k * width + left - 8 : k * width + left, :]))
            left -= 8
        if left:
            parts.append(flip(ref[k * width : k * width + 8, :])[8 - left :])
        return jnp.concatenate(parts, axis=0)

    tiles = [one(k) for k in range(count)]
    return lambda k: tiles[k]


def fill(hi, lo, dst, ref, src, count, offs):
    def body(i, carry):
        for b in range(3):
            for t in range(2):
                x = ref[src + i, t, offs[b] : offs[b] + MW, :]
                h = x.astype(BF16)
                at = b * 2 * LANES + t * LANES
                hi[dst + i, :, at : at + LANES] = h
                lo[dst + i, :, at : at + LANES] = (x - h.astype(F32)).astype(BF16)
        return carry

    lax.fori_loop(0, count, body, 0)


def products(hi, lo, wh, wl, taps, row, chunk, dilate):
    total = None
    for a in taps:
        at = pl.ds(row + a * dilate, chunk)
        lh = hi[at].reshape(chunk * MW, hi.shape[-1])
        ll = lo[at].reshape(chunk * MW, hi.shape[-1])
        for left, right in ((lh, wh), (ll, wh), (lh, wl)):
            term = jnp.dot(left, right[a], preferred_element_type=F32)
            total = term if total is None else total + term
    return total


def conv(hi, lo, wh, wl, bias, dilate, base, count, chunk, emit):
    def body(i, carry):
        row = i * chunk
        total = products(hi, lo, wh, wl, (0, 1, 2), base + row, chunk, dilate)
        emit(row, jax.nn.gelu(total + bias))
        return carry

    if count == chunk:
        body(0, 0)
    else:
        lax.fori_loop(0, count // chunk, body, 0)


def add_rows(out, out_row, res, res_row, off, chunk):
    def emit(row, grown):
        for q in range(chunk):
            for t in range(2):
                out[out_row + row + q, t, 0:MW, :] = (
                    res[res_row + row + q, t, off : off + MW, :]
                    + grown[q * MW : (q + 1) * MW, t * LANES : (t + 1) * LANES]
                )

    return emit


def put_row(dst, row, at, tiles):
    for t in range(2):
        dst[row, t, at : at + tiles[t].shape[0], :] = tiles[t]


def widen(x):
    return jnp.concatenate([x, jnp.zeros(x.shape[:-1] + (LANES - x.shape[-1],), F32)], axis=-1)


def tile_at(ref, col, lo, hi, t):
    return ref[col, lo:hi, 0:LANES] if t == 0 else widen(ref[col, lo:hi, LANES : ref.shape[-1]])


def strided(dst, first, t, col):
    rows, _, width, _ = dst.shape
    return dst.reshape(rows * 2 * width, LANES), pl.ds((2 * first + t) * width + col, 8, stride=2 * width)


def put_column(dst, first, col, t, tile):
    flat, at = strided(dst, first, t, col)
    flat[at, :] = tile


def get_column(src, first, col, t):
    flat, at = strided(src, first, t, col)
    return flat[at, :]


def lanes_of(ref, row):
    x = ref[row : row + 1, :].astype(F32)
    return [x[:, 0:LANES], widen(x[:, LANES:])]


def bias_of(ref, row):
    return jnp.concatenate(lanes_of(ref, row), axis=1)


def k_first(par, field, south, main, ewi, ewc, top):
    cols, rows, channels = field.shape
    rem = channels - LANES - HALF
    even = par[0] == 0

    def edge(flip):
        def get(k, t):
            pick = []
            for col in (k, cols - HALO + k):
                tiles = [tile_at(field, col, 0, rows, t), tile_at(south, col, 0, south.shape[1], t)]
                pick.append(jnp.concatenate(tiles, axis=0))
            return jnp.where(even != flip, pick[1], pick[0])

        return get

    tall = rows + south.shape[1]
    pack(edge(False), putter(ewi, tall), HALO, tall, rem)
    pack(edge(True), putter(ewc, tall), HALO, tall, rem)
    for col in range(cols):
        for t in range(2):
            put_column(top, 0, col, t, tile_at(field, col, rows - 8, rows, t))
    pack(lambda k, t: top[7 - k, t, 0:cols, :], putter(main, cols), 3, cols, rem)


def k_weights(w, *refs):
    layers, _, channels, _ = w.shape
    outs, (buf, sems) = refs[: 2 * layers], refs[2 * layers :]
    copies = [pltpu.make_async_copy(w.at[i], buf.at[i], sems.at[i]) for i in range(layers)]
    for copy in copies:
        copy.start()
    for i in range(layers):
        wh, wl = outs[2 * i : 2 * i + 2]
        copies[i].wait()
        for k in range(9):
            x = buf[i, k]
            h = x.astype(BF16)
            at = (k % 3) * 2 * LANES
            for ref, value in ((wh, h), (wl, (x - h.astype(F32)).astype(BF16))):
                wide = jnp.concatenate([value, jnp.zeros((channels, 2 * LANES - channels), BF16)], axis=1)
                ref[k // 3, at : at + channels, :] = wide
                ref[k // 3, at + channels : at + 2 * LANES, :] = jnp.zeros((2 * LANES - channels, 2 * LANES), BF16)


def sided(par, ewi, ewc, width, count):
    even = par[0] == 0
    i, c = slots_of(ewi, width), slots_of(ewc, width)
    west = [jnp.where(even, c(k), i(k)) for k in range(count)]
    east = [jnp.where(even, i(k), c(k)) for k in range(count)]
    return (lambda k: west[k]), (lambda k: east[k])


def k_corner(par, ewi, ewc, out, top, *, tall, rows, rem):
    west, east = sided(par, ewi, ewc, tall, slot_count(HALO))
    for side, slot in enumerate((west, east)):
        for k in range(HALO):
            tiles = unpack(slot, k, HALO, tall, rem)
            for t in range(2):
                put_column(top, 0, side * HALO + k, t, tiles[t][rows - 8 : rows])
    pack(lambda k, t: top[7 - k, t], putter(out, 2 * HALO), 3, 2 * HALO, rem)


def k_corner2(par, ewi, ewc, out, *, rows, rem):
    west, east = sided(par, ewi, ewc, HALO, slot_count(rows))
    tiles = []
    for k in range(8):
        w = unpack(west, rows - 1 - k, rows, HALO, rem)
        e = unpack(east, rows - 1 - k, rows, HALO, rem)
        tiles.append([jnp.concatenate([w[t], e[t]], axis=0) for t in range(2)])
    pack(lambda k, t: tiles[k][t], putter(out, 2 * HALO), 8, 2 * HALO, rem)


def k_a(par, field, south, ewi, ewc, wh, wl, bias, st1, se, edge0, x0, hi, lo):
    cols, rows, channels = field.shape
    rem = channels - LANES - HALF
    deep = south.shape[1]
    west, east = sided(par, ewi, ewc, rows + deep, slot_count(HALO))

    def put(col, tiles):
        for t in range(2):
            for h in range(0, rows, 8):
                put_column(x0, h, col, t, tiles[t][h : h + 8])
            put_column(se, 0, col, t, tiles[t][rows : rows + 8])

    for k in range(HALO):
        put(k, unpack(west, k, HALO, rows + deep, rem))
        put(HALO + cols + k, unpack(east, k, HALO, rows + deep, rem))
    for col in range(cols):
        for t in range(2):
            for h in range(0, rows, 8):
                put_column(x0, h, HALO + col, t, tile_at(field, col, h, h + 8, t))
            put_column(se, 0, HALO + col, t, tile_at(south, col, 0, 8, t))
    edge0[...] = x0[rows - 2 :]
    offs = (1, 2, 3)
    fill(hi, lo, 0, se, deep - 1, 1, offs)
    fill(hi, lo, 1, x0, 0, rows, offs)
    conv(hi, lo, wh, wl, bias_of(bias, 0), 1, 0, rows - 1, 5, add_rows(st1, 0, x0, 0, 2, 5))


def signed(tiles, sign):
    return tiles if sign is None else [tiles[t] * sign[t] for t in range(2)]


def north_rows(dst, dst_row, main, sign, count, width, left, rem):
    slot = turned(main, width, slot_count(count))
    for k in range(count):
        put_row(dst, dst_row + k, left, signed(unpack(slot, k, count, width, rem), sign))


def north_corners(dst, dst_row, corner, sign, count, cols, left, rem):
    width = 2 * HALO
    slot = turned(corner, width, slot_count(count))
    for k in range(count):
        t = signed(unpack(slot, k, count, width, rem), sign)
        put_row(dst, dst_row + k, left - HALO, [x[0:HALO] for x in t])
        put_row(dst, dst_row + k, left + cols, [x[HALO:] for x in t])


def k_b(edge0, main, corner, st1, sign, wh0, wl0, wh1, wl1, bias, st2, out, x0, xr, x1, hi, lo, *, cols, rem):
    rows = st1.shape[0] + 1
    sign = lanes_of(sign, 0)
    north_rows(xr, 1, main, None, 3, cols, HALO, rem)
    north_corners(xr, 1, corner, None, 3, cols, HALO, rem)
    x0[0:2] = edge0[...]
    for t in range(2):
        x0[2, t] = xr[1, t] * sign[t]
        xr[0, t] = edge0[1, t] * sign[t]
    x1[0:5] = st1[rows - 6 : rows - 1]
    offs = (1, 2, 3)
    fill(hi, lo, 0, x0, 0, 3, offs)
    fill(hi, lo, 3, xr, 0, 4, offs[::-1])
    total = None
    for a in range(3):
        both = [jnp.concatenate([x[a : a + 1], x[5 - a : 7 - a]]).reshape(3 * MW, x.shape[-1]) for x in (hi, lo)]
        for left, right in ((both[0], wh0), (both[1], wh0), (both[0], wl0)):
            term = jnp.dot(left, right[a], preferred_element_type=F32)
            total = term if total is None else total + term
    grown = jax.nn.gelu(total + bias_of(bias, 0))
    for q in range(3):
        for t in range(2):
            g = grown[q * MW : (q + 1) * MW, t * LANES : (t + 1) * LANES]
            if q == 0:
                x1[5, t, 0:MW, :] = x0[1, t, 2 : 2 + MW, :] + g
            else:
                x1[5 + q, t, 0:MW, :] = sign[t] * (xr[q, t, 2 : 2 + MW, :] + g)
    fill(hi, lo, 0, x1, 0, 8, (0, 2, 4))
    conv(hi, lo, wh1, wl1, bias_of(bias, 1), 2, 0, 4, 4, add_rows(st2, 0, x1, 2, 2, 4))
    wide = cols + 8
    pack(lambda k, t: st2[3 - k, t, 0:wide, :], putter(out, wide), 4, wide, rem)


def k_c(st1, st2b, se, wh1, wl1, wh2, wl2, bias, st2, st3, out, hi, lo, *, cols, rem):
    south = se.shape[0]
    rows = st2.shape[0]
    low = rows - 4
    fill(hi, lo, 0, se, south - 2, 2, (2, 4, 6))
    fill(hi, lo, 2, st1, 0, low + 2, (0, 2, 4))
    conv(hi, lo, wh1, wl1, bias_of(bias, 1), 2, 0, low, 4, add_rows(st2, 0, st1, 0, 2, 4))
    st2[low:rows] = st2b[...]
    fill(hi, lo, 0, se, south - 4, 4, (4, 8, 12))
    fill(hi, lo, 4, st2, 0, rows, (0, 4, 8))
    conv(hi, lo, wh2, wl2, bias_of(bias, 2), 4, 0, low, 4, add_rows(st3, 0, st2, 0, 4, 4))
    pack(lambda k, t: st3[low - 1 - k, t, 0:cols, :], putter(out, cols), 4, cols, rem)


def k_d(par, st2, north, st3a, sign, wh, wl, bias, st3b, out, ewi, ewc, x2, hi, lo, *, cols, rem):
    rows = st2.shape[0]
    wide = cols + 8
    north_rows(x2, 0, north, lanes_of(sign, 0), 4, wide, 0, rem)
    fill(hi, lo, 0, st2, rows - 8, 8, (0, 4, 8))
    fill(hi, lo, 8, x2, 0, 4, (0, 4, 8))
    conv(hi, lo, wh, wl, bias_of(bias, 2), 4, 0, 4, 4, add_rows(st3b, 0, st2, rows - 4, 4, 4))
    pack(lambda k, t: st3b[3 - k, t, 0:cols, :], putter(out, cols), 4, cols, rem)
    even = par[0] == 0

    def edge(flip):
        def get(k, t):
            ref, row = (st3a, k) if k < rows - 4 else (st3b, k - rows + 4)
            west, east = ref[row, t, 0:HALO, :], ref[row, t, cols - HALO : cols, :]
            return jnp.where(even != flip, east, west)

        return get

    pack(edge(False), putter(ewi, HALO), rows, HALO, rem)
    pack(edge(True), putter(ewc, HALO), rows, HALO, rem)


def put_out(out, first, src, cols, channels):
    for col in range(cols):
        out[col, first : first + 8, 0:LANES] = get_column(src, 0, col, 0)
        out[col, first : first + 8, LANES:channels] = get_column(src, 0, col, 1)[:, 0 : channels - LANES]


def k_f(par, st3a, st3b, ewi, ewc, se, wh, wl, bias, outlo, acc, x3, end, hi, lo, *, cols, channels):
    rem = channels - LANES - HALF
    rows = x3.shape[0]
    south = se.shape[0]
    west, east = sided(par, ewi, ewc, HALO, slot_count(rows))
    for k in range(rows):
        ref, row = (st3a, k) if k < rows - 4 else (st3b, k - rows + 4)
        put_row(x3, k, 0, unpack(west, k, rows, HALO, rem))
        put_row(x3, k, HALO, [ref[row, t, 0:cols, :] for t in range(2)])
        put_row(x3, k, HALO + cols, unpack(east, k, rows, HALO, rem))
    offs = (0, 8, 16)
    fill(hi, lo, 0, se, 0, south, offs)
    fill(hi, lo, south, x3, 0, rows, offs)
    bias = bias_of(bias, 3)
    conv(hi, lo, wh, wl, bias, 8, 0, rows - 8, 4, add_rows(end, 0, x3, 0, 8, 4))

    def body(i, carry):
        total = products(hi, lo, wh, wl, (0, 1), rows - 8 + 4 * i, 4, 8)
        acc[pl.ds(4 * i, 4)] = (total + bias).reshape(4, MW, 2 * LANES)
        return carry

    lax.fori_loop(0, 2, body, 0)
    put_out(outlo, 0, end, cols, channels)


def k_g(outlo, acc, st3a, st3b, na, nb, nc, sign, wh, wl, out, xn, end, hi, lo, *, rem):
    cols, rows, channels = out.shape
    sign = lanes_of(sign, 0)
    north_rows(xn, 0, nb, sign, 4, cols, HALO, rem)
    north_rows(xn, 4, na, sign, 4, cols, HALO, rem)
    north_corners(xn, 0, nc, sign, 8, cols, HALO, rem)
    out[:, 0 : rows - 8, :] = outlo[...]
    fill(hi, lo, 0, xn, 0, 8, (0, 8, 16))
    for i in range(2):
        at = pl.ds(4 * i, 4)
        lh = hi[at].reshape(4 * MW, hi.shape[-1])
        ll = lo[at].reshape(4 * MW, hi.shape[-1])
        total = acc[at].reshape(4 * MW, 2 * LANES)
        for left, right in ((lh, wh), (ll, wh), (lh, wl)):
            total = total + jnp.dot(left, right[2], preferred_element_type=F32)
        grown = jax.nn.gelu(total)
        for q in range(4):
            r = rows - 8 + 4 * i + q
            ref, row = (st3a, r) if r < rows - 4 else (st3b, r - rows + 4)
            for t in range(2):
                end[4 * i + q, t] = ref[row, t] + grown[q * MW : (q + 1) * MW, t * LANES : (t + 1) * LANES]
    put_out(out, rows - 8, end, cols, channels)


VM = pl.BlockSpec(memory_space=pltpu.VMEM)
SM = pl.BlockSpec(memory_space=pltpu.SMEM)


def lhs(rows):
    return [pltpu.VMEM((rows, MW, 6 * LANES), BF16)] * 2


def call(kernel, outs, scratch, args, smem=0, flops=0, limit=16, name=None):
    moved = sum(a.size * a.dtype.itemsize for a in args[smem:])
    outs = [o if isinstance(o, jax.ShapeDtypeStruct) else jax.ShapeDtypeStruct(o, F32) for o in outs]
    return pl.pallas_call(
        kernel,
        out_shape=outs,
        in_specs=[SM] * smem + [VM if name != "weights" else pl.BlockSpec(memory_space=pl.ANY)] * (len(args) - smem),
        out_specs=[VM] * len(outs),
        scratch_shapes=scratch,
        compiler_params=pltpu.CompilerParams(vmem_limit_bytes=limit * 2**20),
        cost_estimate=pl.CostEstimate(flops=flops, bytes_accessed=moved, transcendentals=0),
        name=name,
    )(*args)


def local(field, south_rows, sign_mask, weights, biases):
    rows, cols, channels = field.shape
    south = south_rows.shape[0]
    layers = weights.shape[0]
    rem = channels - LANES - HALF
    devices = lax.axis_size("lon")
    mirror = [(i, devices - 1 - i) for i in range(devices)]
    intra = [(i, i ^ 1) for i in range(devices)]
    cross = [(i, (i + 1) % devices if i % 2 else (i - 1) % devices) for i in range(devices)]
    send = lambda x, route: lax.ppermute(x, "lon", route)
    par = (lax.axis_index("lon") % 2).astype(jnp.int32).reshape(1)
    sign = sign_mask.reshape(1, channels)
    field = jnp.swapaxes(field, 0, 1)
    south_rows = jnp.swapaxes(south_rows, 0, 1)
    row_flops = MW * 6 * LANES * 2 * LANES * 2 * 9
    tall = rows + south

    def state(n, width):
        return (n, 2, width, LANES)

    ew_rows = slot_count(HALO) * tall
    main, ewi, ewc = call(
        k_first,
        [(slot_count(3) * cols, LANES), (ew_rows, LANES), (ew_rows, LANES)],
        [pltpu.VMEM(state(8, 56), F32)], [par, field, south_rows], smem=1, name="first",
    )
    ewi, ewc, main = send(ewi, intra), send(ewc, cross), send(main, mirror)
    split = call(
        k_weights,
        [jax.ShapeDtypeStruct((3, 6 * LANES, 2 * LANES), BF16)] * (2 * layers),
        [pltpu.VMEM(weights.shape, F32), pltpu.SemaphoreType.DMA((layers,))],
        [weights], name="weights", limit=24,
    )
    (corner,) = call(
        functools.partial(k_corner, tall=tall, rows=rows, rem=rem),
        [(slot_count(3) * 2 * HALO, LANES)], [pltpu.VMEM(state(8, 2 * HALO), F32)],
        [par, ewi, ewc], smem=1, name="corner",
    )
    corner = send(corner, mirror)
    st1, se, edge0 = call(
        k_a,
        [state(rows - 1, 72), state(south, 80), state(2, 72)],
        [pltpu.VMEM(state(rows, 72), F32)] + lhs(rows + 1),
        [par, field, south_rows, ewi, ewc, *split[0:2], biases],
        smem=1, flops=(rows - 1) * row_flops, name="a",
    )
    st2b, north = call(
        functools.partial(k_b, cols=cols, rem=rem),
        [state(4, 72), (slot_count(4) * (cols + 8), LANES)],
        [pltpu.VMEM(state(3, 72), F32), pltpu.VMEM(state(4, 72), F32), pltpu.VMEM(state(8, 72), F32)] + lhs(8),
        [edge0, main, corner, st1, sign, *split[0:4], biases],
        flops=7 * row_flops, name="b",
    )
    north = send(north, mirror)
    st2, st3a, na = call(
        functools.partial(k_c, cols=cols, rem=rem),
        [state(rows, 72), state(rows - 4, MW), (slot_count(4) * cols, LANES)],
        lhs(rows + 4),
        [st1, st2b, se, *split[2:6], biases],
        flops=(2 * rows - 8) * row_flops, name="c",
    )
    na = send(na, mirror)
    ew_rows = slot_count(rows) * HALO
    st3b, nb, ewi, ewc = call(
        functools.partial(k_d, cols=cols, rem=rem),
        [state(4, MW), (slot_count(4) * cols, LANES), (ew_rows, LANES), (ew_rows, LANES)],
        [pltpu.VMEM(state(4, 72), F32)] + lhs(12),
        [par, st2, north, st3a, sign, *split[4:6], biases],
        smem=1, flops=4 * row_flops, name="d",
    )
    ewi, ewc, nb = send(ewi, intra), send(ewc, cross), send(nb, mirror)
    (nc,) = call(
        functools.partial(k_corner2, rows=rows, rem=rem),
        [(slot_count(8) * 2 * HALO, LANES)], [], [par, ewi, ewc], smem=1, name="corner2",
    )
    nc = send(nc, mirror)
    outlo, acc = call(
        functools.partial(k_f, cols=cols, channels=channels),
        [(cols, rows - 8, channels), (8, MW, 2 * LANES)],
        [pltpu.VMEM(state(rows, 80), F32), pltpu.VMEM(state(8, MW), F32)] + lhs(rows + south),
        [par, st3a, st3b, ewi, ewc, se, *split[6:8], biases],
        smem=1, flops=(rows - 3) * row_flops, name="f",
    )
    (out,) = call(
        functools.partial(k_g, rem=rem),
        [(cols, rows, channels)],
        [pltpu.VMEM(state(8, 80), F32), pltpu.VMEM(state(8, MW), F32)] + lhs(8),
        [outlo, acc, st3a, st3b, na, nb, nc, sign, *split[6:8]],
        flops=3 * row_flops, name="g",
    )
    return jnp.swapaxes(out, 0, 1)


def solution(mesh):
    in_specs = (P(None, "lon", None), P(None, "lon", None), P(), P(), P())
    out_specs = P(None, "lon", None)
    return jax.shard_map(local, mesh=mesh, in_specs=in_specs, out_specs=out_specs, check_vma=False)
```

time: 112 us -> 70.2 us (0.63)
  the two profiles are of different devices: /device:TPU:0 before, /device:TPU:9 now
where the time goes in v2:
time: 70.2 us; the launch traced here: 70 us
  Pallas kernels  29.3 us (42%)
  waiting for transfers between devices  22.5 us (32%)
  starting transfers between devices  12.9 us (18%)
  local copies, waits for them, and re-layouts  5.27 us (8%)
    pallas_call x10, Pallas kernels, call(): pl.pallas_call(kernel, out_shape=outs, in_specs=[SM] * smem + [VM if name...  29.3 us
    ppermute x10, waiting for transfers between devices, local(): send = lambda x, route: lax.ppermute(x, 'lon', route)  22.5 us
    ppermute x10, starting transfers between devices, local(): send = lambda x, route: lax.ppermute(x, 'lon', route)  12.9 us
    unnamed x14, local copies, waits for them, and re-layouts  5.27 us
  transfers between devices with their start and end apart: 10, of which 5 were waited for; matrix products, arithmetic and copies ran while one was open for 0% of the time, Pallas kernels for 30%

profile of v2, /device:TPU:9, one launch (start us, length us, event | category | flops | bytes accessed | tf_op | source)
XLA Modules:
  0.0 70.0 jit_solution(14014300883191365612)
XLA Ops:
  0.0 1.2 %copy-done.1 = f32[16,52,200]{2,0,1:T(8,128)S(1)} copy-done((f32[16,52,200]{2,0,1:T(8,128)S(1)}, f32[16,52,200]{2,0,1:T(8,128)}, u32[]{:S(2)}) %copy-start.1) | copy-done | bytes 665624
  1.2 1.0 %copy-done.3 = f32[8,52,200]{2,0,1:T(8,128)S(1)} copy-done((f32[8,52,200]{2,0,1:T(8,128)S(1)}, f32[8,52,200]{2,0,1:T(8,128)}, u32[]{:S(2)}) %copy-start.3) | copy-done | bytes 332824
  2.4 0.7 %collective-permute-start = (f32[312,128]{1,0:T(8,128)S(1)}, f32[312,128]{1,0:T(8,128)S(1)}, u32[]{:S(2)}, u32[]{:S(2)}) collective-permute-start(f32[312,128]{1,0:T(8,128)S(1)} %get-tuple-element.30), channel_id=1, source_target_pairs={{0,1},{1,0},{2,3},{3,2},{4,5},{5,4},{6,7},{7,6},{8,9},{9,8},{10,11... | collective-permute-start | bytes 479240 | tf_op jit(solution)/shard_map/ppermute | solution.py:459
  3.1 1.2 %collective-permute-start.1 = (f32[312,128]{1,0:T(8,128)S(1)}, f32[312,128]{1,0:T(8,128)S(1)}, u32[]{:S(2)}, u32[]{:S(2)}) collective-permute-start(f32[312,128]{1,0:T(8,128)S(1)} %get-tuple-element.31), channel_id=1, source_target_pairs={{0,31},{1,2},{2,1},{3,4},{4,3},{5,6},{6,5},{7,8},{8,7},{9,10},{10,... | collective-permute-start | bytes 479240 | tf_op jit(solution)/shard_map/ppermute | solution.py:459
  4.3 2.5 %collective-permute-start.2 = (f32[260,128]{1,0:T(8,128)S(1)}, f32[260,128]{1,0:T(8,128)S(1)}, u32[]{:S(2)}, u32[]{:S(2)}) collective-permute-start(f32[260,128]{1,0:T(8,128)S(1)} %get-tuple-element.36), channel_id=1, source_target_pairs={{0,31},{1,30},{2,29},{3,28},{4,27},{5,26},{6,25},{7,24},{8,23},{9,... | collective-permute-start | bytes 399368 | tf_op jit(solution)/shard_map/ppermute | solution.py:459
  6.8 3.1 %copy-done = f32[4,9,200,200]{3,2,1,0:T(8,128)S(1)} copy-done((f32[4,9,200,200]{3,2,1,0:T(8,128)S(1)}, f32[4,9,200,200]{3,2,1,0:T(8,128)}, u32[]{:S(2)}) %copy-start) | copy-done | bytes 5760024
  9.9 1.9 %weights.1 = (bf16[3,768,256]{2,1,0:T(8,128)(2,1)S(1)}, bf16[3,768,256]{2,1,0:T(8,128)(2,1)S(1)}, bf16[3,768,256]{2,1,0:T(8,128)(2,1)S(1)}, bf16[3,768,256]{2,1,...) custom-call(f32[4,9,200,200]{3,2,1,0:T(8,128)S(1)} %copy-done), custom_call_target="tpu_custom_call" | custom-call | bytes 5760000 | tf_op jit(solution)/shard_map/weights/pallas_call | solution.py:438
  12.1 2.2 %collective-permute-start.3 = (f32[80,128]{1,0:T(8,128)S(1)}, f32[80,128]{1,0:T(8,128)S(1)}, u32[]{:S(2)}, u32[]{:S(2)}) collective-permute-start(f32[80,128]{1,0:T(8,128)S(1)} %corner.1), channel_id=1, source_target_pairs={{0,31},{1,30},{2,29},{3,28},{4,27},{5,26},{6,25},{7,24},{8,23},{9,... | collective-permute-start | bytes 122888 | tf_op jit(solution)/shard_map/ppermute | solution.py:459
  14.3 5.4 %a.1 = (f32[15,2,72,128]{3,2,1,0:T(8,128)S(1)}, f32[8,2,80,128]{3,2,1,0:T(8,128)S(1)}, f32[2,2,72,128]{3,2,1,0:T(8,128)S(1)}) custom-call(s32[1]{0:T(128)} %bitcast.par, f32[52,16,200]{2,1,0:T(8,128)S(1)} %bitcast.6, f32[52,8,200]{2,1,0:T(8,128)S(1)} %bitcast.8, f32[312,128]{1,0:T(8,128)S(1)} %collective-permute-done.ewi, ...), custom_call_target="tpu_custom_call" | custom-call | flops 3397386240 | bytes 3680384 | tf_op jit(solution)/shard_map/a/pallas_call | solution.py:438
  19.7 4.1 %b.1 = (f32[4,2,72,128]{3,2,1,0:T(8,128)S(1)}, f32[420,128]{1,0:T(8,128)S(1)}) custom-call(f32[2,2,72,128]{3,2,1,0:T(8,128)S(1)} %get-tuple-element.35.edge0, f32[260,128]{1,0:T(8,128)S(1)} %collective-permute-done.2.main, f32[80,128]{1,0:T(8,128)S(1)} %collective-permute-done.3.corner, f32[15,2,72,128]{3,2,1,0:T(8,128)S(1)} %get-tuple-element.34.st1, ...), custom_call_target="tpu_custom_call" | custom-call | flops 1585446912 | bytes 6150048 | tf_op jit(solution)/shard_map/b/pallas_call | solution.py:438
  23.8 1.4 %collective-permute-start.4 = (f32[420,128]{1,0:T(8,128)S(1)}, f32[420,128]{1,0:T(8,128)S(1)}, u32[]{:S(2)}, u32[]{:S(2)}) collective-permute-start(f32[420,128]{1,0:T(8,128)S(1)} %get-tuple-element.45), channel_id=1, source_target_pairs={{0,31},{1,30},{2,29},{3,28},{4,27},{5,26},{6,25},{7,24},{8,23},{9,... | collective-permute-start | bytes 645128 | tf_op jit(solution)/shard_map/ppermute | solution.py:459
  25.2 8.2 %c.1 = (f32[16,2,72,128]{3,2,1,0:T(8,128)S(1)}, f32[12,2,64,128]{3,2,1,0:T(8,128)S(1)}, f32[364,128]{1,0:T(8,128)S(1)}) custom-call(f32[15,2,72,128]{3,2,1,0:T(8,128)S(1)} %get-tuple-element.34.st1, f32[4,2,72,128]{3,2,1,0:T(8,128)S(1)} %get-tuple-element.39.st2b, f32[8,2,80,128]{3,2,1,0:T(8,128)S(1)} %get-tuple-element.40.se, ...), custom_call_target="tpu_custom_call" | custom-call | flops 5435817984 | bytes 6777984 | tf_op jit(solution)/shard_map/c/pallas_call | solution.py:438
  33.4 4.7 %collective-permute-done.4.north = f32[420,128]{1,0:T(8,128)S(1)} collective-permute-done((f32[420,128]{1,0:T(8,128)S(1)}, f32[420,128]{1,0:T(8,128)S(1)}, u32[]{:S(2)}, u32[]{:S(2)}) %collective-permute-start.4) | collective-permute-done | bytes 215072 | tf_op jit(solution)/shard_map/ppermute | solution.py:459
  38.1 1.7 %d.1 = (f32[4,2,64,128]{3,2,1,0:T(8,128)S(1)}, f32[364,128]{1,0:T(8,128)S(1)}, f32[200,128]{1,0:T(8,128)S(1)}, f32[200,128]{1,0:T(8,128)S(1)}) custom-call(s32[1]{0:T(128)} %bitcast.par, f32[16,2,72,128]{3,2,1,0:T(8,128)S(1)} %get-tuple-element.44.st2, f32[420,128]{1,0:T(8,128)S(1)} %collective-permute-done.4.north, ...), custom_call_target="tpu_custom_call" | custom-call | flops 905969664 | bytes 4544416 | tf_op jit(solution)/shard_map/d/pallas_call | solution.py:438
  39.9 0.6 collective-permute-start.5
  40.5 0.6 collective-permute-start.6
  41.1 1.3 %collective-permute-start.7 = (f32[364,128]{1,0:T(8,128)S(1)}, f32[364,128]{1,0:T(8,128)S(1)}, u32[]{:S(2)}, u32[]{:S(2)}) collective-permute-start(f32[364,128]{1,0:T(8,128)S(1)} %get-tuple-element.53), channel_id=1, source_target_pairs={{0,31},{1,30},{2,29},{3,28},{4,27},{5,26},{6,25},{7,24},{8,23},{9,... | collective-permute-start | bytes 559112 | tf_op jit(solution)/shard_map/ppermute | solution.py:459
  42.4 2.3 %collective-permute-start.8 = (f32[364,128]{1,0:T(8,128)S(1)}, f32[364,128]{1,0:T(8,128)S(1)}, u32[]{:S(2)}, u32[]{:S(2)}) collective-permute-start(f32[364,128]{1,0:T(8,128)S(1)} %get-tuple-element.54), channel_id=1, source_target_pairs={{0,31},{1,30},{2,29},{3,28},{4,27},{5,26},{6,25},{7,24},{8,23},{9,... | collective-permute-start | bytes 559112 | tf_op jit(solution)/shard_map/ppermute | solution.py:459
  44.6 1.6 %collective-permute-done.6.ewc = f32[200,128]{1,0:T(8,128)S(1)} collective-permute-done((f32[200,128]{1,0:T(8,128)S(1)}, f32[200,128]{1,0:T(8,128)S(1)}, u32[]{:S(2)}, u32[]{:S(2)}) %collective-permute-start.6) | collective-permute-done | bytes 102432 | tf_op jit(solution)/shard_map/ppermute | solution.py:459
  46.5 4.9 %f.1 = (f32[52,8,200]{2,1,0:T(8,128)S(1)}, f32[8,64,256]{2,1,0:T(8,128)S(1)}) custom-call(s32[1]{0:T(128)} %bitcast.par, f32[12,2,64,128]{3,2,1,0:T(8,128)S(1)} %get-tuple-element.43.st3a, f32[4,2,64,128]{3,2,1,0:T(8,128)S(1)} %get-tuple-element.46.st3b, f32[200,128]{1,0:T(8,128)S(1)} %collective-permute-done.5.ewi, ...), custom_call_target="tpu_custom_call" | custom-call | flops 2944401408 | bytes 4271232 | tf_op jit(solution)/shard_map/f/pallas_call | solution.py:438
  51.4 9.8 %collective-permute-done.7.na = f32[364,128]{1,0:T(8,128)S(1)} collective-permute-done((f32[364,128]{1,0:T(8,128)S(1)}, f32[364,128]{1,0:T(8,128)S(1)}, u32[]{:S(2)}, u32[]{:S(2)}) %collective-permute-start.7) | collective-permute-done | bytes 186400 | tf_op jit(solution)/shard_map/ppermute | solution.py:459
  61.2 4.0 %collective-permute-done.8.nb = f32[364,128]{1,0:T(8,128)S(1)} collective-permute-done((f32[364,128]{1,0:T(8,128)S(1)}, f32[364,128]{1,0:T(8,128)S(1)}, u32[]{:S(2)}, u32[]{:S(2)}) %collective-permute-start.8) | collective-permute-done | bytes 186400 | tf_op jit(solution)/shard_map/ppermute | solution.py:459
  65.3 2.2 %collective-permute-done.9.nc = f32[208,128]{1,0:T(8,128)S(1)} collective-permute-done((f32[208,128]{1,0:T(8,128)S(1)}, f32[208,128]{1,0:T(8,128)S(1)}, u32[]{:S(2)}, u32[]{:S(2)}) %collective-permute-start.9) | collective-permute-done | bytes 106528 | tf_op jit(solution)/shard_map/ppermute | solution.py:459
  67.5 2.5 %g.1 = f32[52,16,200]{2,1,0:T(8,128)} custom-call(f32[52,8,200]{2,1,0:T(8,128)S(1)} %get-tuple-element.51.outlo, f32[8,64,256]{2,1,0:T(8,128)S(1)} %get-tuple-element.52.acc, f32[12,2,64,128]{3,2,1,0:T(8,128)S(1)} %get-tuple-element.43.st3a, f32[4,2,64,128]{3,2,1,0:T(8,128)S(1)} %get-tuple-element.46.st3b, f32[364,128]{1,0:T(8,128)S(1)} %collective-permute-done.7.na, ...), custom_call_target="tpu_custom_call" | custom-call | flops 679477248 | bytes 4744992 | tf_op jit(solution)/shard_map/g/pallas_call | solution.py:438
  (20 shorter events, 0.7 us)
Async XLA Ops:
  0.0 1.2 %copy-start.1 = (f32[16,52,200]{2,0,1:T(8,128)S(1)}, f32[16,52,200]{2,0,1:T(8,128)}, u32[]{:S(2)}) copy-start(f32[16,52,200]{2,0,1:T(8,128)} %param.5) | copy-start | bytes 1996804
  1.2 1.0 %copy-start.3 = (f32[8,52,200]{2,0,1:T(8,128)S(1)}, f32[8,52,200]{2,0,1:T(8,128)}, u32[]{:S(2)}) copy-start(f32[8,52,200]{2,0,1:T(8,128)} %param.6) | copy-start | bytes 998404
  2.4 9.5 %collective-permute-start = (f32[312,128]{1,0:T(8,128)S(1)}, f32[312,128]{1,0:T(8,128)S(1)}, u32[]{:S(2)}, u32[]{:S(2)}) collective-permute-start(f32[312,128]{1,0:T(8,128)S(1)} %get-tuple-element.30), channel_id=1, source_target_pairs={{0,1},{1,0},{2,3},{3,2},{4,5},{5,4},{6,7},{7,6},{8,9},{9,8},{10,11... | collective-permute-start | bytes 479240 | tf_op jit(solution)/shard_map/ppermute | solution.py:459
  3.1 8.8 %collective-permute-start.1 = (f32[312,128]{1,0:T(8,128)S(1)}, f32[312,128]{1,0:T(8,128)S(1)}, u32[]{:S(2)}, u32[]{:S(2)}) collective-permute-start(f32[312,128]{1,0:T(8,128)S(1)} %get-tuple-element.31), channel_id=1, source_target_pairs={{0,31},{1,2},{2,1},{3,4},{4,3},{5,6},{6,5},{7,8},{8,7},{9,10},{10,... | collective-permute-start | bytes 479240 | tf_op jit(solution)/shard_map/ppermute | solution.py:459
  4.3 15.4 %collective-permute-start.2 = (f32[260,128]{1,0:T(8,128)S(1)}, f32[260,128]{1,0:T(8,128)S(1)}, u32[]{:S(2)}, u32[]{:S(2)}) collective-permute-start(f32[260,128]{1,0:T(8,128)S(1)} %get-tuple-element.36), channel_id=1, source_target_pairs={{0,31},{1,30},{2,29},{3,28},{4,27},{5,26},{6,25},{7,24},{8,23},{9,... | collective-permute-start | bytes 399368 | tf_op jit(solution)/shard_map/ppermute | solution.py:459
  6.8 3.1 %copy-start = (f32[4,9,200,200]{3,2,1,0:T(8,128)S(1)}, f32[4,9,200,200]{3,2,1,0:T(8,128)}, u32[]{:S(2)}) copy-start(f32[4,9,200,200]{3,2,1,0:T(8,128)} %w.1) | copy-start | bytes 17280004
  9.9 4.4 %copy-start.2 = (f32[16,52,200]{2,0,1:T(8,128)S(1)}, f32[16,52,200]{2,0,1:T(8,128)}, u32[]{:S(2)}) copy-start(f32[16,52,200]{2,0,1:T(8,128)} %param.5) | copy-start | bytes 1996804
  9.9 4.4 %copy-start.4 = (f32[8,52,200]{2,0,1:T(8,128)S(1)}, f32[8,52,200]{2,0,1:T(8,128)}, u32[]{:S(2)}) copy-start(f32[8,52,200]{2,0,1:T(8,128)} %param.6) | copy-start | bytes 998404
  9.9 4.4 %copy-start.5 = (f32[4,200]{1,0:T(4,128)S(1)}, f32[4,200]{1,0:T(4,128)}, u32[]{:S(2)}) copy-start(f32[4,200]{1,0:T(4,128)} %bias.9) | copy-start | bytes 9604
  12.1 7.7 %collective-permute-start.3 = (f32[80,128]{1,0:T(8,128)S(1)}, f32[80,128]{1,0:T(8,128)S(1)}, u32[]{:S(2)}, u32[]{:S(2)}) collective-permute-start(f32[80,128]{1,0:T(8,128)S(1)} %corner.1), channel_id=1, source_target_pairs={{0,31},{1,30},{2,29},{3,28},{4,27},{5,26},{6,25},{7,24},{8,23},{9,... | collective-permute-start | bytes 122888 | tf_op jit(solution)/shard_map/ppermute | solution.py:459
  14.3 5.5 %copy-start.6 = (s32[200]{0:T(256)S(1)}, s32[200]{0:T(256)}, u32[]{:S(2)}) copy-start(s32[200]{0:T(256)} %param.7) | copy-start | bytes 2404
  23.8 14.3 %collective-permute-start.4 = (f32[420,128]{1,0:T(8,128)S(1)}, f32[420,128]{1,0:T(8,128)S(1)}, u32[]{:S(2)}, u32[]{:S(2)}) collective-permute-start(f32[420,128]{1,0:T(8,128)S(1)} %get-tuple-element.45), channel_id=1, source_target_pairs={{0,31},{1,30},{2,29},{3,28},{4,27},{5,26},{6,25},{7,24},{8,23},{9,... | collective-permute-start | bytes 645128 | tf_op jit(solution)/shard_map/ppermute | solution.py:459
  39.9 4.7 %collective-permute-start.5 = (f32[200,128]{1,0:T(8,128)S(1)}, f32[200,128]{1,0:T(8,128)S(1)}, u32[]{:S(2)}, u32[]{:S(2)}) collective-permute-start(f32[200,128]{1,0:T(8,128)S(1)} %get-tuple-element.47), channel_id=1, source_target_pairs={{0,1},{1,0},{2,3},{3,2},{4,5},{5,4},{6,7},{7,6},{8,9},{9,8},{10,11... | collective-permute-start | bytes 307208 | tf_op jit(solution)/shard_map/ppermute | solution.py:459
  40.5 5.8 %collective-permute-start.6 = (f32[200,128]{1,0:T(8,128)S(1)}, f32[200,128]{1,0:T(8,128)S(1)}, u32[]{:S(2)}, u32[]{:S(2)}) collective-permute-start(f32[200,128]{1,0:T(8,128)S(1)} %get-tuple-element.48), channel_id=1, source_target_pairs={{0,31},{1,2},{2,1},{3,4},{4,3},{5,6},{6,5},{7,8},{8,7},{9,10},{10,... | collective-permute-start | bytes 307208 | tf_op jit(solution)/shard_map/ppermute | solution.py:459
  41.1 20.2 %collective-permute-start.7 = (f32[364,128]{1,0:T(8,128)S(1)}, f32[364,128]{1,0:T(8,128)S(1)}, u32[]{:S(2)}, u32[]{:S(2)}) collective-permute-start(f32[364,128]{1,0:T(8,128)S(1)} %get-tuple-element.53), channel_id=1, source_target_pairs={{0,31},{1,30},{2,29},{3,28},{4,27},{5,26},{6,25},{7,24},{8,23},{9,... | collective-permute-start | bytes 559112 | tf_op jit(solution)/shard_map/ppermute | solution.py:459
  42.4 22.9 %collective-permute-start.8 = (f32[364,128]{1,0:T(8,128)S(1)}, f32[364,128]{1,0:T(8,128)S(1)}, u32[]{:S(2)}, u32[]{:S(2)}) collective-permute-start(f32[364,128]{1,0:T(8,128)S(1)} %get-tuple-element.54), channel_id=1, source_target_pairs={{0,31},{1,30},{2,29},{3,28},{4,27},{5,26},{6,25},{7,24},{8,23},{9,... | collective-permute-start | bytes 559112 | tf_op jit(solution)/shard_map/ppermute | solution.py:459
  46.4 21.0 %collective-permute-start.9 = (f32[208,128]{1,0:T(8,128)S(1)}, f32[208,128]{1,0:T(8,128)S(1)}, u32[]{:S(2)}, u32[]{:S(2)}) collective-permute-start(f32[208,128]{1,0:T(8,128)S(1)} %corner2.1), channel_id=1, source_target_pairs={{0,31},{1,30},{2,29},{3,28},{4,27},{5,26},{6,25},{7,24},{8,23},{9,... | collective-permute-start | bytes 319496 | tf_op jit(solution)/shard_map/ppermute | solution.py:459

commit v3 on v2

v3 whole, which is shorter than its diff:
```python
import functools

import jax
import jax.numpy as jnp
from jax import lax
from jax.experimental import pallas as pl
from jax.experimental.pallas import tpu as pltpu
from jax.sharding import PartitionSpec as P

F32 = jnp.float32
BF16 = jnp.bfloat16
LANES = 128
HALF = 64
MW = 64
HALO = 8


def merged(rows):
    return rows % 2 == 1 and rows <= 8


def rest_groups(rows, width, rem):
    groups = max(1, LANES // (rows * rem))
    return groups, width if groups == 1 else (-(-width // groups) + 7) // 8 * 8


def packed_rows(rows, width, rem):
    full = rows + (rows + 1) // 2
    return full * width + (0 if merged(rows) else rest_groups(rows, width, rem)[1])


def lane_of(width):
    return lax.broadcasted_iota(jnp.int32, (width, LANES), 1)


def roll(x, shift):
    shift = shift % LANES
    return x if shift == 0 else pltpu.roll(x, shift, 1)


def pack(get, put, rows, width, rem):
    lane = lane_of(width)
    halves = (rows + 1) // 2
    for k in range(rows):
        put(k, get(k, 0))
    second = [get(k, 1) for k in range(rows)]
    for p in range(halves):
        other = roll(second[2 * p + 1], HALF) if 2 * p + 1 < rows else jnp.zeros((width, LANES), F32)
        tile = jnp.where(lane < HALF, second[2 * p], other)
        if merged(rows) and p == halves - 1:
            for k in range(rows):
                at = HALF + rem * k
                tile = jnp.where((lane >= at) & (lane < at + rem), roll(second[k], rem * k), tile)
        put(rows + p, tile)
    if not merged(rows):
        tile = jnp.zeros((width, LANES), F32)
        for k in range(rows):
            tile = jnp.where((lane >= rem * k) & (lane < rem * k + rem), roll(second[k], rem * k - HALF), tile)
        groups, high = rest_groups(rows, width, rem)
        total = None
        for g in range(groups):
            part = tile[g * high : min(width, (g + 1) * high)]
            if part.shape[0] < high:
                part = jnp.concatenate([part, jnp.zeros((high - part.shape[0], LANES), F32)], axis=0)
            part = roll(part, g * rows * rem)
            total = part if total is None else total + part
        put(rows + halves, total)


def unpack(slot, k, rows, width, rem):
    lane = lane_of(width)
    halves = (rows + 1) // 2
    half = roll(slot(rows + k // 2), HALF * (k % 2))
    if merged(rows):
        rest = roll(slot(rows + halves - 1), -rem * k)
    else:
        rest = roll(slot(rows + halves), HALF - rem * k)
    tile = jnp.where(lane < HALF, half, jnp.where(lane < HALF + rem, rest, 0.0))
    return slot(k), tile


def slots_of(ref, rows, width, rem):
    full = rows + (rows + 1) // 2
    tiles = [ref[k * width : (k + 1) * width, :] for k in range(full)]
    if not merged(rows):
        groups, high = rest_groups(rows, width, rem)
        block = ref[full * width : full * width + high, :]
        parts = [roll(block, -g * rows * rem)[: min(high, width - g * high)] for g in range(groups)]
        tiles.append(parts[0] if groups == 1 else jnp.concatenate(parts, axis=0))
    return tiles


def putter(ref, width):
    def put(k, tile):
        ref[k * width : (k + 1) * width, :] = tile

    return put


def turned(tiles):
    order = 7 - lax.broadcasted_iota(jnp.int32, (8, LANES), 0)
    flip = lambda x: jnp.take_along_axis(x, order, axis=0)

    def one(x):
        parts, left = [], x.shape[0]
        while left >= 8:
            parts.append(flip(x[left - 8 : left]))
            left -= 8
        if left:
            parts.append(flip(x[0:8])[8 - left :])
        return jnp.concatenate(parts, axis=0)

    return [one(x) for x in tiles]


def fill_row(hi, lo, dst, ref, row, offs):
    for b in range(3):
        for t in range(2):
            x = ref[row, t, offs[b] : offs[b] + MW, :]
            h = x.astype(BF16)
            at = b * 2 * LANES + t * LANES
            hi[dst, :, at : at + LANES] = h
            lo[dst, :, at : at + LANES] = (x - h.astype(F32)).astype(BF16)


def fill(hi, lo, dst, ref, src, count, offs):
    for i in range(count):
        fill_row(hi, lo, dst + i, ref, src + i, offs)


def run(ref, first, count, offs):
    return [(ref, first + i, offs) for i in range(count)]


def products(hi, lo, wh, wl, taps, row, chunk, dilate):
    total = None
    for a in taps:
        at = slice(row + a * dilate, row + a * dilate + chunk)
        lh = hi[at].reshape(chunk * MW, hi.shape[-1])
        ll = lo[at].reshape(chunk * MW, hi.shape[-1])
        for left, right in ((lh, wh), (ll, wh), (lh, wl)):
            term = jnp.dot(left, right[a], preferred_element_type=F32)
            total = term if total is None else total + term
    return total


def conv(buffers, wh, wl, bias, dilate, sources, count, chunk, emit):
    hi, lo = buffers
    filled = 0
    for row in range(0, count, chunk):
        while filled < row + chunk + 2 * dilate:
            fill_row(hi, lo, filled, *sources[filled])
            filled += 1
        total = products(hi, lo, wh, wl, (0, 1, 2), row, chunk, dilate)
        emit(row, jax.nn.gelu(total + bias))


def add_rows(out, out_row, res, res_row, off, chunk):
    def emit(row, grown):
        for q in range(chunk):
            for t in range(2):
                out[out_row + row + q, t, 0:MW, :] = (
                    res[res_row + row + q, t, off : off + MW, :]
                    + grown[q * MW : (q + 1) * MW, t * LANES : (t + 1) * LANES]
                )

    return emit


def put_row(dst, row, at, tiles):
    for t in range(2):
        dst[row, t, at : at + tiles[t].shape[0], :] = tiles[t]


def widen(x):
    return jnp.concatenate([x, jnp.zeros(x.shape[:-1] + (LANES - x.shape[-1],), F32)], axis=-1)


def tile_at(ref, col, lo, hi, t):
    return ref[col, lo:hi, 0:LANES] if t == 0 else widen(ref[col, lo:hi, LANES : ref.shape[-1]])


def strided(dst, first, t, col):
    rows, _, width, _ = dst.shape
    return dst.reshape(rows * 2 * width, LANES), pl.ds((2 * first + t) * width + col, 8, stride=2 * width)


def put_column(dst, first, col, t, tile):
    flat, at = strided(dst, first, t, col)
    flat[at, :] = tile


def get_column(src, first, col, t):
    flat, at = strided(src, first, t, col)
    return flat[at, :]


def lanes_of(ref, row):
    x = ref[row : row + 1, :].astype(F32)
    return [x[:, 0:LANES], widen(x[:, LANES:])]


def bias_of(ref, row):
    return jnp.concatenate(lanes_of(ref, row), axis=1)


def k_first(par, field, south, main, ewi, ewc, top):
    cols, rows, channels = field.shape
    rem = channels - LANES - HALF
    even = par[0] == 0

    def edge(flip):
        def get(k, t):
            pick = []
            for col in (k, cols - HALO + k):
                tiles = [tile_at(field, col, 0, rows, t), tile_at(south, col, 0, south.shape[1], t)]
                pick.append(jnp.concatenate(tiles, axis=0))
            return jnp.where(even != flip, pick[1], pick[0])

        return get

    tall = rows + south.shape[1]
    pack(edge(False), putter(ewi, tall), HALO, tall, rem)
    pack(edge(True), putter(ewc, tall), HALO, tall, rem)
    for col in range(cols):
        for t in range(2):
            put_column(top, 0, col, t, tile_at(field, col, rows - 8, rows, t))
    pack(lambda k, t: top[7 - k, t, 0:cols, :], putter(main, cols), 3, cols, rem)


def k_weights(w, *refs):
    layers, _, channels, _ = w.shape
    outs, (buf, sems) = refs[: 2 * layers], refs[2 * layers :]
    copies = [pltpu.make_async_copy(w.at[i], buf.at[i], sems.at[i]) for i in range(layers)]
    for copy in copies:
        copy.start()
    for i in range(layers):
        wh, wl = outs[2 * i : 2 * i + 2]
        copies[i].wait()
        for k in range(9):
            x = buf[i, k]
            h = x.astype(BF16)
            at = (k % 3) * 2 * LANES
            for ref, value in ((wh, h), (wl, (x - h.astype(F32)).astype(BF16))):
                wide = jnp.concatenate([value, jnp.zeros((channels, 2 * LANES - channels), BF16)], axis=1)
                ref[k // 3, at : at + channels, :] = wide
                ref[k // 3, at + channels : at + 2 * LANES, :] = jnp.zeros((2 * LANES - channels, 2 * LANES), BF16)


def sided(par, ewi, ewc, rows, width, rem):
    even = par[0] == 0
    i, c = slots_of(ewi, rows, width, rem), slots_of(ewc, rows, width, rem)
    west = [jnp.where(even, y, x) for x, y in zip(i, c)]
    east = [jnp.where(even, x, y) for x, y in zip(i, c)]
    return west.__getitem__, east.__getitem__


def k_corner(par, ewi, ewc, out, top, *, tall, rows, rem):
    west, east = sided(par, ewi, ewc, HALO, tall, rem)
    for side, slot in enumerate((west, east)):
        for k in range(HALO):
            tiles = unpack(slot, k, HALO, tall, rem)
            for t in range(2):
                put_column(top, 0, side * HALO + k, t, tiles[t][rows - 8 : rows])
    pack(lambda k, t: top[7 - k, t], putter(out, 2 * HALO), 3, 2 * HALO, rem)


def k_corner2(par, ewi, ewc, out, *, rows, rem):
    west, east = sided(par, ewi, ewc, rows, HALO, rem)
    tiles = []
    for k in range(8):
        w = unpack(west, rows - 1 - k, rows, HALO, rem)
        e = unpack(east, rows - 1 - k, rows, HALO, rem)
        tiles.append([jnp.concatenate([w[t], e[t]], axis=0) for t in range(2)])
    pack(lambda k, t: tiles[k][t], putter(out, 2 * HALO), 8, 2 * HALO, rem)


def k_a(par, field, south, ewi, ewc, wh, wl, bias, st1, se, x0, *buffers):
    cols, rows, channels = field.shape
    rem = channels - LANES - HALF
    deep = south.shape[1]
    west, east = sided(par, ewi, ewc, HALO, rows + deep, rem)

    def put(col, tiles):
        for t in range(2):
            for h in range(0, rows, 8):
                put_column(x0, h, col, t, tiles[t][h : h + 8])
            put_column(se, 0, col, t, tiles[t][rows : rows + 8])

    for k in range(HALO):
        put(k, unpack(west, k, HALO, rows + deep, rem))
        put(HALO + cols + k, unpack(east, k, HALO, rows + deep, rem))
    for col in range(cols):
        for t in range(2):
            for h in range(0, rows, 8):
                put_column(x0, h, HALO + col, t, tile_at(field, col, h, h + 8, t))
            put_column(se, 0, HALO + col, t, tile_at(south, col, 0, 8, t))
    sources = run(se, deep - 1, 1, (1, 2, 3)) + run(x0, 0, rows, (1, 2, 3))
    conv(buffers, wh, wl, bias_of(bias, 0), 1, sources, rows - 1, 5, add_rows(st1, 0, x0, 0, 2, 5))


def signed(tiles, sign):
    return tiles if sign is None else [tiles[t] * sign[t] for t in range(2)]


def north_rows(dst, dst_row, main, sign, count, width, left, rem):
    slot = turned(slots_of(main, count, width, rem)).__getitem__
    for k in range(count):
        put_row(dst, dst_row + k, left, signed(unpack(slot, k, count, width, rem), sign))


def north_corners(dst, dst_row, corner, sign, count, cols, left, rem):
    width = 2 * HALO
    slot = turned(slots_of(corner, count, width, rem)).__getitem__
    for k in range(count):
        t = signed(unpack(slot, k, count, width, rem), sign)
        put_row(dst, dst_row + k, left - HALO, [x[0:HALO] for x in t])
        put_row(dst, dst_row + k, left + cols, [x[HALO:] for x in t])


def k_b(edge, main, corner, st1, sign, wh0, wl0, wh1, wl1, bias, st2, out, x0, xr, x1, hi, lo, *buffers, cols, rem):
    rows = edge.shape[0]
    sign = lanes_of(sign, 0)
    north_rows(xr, 1, main, None, 3, cols, HALO, rem)
    north_corners(xr, 1, corner, None, 3, cols, HALO, rem)
    x0[0:2] = edge[rows - 2 :]
    for t in range(2):
        x0[2, t] = xr[1, t] * sign[t]
        xr[0, t] = edge[rows - 1, t] * sign[t]
    x1[0:5] = st1[rows - 6 : rows - 1]
    offs = (1, 2, 3)
    fill(hi, lo, 0, x0, 0, 3, offs)
    fill(hi, lo, 3, xr, 0, 4, offs[::-1])
    total = None
    for a in range(3):
        both = [jnp.concatenate([x[a : a + 1], x[5 - a : 7 - a]]).reshape(3 * MW, x.shape[-1]) for x in (hi, lo)]
        for left, right in ((both[0], wh0), (both[1], wh0), (both[0], wl0)):
            term = jnp.dot(left, right[a], preferred_element_type=F32)
            total = term if total is None else total + term
    grown = jax.nn.gelu(total + bias_of(bias, 0))
    for q in range(3):
        for t in range(2):
            g = grown[q * MW : (q + 1) * MW, t * LANES : (t + 1) * LANES]
            if q == 0:
                x1[5, t, 0:MW, :] = x0[1, t, 2 : 2 + MW, :] + g
            else:
                x1[5 + q, t, 0:MW, :] = sign[t] * (xr[q, t, 2 : 2 + MW, :] + g)
    conv(buffers, wh1, wl1, bias_of(bias, 1), 2, run(x1, 0, 8, (0, 2, 4)), 4, 4, add_rows(st2, 0, x1, 2, 2, 4))
    wide = cols + 8
    pack(lambda k, t: st2[3 - k, t, 0:wide, :], putter(out, wide), 4, wide, rem)


def k_c1(st1, st2b, wh1, wl1, wh2, wl2, bias, st2, st3, out, h1, l1, h2, l2, *, cols, rem):
    conv((h1, l1), wh1, wl1, bias_of(bias, 1), 2, run(st1, 2, 12, (0, 2, 4)), 8, 4, add_rows(st2, 0, st1, 4, 2, 4))
    st2[8:12] = st2b[...]
    conv((h2, l2), wh2, wl2, bias_of(bias, 2), 4, run(st2, 0, 12, (0, 4, 8)), 4, 4, add_rows(st3, 0, st2, 4, 4, 4))
    pack(lambda k, t: st3[3 - k, t, 0:cols, :], putter(out, cols), 4, cols, rem)


def k_c2(st1, st2m, se, wh1, wl1, wh2, wl2, bias, st3, x2, h1, l1, h2, l2):
    south = se.shape[0]
    sources = run(se, south - 2, 2, (2, 4, 6)) + run(st1, 0, 6, (0, 2, 4))
    conv((h1, l1), wh1, wl1, bias_of(bias, 1), 2, sources, 4, 4, add_rows(x2, 0, st1, 0, 2, 4))
    x2[4:8] = st2m[0:4]
    sources = run(se, south - 4, 4, (4, 8, 12)) + run(x2, 0, 4, (0, 4, 8)) + run(st2m, 0, 8, (0, 4, 8))
    conv((h2, l2), wh2, wl2, bias_of(bias, 2), 4, sources, 8, 4, add_rows(st3, 0, x2, 0, 4, 4))


def row_of(parts, row):
    for part in parts:
        if row < part.shape[0]:
            return part, row
        row -= part.shape[0]


def k_d(par, st2, north, st3l, st3m, sign, wh, wl, bias, st3b, out, ewi, ewc, x2, hi, lo, *, cols, rem):
    wide = cols + 8
    north_rows(x2, 0, north, lanes_of(sign, 0), 4, wide, 0, rem)
    sources = run(st2, 4, 8, (0, 4, 8)) + run(x2, 0, 4, (0, 4, 8))
    conv((hi, lo), wh, wl, bias_of(bias, 2), 4, sources, 4, 4, add_rows(st3b, 0, st2, 8, 4, 4))
    pack(lambda k, t: st3b[3 - k, t, 0:cols, :], putter(out, cols), 4, cols, rem)
    even = par[0] == 0
    parts = (st3l, st3m, st3b)
    rows = sum(x.shape[0] for x in parts)

    def edge(flip):
        def get(k, t):
            ref, row = row_of(parts, k)
            west, east = ref[row, t, 0:HALO, :], ref[row, t, cols - HALO : cols, :]
            return jnp.where(even != flip, east, west)

        return get

    pack(edge(False), putter(ewi, HALO), rows, HALO, rem)
    pack(edge(True), putter(ewc, HALO), rows, HALO, rem)


def put_out(out, first, src, cols, channels):
    for col in range(cols):
        out[col, first : first + 8, 0:LANES] = get_column(src, 0, col, 0)
        out[col, first : first + 8, LANES:channels] = get_column(src, 0, col, 1)[:, 0 : channels - LANES]


def k_f(st3l, st3m, st3b, se, wh, wl, bias, acc, x3, hi, lo, *, cols):
    rows = acc.shape[0]
    south = se.shape[0]
    zero = jnp.zeros((2, HALO, LANES), F32)
    for k in range(rows + south):
        ref, row = (se, k) if k < south else row_of((st3l, st3m, st3b), k - south)
        x3[k, :, 0:HALO, :] = zero
        at = HALO if k < south else 0
        x3[k, :, HALO : HALO + cols, :] = ref[row, :, at : at + cols, :]
        x3[k, :, HALO + cols : 2 * HALO + cols, :] = zero
    bias = bias_of(bias, 3)
    filled = 0
    for row in range(0, rows, 4):
        taps = (0, 1, 2) if row < rows - 8 else (0, 1)
        while filled < row + 4 + 8 * taps[-1]:
            fill_row(hi, lo, filled, x3, filled, (0, 8, 16))
            filled += 1
        total = products(hi, lo, wh, wl, taps, row, 4, 8)
        acc[row : row + 4] = (total + bias).reshape(4, MW, 2 * LANES)


def split_bf16(x):
    h = x.astype(BF16)
    return h, (x - h.astype(F32)).astype(BF16)


def edge_sums(tiles_of, wh, wl, taps):
    total = None
    for a in taps:
        h, l = split_bf16(tiles_of(a))
        for left, right in ((h, wh), (l, wh), (h, wl)):
            term = jnp.dot(left, right(a), preferred_element_type=F32)
            total = term if total is None else total + term
    return total


def side_weights(ref, b):
    at = b * 2 * LANES
    return lambda a: ref[a, at : at + 2 * LANES, :]


def k_g(par, acc, st3l, st3m, st3b, se, ewi, ewc, na, nb, sign, wh, wl, out, accn, xn, halo, end, hi, lo, *, cols, rem):
    rows = acc.shape[0]
    channels = out.shape[-1]
    south = se.shape[0]
    sign = lanes_of(sign, 0)
    zero = jnp.zeros((8, 2, HALO, LANES), F32)
    xn[:, :, 0:HALO, :] = zero
    xn[:, :, HALO + cols : 2 * HALO + cols, :] = zero
    north_rows(xn, 0, nb, sign, 4, cols, HALO, rem)
    north_rows(xn, 4, na, sign, 4, cols, HALO, rem)
    fill(hi, lo, 0, xn, 0, 8, (0, 8, 16))
    accn[0 : rows - 8] = acc[0 : rows - 8]
    for i in range(2):
        at = slice(4 * i, 4 * i + 4)
        lh = hi[at].reshape(4 * MW, hi.shape[-1])
        ll = lo[at].reshape(4 * MW, hi.shape[-1])
        total = acc[rows - 8 + 4 * i : rows - 4 + 4 * i].reshape(4 * MW, 2 * LANES)
        for left, right in ((lh, wh), (ll, wh), (lh, wl)):
            total = total + jnp.dot(left, right[2], preferred_element_type=F32)
        accn[rows - 8 + 4 * i : rows - 4 + 4 * i] = total.reshape(4, MW, 2 * LANES)
    for side, slot in enumerate(sided(par, ewi, ewc, rows, HALO, rem)):
        b, to = ((0, 0), (2, cols - HALO))[side]
        at = side * (HALO + cols)
        for k in range(south):
            for t in range(2):
                halo[side, k * HALO : (k + 1) * HALO, t * LANES : (t + 1) * LANES] = se[k, t, at : at + HALO, :]
        for k in range(rows):
            tiles = unpack(slot, k, rows, HALO, rem)
            for t in range(2):
                halo[side, (south + k) * HALO : (south + k + 1) * HALO, t * LANES : (t + 1) * LANES] = tiles[t]
        halo[side, (south + rows) * HALO :, :] = jnp.zeros((8 * HALO, 2 * LANES), F32)
        total = edge_sums(
            lambda a: halo[side, 8 * a * HALO : (8 * a + rows) * HALO, :],
            side_weights(wh, b), side_weights(wl, b), (0, 1, 2),
        )
        for k in range(rows):
            accn[k, to : to + HALO, :] += total[k * HALO : (k + 1) * HALO]
    for half in range(0, rows, 8):
        for k in range(8):
            grown = jax.nn.gelu(accn[half + k])
            ref, row = row_of((st3l, st3m, st3b), half + k)
            for t in range(2):
                end[half // 8, k, t] = ref[row, t] + grown[:, t * LANES : (t + 1) * LANES]
        put_out(out, half, end.at[half // 8], cols, channels)


def k_h(before, accn, st3m, st3b, nc, sign, wh, wl, out, xc, end, done, sems, *, cols, rem):
    rows = accn.shape[0]
    channels = out.shape[-1]
    slot = turned(slots_of(nc, 8, 2 * HALO, rem)).__getitem__
    for k in range(8):
        tiles = signed(unpack(slot, k, 8, 2 * HALO, rem), lanes_of(sign, 0))
        for t in range(2):
            for side in range(2):
                xc[side, k * HALO : (k + 1) * HALO, t * LANES : (t + 1) * LANES] = tiles[t][side * HALO : (side + 1) * HALO]
    copies = []
    for side in range(2):
        b, at = ((0, 0), (2, cols - HALO))[side]
        total = edge_sums(lambda a: xc[side], side_weights(wh, b), side_weights(wl, b), (2,))
        for k in range(8):
            ref, row = row_of((st3m, st3b), k)
            grown = jax.nn.gelu(accn[rows - 8 + k, at : at + HALO, :] + total[k * HALO : (k + 1) * HALO])
            for t in range(2):
                end[k, t] = ref[row, t, at : at + HALO, :] + grown[:, t * LANES : (t + 1) * LANES]
        put_out(done.at[side], 0, end, HALO, channels)
        copies.append(
            pltpu.make_async_copy(done.at[side], out.at[pl.ds(at, HALO), pl.ds(rows - 8, 8), :], sems.at[side])
        )
        copies[-1].start()
    for copy in copies:
        copy.wait()


VM = pl.BlockSpec(memory_space=pltpu.VMEM)
SM = pl.BlockSpec(memory_space=pltpu.SMEM)
HB = pl.BlockSpec(memory_space=pl.ANY)


def lhs(rows):
    return [pltpu.VMEM((rows, MW, 6 * LANES), BF16)] * 2


def call(kernel, outs, scratch, args, smem=0, flops=0, limit=16, hbm=(), alias=None):
    moved = sum(a.size * a.dtype.itemsize for a in args[smem:])
    outs = [o if isinstance(o, jax.ShapeDtypeStruct) else jax.ShapeDtypeStruct(o, F32) for o in outs]
    return pl.pallas_call(
        kernel,
        out_shape=outs,
        in_specs=[SM if i < smem else HB if i in hbm else VM for i in range(len(args))],
        out_specs=[HB if alias else VM] * len(outs),
        input_output_aliases=alias or {},
        scratch_shapes=scratch,
        compiler_params=pltpu.CompilerParams(vmem_limit_bytes=limit * 2**20),
        cost_estimate=pl.CostEstimate(flops=flops, bytes_accessed=moved, transcendentals=0),
    )(*args)


def layers_of(field, south_rows, sign_mask, weights, biases):
    rows, cols, channels = field.shape
    south = south_rows.shape[0]
    layers = weights.shape[0]
    rem = channels - LANES - HALF
    devices = lax.axis_size("lon")
    mirror = [(i, devices - 1 - i) for i in range(devices)]
    intra = [(i, i ^ 1) for i in range(devices)]
    cross = [(i, (i + 1) % devices if i % 2 else (i - 1) % devices) for i in range(devices)]
    send = lambda x, route: lax.ppermute(x, "lon", route)
    par = (lax.axis_index("lon") % 2).astype(jnp.int32).reshape(1)
    sign = sign_mask.reshape(1, channels)
    field = jnp.swapaxes(field, 0, 1)
    south_rows = jnp.swapaxes(south_rows, 0, 1)
    row_flops = MW * 6 * LANES * 2 * LANES * 2 * 9
    tall = rows + south

    def state(n, width):
        return (n, 2, width, LANES)

    ew_rows = packed_rows(HALO, tall, rem)
    main, ewi, ewc = call(
        k_first,
        [(packed_rows(3, cols, rem), LANES), (ew_rows, LANES), (ew_rows, LANES)],
        [pltpu.VMEM(state(8, 56), F32)], [par, field, south_rows], smem=1,
    )
    ewi, ewc, main = send(ewi, intra), send(ewc, cross), send(main, mirror)
    split = call(
        k_weights,
        [jax.ShapeDtypeStruct((3, 6 * LANES, 2 * LANES), BF16)] * (2 * layers),
        [pltpu.VMEM(weights.shape, F32), pltpu.SemaphoreType.DMA((layers,))],
        [weights], limit=24, hbm=(0,),
    )
    (corner,) = call(
        functools.partial(k_corner, tall=tall, rows=rows, rem=rem),
        [(packed_rows(3, 2 * HALO, rem), LANES)], [pltpu.VMEM(state(8, 2 * HALO), F32)],
        [par, ewi, ewc], smem=1,
    )
    corner = send(corner, mirror)
    st1, se, x0 = call(
        k_a,
        [state(rows - 1, 72), state(south, 80), state(rows, 72)],
        lhs(rows + 1),
        [par, field, south_rows, ewi, ewc, *split[0:2], biases],
        smem=1, flops=15 * row_flops,
    )
    st2b, north = call(
        functools.partial(k_b, cols=cols, rem=rem),
        [state(4, 72), (packed_rows(4, cols + 8, rem), LANES)],
        [pltpu.VMEM(state(3, 72), F32), pltpu.VMEM(state(4, 72), F32), pltpu.VMEM(state(8, 72), F32)] + lhs(7) + lhs(8),
        [x0, main, corner, st1, sign, *split[0:4], biases],
        flops=7 * row_flops,
    )
    north = send(north, mirror)
    st2m, st3m, na = call(
        functools.partial(k_c1, cols=cols, rem=rem),
        [state(12, 72), state(4, MW), (packed_rows(4, cols, rem), LANES)],
        lhs(12) + lhs(12),
        [st1, st2b, *split[2:6], biases],
        flops=12 * row_flops,
    )
    na = send(na, mirror)
    (st3l,) = call(
        k_c2,
        [state(8, MW)],
        [pltpu.VMEM(state(8, 72), F32)] + lhs(8) + lhs(16),
        [st1, st2m, se, *split[2:6], biases],
        flops=12 * row_flops,
    )
    ew_rows = packed_rows(rows, HALO, rem)
    st3b, nb, ewi, ewc = call(
        functools.partial(k_d, cols=cols, rem=rem),
        [state(4, MW), (packed_rows(4, cols, rem), LANES), (ew_rows, LANES), (ew_rows, LANES)],
        [pltpu.VMEM(state(4, 72), F32)] + lhs(12),
        [par, st2m, north, st3l, st3m, sign, *split[4:6], biases],
        smem=1, flops=4 * row_flops,
    )
    ewi, ewc = send(ewi, intra), send(ewc, cross)
    nb = send(nb, mirror)
    (nc,) = call(
        functools.partial(k_corner2, rows=rows, rem=rem),
        [(packed_rows(8, 2 * HALO, rem), LANES)], [], [par, ewi, ewc], smem=1,
    )
    nc = send(nc, mirror)
    (acc,) = call(
        functools.partial(k_f, cols=cols),
        [(rows, MW, 2 * LANES)],
        [pltpu.VMEM(state(rows + south, 80), F32)] + lhs(rows + south),
        [st3l, st3m, st3b, se, *split[6:8], biases],
        flops=(rows - 3) * row_flops,
    )
    out, acc = call(
        functools.partial(k_g, cols=cols, rem=rem),
        [(cols, rows, channels), (rows, MW, 2 * LANES)],
        [pltpu.VMEM(state(8, 80), F32), pltpu.VMEM((2, (rows + south + 8) * HALO, 2 * LANES), F32),
         pltpu.VMEM((2,) + state(8, MW), F32)] + lhs(8),
        [par, acc, st3l, st3m, st3b, se, ewi, ewc, na, nb, sign, *split[6:8]],
        smem=1, flops=4 * row_flops,
    )
    (out,) = call(
        functools.partial(k_h, cols=cols, rem=rem),
        [(cols, rows, channels)],
        [pltpu.VMEM((2, 8 * HALO, 2 * LANES), F32), pltpu.VMEM(state(8, HALO), F32),
         pltpu.VMEM((2, HALO, 8, channels), F32), pltpu.SemaphoreType.DMA((2,))],
        [out, acc, st3m, st3b, nc, sign, *split[6:8]],
        hbm=(0,), alias={0: 0}, flops=row_flops,
    )
    return jnp.swapaxes(out, 0, 1)


def solution(mesh):
    in_specs = (P(None, "lon", None), P(None, "lon", None), P(), P(), P())
    out_specs = P(None, "lon", None)
    return jax.shard_map(layers_of, mesh=mesh, in_specs=in_specs, out_specs=out_specs, check_vma=False)
```

time: 70.2 us -> 66.1 us (0.942)
  the two profiles are of different devices: /device:TPU:9 before, /device:TPU:8 now
where the time goes in v3:
time: 66.1 us; the launch traced here: 65.9 us
  Pallas kernels  27.7 us (42%)
  waiting for transfers between devices  17.1 us (26%)
  starting transfers between devices  15.5 us (23%)
  local copies, waits for them, and re-layouts  5.27 us (8%)
    pallas_call x12, Pallas kernels, call(): pl.pallas_call(kernel, out_shape=outs, in_specs=[SM if i < smem else HB i...  27.7 us
    ppermute x10, waiting for transfers between devices, layers_of(): send = lambda x, route: lax.ppermute(x, 'lon', route)  17.1 us
    ppermute x10, starting transfers between devices, layers_of(): send = lambda x, route: lax.ppermute(x, 'lon', route)  15.5 us
    unnamed x14, local copies, waits for them, and re-layouts  5.27 us
  transfers between devices with their start and end apart: 10, of which 4 were waited for; matrix products, arithmetic and copies ran while one was open for 0% of the time, Pallas kernels for 33%

profile of v3, /device:TPU:8, one launch (start us, length us, event | category | flops | bytes accessed | tf_op | source)
XLA Modules:
  0.0 65.9 jit_solution(14406918851123661523)
XLA Ops:
  0.0 1.2 %copy-done.1 = f32[16,52,200]{2,0,1:T(8,128)S(1)} copy-done((f32[16,52,200]{2,0,1:T(8,128)S(1)}, f32[16,52,200]{2,0,1:T(8,128)}, u32[]{:S(2)}) %copy-start.1) | copy-done | bytes 665624
  1.2 1.0 %copy-done.3 = f32[8,52,200]{2,0,1:T(8,128)S(1)} copy-done((f32[8,52,200]{2,0,1:T(8,128)S(1)}, f32[8,52,200]{2,0,1:T(8,128)}, u32[]{:S(2)}) %copy-start.3) | copy-done | bytes 332824
  2.2 0.2 shard_map.55
  2.5 2.4 %collective-permute-start.1 = (f32[304,128]{1,0:T(8,128)S(1)}, f32[304,128]{1,0:T(8,128)S(1)}, u32[]{:S(2)}, u32[]{:S(2)}) collective-permute-start(f32[304,128]{1,0:T(8,128)S(1)} %get-tuple-element.31), channel_id=1, source_target_pairs={{0,31},{1,2},{2,1},{3,4},{4,3},{5,6},{6,5},{7,8},{8,7},{9,10},{10,... | collective-permute-start | bytes 466952 | tf_op jit(solution)/shard_map/ppermute | solution.py:551
  4.9 2.3 %collective-permute-start.2 = (f32[260,128]{1,0:T(8,128)S(1)}, f32[260,128]{1,0:T(8,128)S(1)}, u32[]{:S(2)}, u32[]{:S(2)}) collective-permute-start(f32[260,128]{1,0:T(8,128)S(1)} %get-tuple-element.36), channel_id=1, source_target_pairs={{0,31},{1,30},{2,29},{3,28},{4,27},{5,26},{6,25},{7,24},{8,23},{9,... | collective-permute-start | bytes 399368 | tf_op jit(solution)/shard_map/ppermute | solution.py:551
  7.2 3.1 %copy-done = f32[4,9,200,200]{3,2,1,0:T(8,128)S(1)} copy-done((f32[4,9,200,200]{3,2,1,0:T(8,128)S(1)}, f32[4,9,200,200]{3,2,1,0:T(8,128)}, u32[]{:S(2)}) %copy-start) | copy-done | bytes 5760024
  10.3 1.9 %shard_map.56 = (bf16[3,768,256]{2,1,0:T(8,128)(2,1)S(1)}, bf16[3,768,256]{2,1,0:T(8,128)(2,1)S(1)}, bf16[3,768,256]{2,1,0:T(8,128)(2,1)S(1)}, bf16[3,768,256]{2...) custom-call(f32[4,9,200,200]{3,2,1,0:T(8,128)S(1)} %copy-done), custom_call_target="tpu_custom_call" | custom-call | bytes 5760000 | tf_op jit(solution)/shard_map/pallas_call | solution.py:530
  12.4 1.9 %collective-permute-start.3 = (f32[80,128]{1,0:T(8,128)S(1)}, f32[80,128]{1,0:T(8,128)S(1)}, u32[]{:S(2)}, u32[]{:S(2)}) collective-permute-start(f32[80,128]{1,0:T(8,128)S(1)} %shard_map.58), channel_id=1, source_target_pairs={{0,31},{1,30},{2,29},{3,28},{4,27},{5,26},{6,25},{7,24},{8,23},{9,... | collective-permute-start | bytes 122888 | tf_op jit(solution)/shard_map/ppermute | solution.py:551
  14.4 4.7 %shard_map.57 = (f32[15,2,72,128]{3,2,1,0:T(8,128)S(1)}, f32[8,2,80,128]{3,2,1,0:T(8,128)S(1)}, f32[16,2,72,128]{3,2,1,0:T(8,128)S(1)}) custom-call(s32[1]{0:T(128)} %bitcast.par, f32[52,16,200]{2,1,0:T(8,128)S(1)} %bitcast.6, f32[52,8,200]{2,1,0:T(8,128)S(1)} %bitcast.8, f32[304,128]{1,0:T(8,128)S(1)} %collective-permute-done.ewi, ...), custom_call_target="tpu_custom_call" | custom-call | flops 3397386240 | bytes 3672192 | tf_op jit(solution)/shard_map/pallas_call | solution.py:530
  19.1 3.2 %shard_map.59 = (f32[4,2,72,128]{3,2,1,0:T(8,128)S(1)}, f32[376,128]{1,0:T(8,128)S(1)}) custom-call(f32[16,2,72,128]{3,2,1,0:T(8,128)S(1)} %get-tuple-element.35.edge, f32[260,128]{1,0:T(8,128)S(1)} %collective-permute-done.2.main, f32[80,128]{1,0:T(8,128)S(1)} %collective-permute-done.3.corner, f32[15,2,72,128]{3,2,1,0:T(8,128)S(1)} %get-tuple-element.34.st1, ...), custom_call_target="tpu_custom_call" | custom-call | flops 1585446912 | bytes 7182240 | tf_op jit(solution)/shard_map/pallas_call | solution.py:530
  22.3 1.7 %collective-permute-start.4 = (f32[376,128]{1,0:T(8,128)S(1)}, f32[376,128]{1,0:T(8,128)S(1)}, u32[]{:S(2)}, u32[]{:S(2)}) collective-permute-start(f32[376,128]{1,0:T(8,128)S(1)} %get-tuple-element.45), channel_id=1, source_target_pairs={{0,31},{1,30},{2,29},{3,28},{4,27},{5,26},{6,25},{7,24},{8,23},{9,... | collective-permute-start | bytes 577544 | tf_op jit(solution)/shard_map/ppermute | solution.py:551
  24.0 4.7 %shard_map.60 = (f32[12,2,72,128]{3,2,1,0:T(8,128)S(1)}, f32[4,2,64,128]{3,2,1,0:T(8,128)S(1)}, f32[328,128]{1,0:T(8,128)S(1)}) custom-call(f32[15,2,72,128]{3,2,1,0:T(8,128)S(1)} %get-tuple-element.34.st1, f32[4,2,72,128]{3,2,1,0:T(8,128)S(1)} %get-tuple-element.39.st2b, bf16[3,768,256]{2,1,0:T(8,128)(2,1)S(1)} %get-tuple-element.37.wh1, ...), custom_call_target="tpu_custom_call" | custom-call | flops 2717908992 | bytes 6122624 | tf_op jit(solution)/shard_map/pallas_call | solution.py:530
  28.7 3.6 %shard_map.61.st3l = f32[8,2,64,128]{3,2,1,0:T(8,128)S(1)} custom-call(f32[15,2,72,128]{3,2,1,0:T(8,128)S(1)} %get-tuple-element.34.st1, f32[12,2,72,128]{3,2,1,0:T(8,128)S(1)} %get-tuple-element.42.st2m.st2, f32[8,2,80,128]{3,2,1,0:T(8,128)S(1)} %get-tuple-element.43.se, bf16[3,768,256]{2,1,0:T(8,128)(2,1)S(1)} %get-tuple-element.37.wh1, ...), custom_call_target="tpu_custom_call" | custom-call | flops 2717908992 | bytes 7367808 | tf_op jit(solution)/shard_map/pallas_call | solution.py:530
  32.3 2.9 %collective-permute-done.4.north = f32[376,128]{1,0:T(8,128)S(1)} collective-permute-done((f32[376,128]{1,0:T(8,128)S(1)}, f32[376,128]{1,0:T(8,128)S(1)}, u32[]{:S(2)}, u32[]{:S(2)}) %collective-permute-start.4) | collective-permute-done | bytes 192544 | tf_op jit(solution)/shard_map/ppermute | solution.py:551
  35.2 1.5 %shard_map.62 = (f32[4,2,64,128]{3,2,1,0:T(8,128)S(1)}, f32[328,128]{1,0:T(8,128)S(1)}, f32[200,128]{1,0:T(8,128)S(1)}, f32[200,128]{1,0:T(8,128)S(1)}) custom-call(s32[1]{0:T(128)} %bitcast.par, f32[12,2,72,128]{3,2,1,0:T(8,128)S(1)} %get-tuple-element.42.st2m.st2, f32[376,128]{1,0:T(8,128)S(1)} %collective-permute-done.4.north, ...), custom_call_target="tpu_custom_call" | custom-call | flops 905969664 | bytes 4226976 | tf_op jit(solution)/shard_map/pallas_call | solution.py:530
  36.8 2.2 %collective-permute-start.6 = (f32[200,128]{1,0:T(8,128)S(1)}, f32[200,128]{1,0:T(8,128)S(1)}, u32[]{:S(2)}, u32[]{:S(2)}) collective-permute-start(f32[200,128]{1,0:T(8,128)S(1)} %get-tuple-element.50), channel_id=1, source_target_pairs={{0,31},{1,2},{2,1},{3,4},{4,3},{5,6},{6,5},{7,8},{8,7},{9,10},{10,... | collective-permute-start | bytes 307208 | tf_op jit(solution)/shard_map/ppermute | solution.py:551
  39.0 1.4 %collective-permute-start.7 = (f32[328,128]{1,0:T(8,128)S(1)}, f32[328,128]{1,0:T(8,128)S(1)}, u32[]{:S(2)}, u32[]{:S(2)}) collective-permute-start(f32[328,128]{1,0:T(8,128)S(1)} %get-tuple-element.51), channel_id=1, source_target_pairs={{0,31},{1,30},{2,29},{3,28},{4,27},{5,26},{6,25},{7,24},{8,23},{9,... | collective-permute-start | bytes 503816 | tf_op jit(solution)/shard_map/ppermute | solution.py:551
  40.4 2.1 %collective-permute-start.8 = (f32[328,128]{1,0:T(8,128)S(1)}, f32[328,128]{1,0:T(8,128)S(1)}, u32[]{:S(2)}, u32[]{:S(2)}) collective-permute-start(f32[328,128]{1,0:T(8,128)S(1)} %get-tuple-element.52), channel_id=1, source_target_pairs={{0,31},{1,30},{2,29},{3,28},{4,27},{5,26},{6,25},{7,24},{8,23},{9,... | collective-permute-start | bytes 503816 | tf_op jit(solution)/shard_map/ppermute | solution.py:551
  43.0 1.3 %collective-permute-start.9 = (f32[200,128]{1,0:T(8,128)S(1)}, f32[200,128]{1,0:T(8,128)S(1)}, u32[]{:S(2)}, u32[]{:S(2)}) collective-permute-start(f32[200,128]{1,0:T(8,128)S(1)} %shard_map.65), channel_id=1, source_target_pairs={{0,31},{1,30},{2,29},{3,28},{4,27},{5,26},{6,25},{7,24},{8,23},{9,... | collective-permute-start | bytes 307208 | tf_op jit(solution)/shard_map/ppermute | solution.py:551
  44.2 3.3 %shard_map.63.acc = f32[16,64,256]{2,1,0:T(8,128)S(1)} custom-call(f32[8,2,64,128]{3,2,1,0:T(8,128)S(1)} %shard_map.61.st3l, f32[4,2,64,128]{3,2,1,0:T(8,128)S(1)} %get-tuple-element.44.st3m, f32[4,2,64,128]{3,2,1,0:T(8,128)S(1)} %get-tuple-element.46.st3b, f32[8,2,80,128]{3,2,1,0:T(8,128)S(1)} %get-tuple-element.43.se, ...), custom_call_target="tpu_custom_call" | custom-call | flops 2944401408 | bytes 4066432 | tf_op jit(solution)/shard_map/pallas_call | solution.py:530
  47.5 10.4 %collective-permute-done.7.na = f32[328,128]{1,0:T(8,128)S(1)} collective-permute-done((f32[328,128]{1,0:T(8,128)S(1)}, f32[328,128]{1,0:T(8,128)S(1)}, u32[]{:S(2)}, u32[]{:S(2)}) %collective-permute-start.7) | collective-permute-done | bytes 167968 | tf_op jit(solution)/shard_map/ppermute | solution.py:551
  57.9 3.6 %collective-permute-done.8.nb = f32[328,128]{1,0:T(8,128)S(1)} collective-permute-done((f32[328,128]{1,0:T(8,128)S(1)}, f32[328,128]{1,0:T(8,128)S(1)}, u32[]{:S(2)}, u32[]{:S(2)}) %collective-permute-start.8) | collective-permute-done | bytes 167968 | tf_op jit(solution)/shard_map/ppermute | solution.py:551
  61.5 3.1 %shard_map.64 = (f32[52,16,200]{2,1,0:T(8,128)}, f32[16,64,256]{2,1,0:T(8,128)S(1)}) custom-call(s32[1]{0:T(128)} %bitcast.par, f32[16,64,256]{2,1,0:T(8,128)S(1)} %shard_map.63.acc, f32[8,2,64,128]{3,2,1,0:T(8,128)S(1)} %shard_map.61.st3l, f32[4,2,64,128]{3,2,1,0:T(8,128)S(1)} %get-tuple-element.44.st3m, f32[4,2,64,128]{3,2,1,0:T(8,128)S(1)} %get-tuple-element.46.st3b, ...), custom_call_target="tpu_custom_call" | custom-call | flops 905969664 | bytes 5653280 | tf_op jit(solution)/shard_map/pallas_call | solution.py:530
  64.6 1.1 %shard_map.66 = f32[52,16,200]{2,1,0:T(8,128)} custom-call(f32[52,16,200]{2,1,0:T(8,128)} %get-tuple-element.53.before, f32[16,64,256]{2,1,0:T(8,128)S(1)} %get-tuple-element.54.accn, f32[4,2,64,128]{3,2,1,0:T(8,128)S(1)} %get-tuple-element.44.st3m, f32[4,2,64,128]{3,2,1,0:T(8,128)S(1)} %get-tuple-element.46.st3b, ...), custom_call_target="tpu_custom_call", output_to_operand_aliasing={{}: (0, {})} | custom-call | flops 226492416 | bytes 4700960 | tf_op jit(solution)/shard_map/pallas_call | solution.py:530
  (22 shorter events, 0.7 us)
Async XLA Ops:
  0.0 1.2 %copy-start.1 = (f32[16,52,200]{2,0,1:T(8,128)S(1)}, f32[16,52,200]{2,0,1:T(8,128)}, u32[]{:S(2)}) copy-start(f32[16,52,200]{2,0,1:T(8,128)} %param.5) | copy-start | bytes 1996804
  1.2 1.0 %copy-start.3 = (f32[8,52,200]{2,0,1:T(8,128)S(1)}, f32[8,52,200]{2,0,1:T(8,128)}, u32[]{:S(2)}) copy-start(f32[8,52,200]{2,0,1:T(8,128)} %param.6) | copy-start | bytes 998404
  2.4 9.9 %collective-permute-start = (f32[304,128]{1,0:T(8,128)S(1)}, f32[304,128]{1,0:T(8,128)S(1)}, u32[]{:S(2)}, u32[]{:S(2)}) collective-permute-start(f32[304,128]{1,0:T(8,128)S(1)} %get-tuple-element.30), channel_id=1, source_target_pairs={{0,1},{1,0},{2,3},{3,2},{4,5},{5,4},{6,7},{7,6},{8,9},{9,8},{10,11... | collective-permute-start | bytes 466952 | tf_op jit(solution)/shard_map/ppermute | solution.py:551
  2.5 9.8 %collective-permute-start.1 = (f32[304,128]{1,0:T(8,128)S(1)}, f32[304,128]{1,0:T(8,128)S(1)}, u32[]{:S(2)}, u32[]{:S(2)}) collective-permute-start(f32[304,128]{1,0:T(8,128)S(1)} %get-tuple-element.31), channel_id=1, source_target_pairs={{0,31},{1,2},{2,1},{3,4},{4,3},{5,6},{6,5},{7,8},{8,7},{9,10},{10,... | collective-permute-start | bytes 466952 | tf_op jit(solution)/shard_map/ppermute | solution.py:551
  4.9 14.2 %collective-permute-start.2 = (f32[260,128]{1,0:T(8,128)S(1)}, f32[260,128]{1,0:T(8,128)S(1)}, u32[]{:S(2)}, u32[]{:S(2)}) collective-permute-start(f32[260,128]{1,0:T(8,128)S(1)} %get-tuple-element.36), channel_id=1, source_target_pairs={{0,31},{1,30},{2,29},{3,28},{4,27},{5,26},{6,25},{7,24},{8,23},{9,... | collective-permute-start | bytes 399368 | tf_op jit(solution)/shard_map/ppermute | solution.py:551
  7.2 3.1 %copy-start = (f32[4,9,200,200]{3,2,1,0:T(8,128)S(1)}, f32[4,9,200,200]{3,2,1,0:T(8,128)}, u32[]{:S(2)}) copy-start(f32[4,9,200,200]{3,2,1,0:T(8,128)} %w.1) | copy-start | bytes 17280004
  10.3 4.1 %copy-start.2 = (f32[16,52,200]{2,0,1:T(8,128)S(1)}, f32[16,52,200]{2,0,1:T(8,128)}, u32[]{:S(2)}) copy-start(f32[16,52,200]{2,0,1:T(8,128)} %param.5) | copy-start | bytes 1996804
  10.3 4.1 %copy-start.4 = (f32[8,52,200]{2,0,1:T(8,128)S(1)}, f32[8,52,200]{2,0,1:T(8,128)}, u32[]{:S(2)}) copy-start(f32[8,52,200]{2,0,1:T(8,128)} %param.6) | copy-start | bytes 998404
  10.3 4.1 %copy-start.5 = (f32[4,200]{1,0:T(4,128)S(1)}, f32[4,200]{1,0:T(4,128)}, u32[]{:S(2)}) copy-start(f32[4,200]{1,0:T(4,128)} %bias.11) | copy-start | bytes 9604
  12.4 6.6 %collective-permute-start.3 = (f32[80,128]{1,0:T(8,128)S(1)}, f32[80,128]{1,0:T(8,128)S(1)}, u32[]{:S(2)}, u32[]{:S(2)}) collective-permute-start(f32[80,128]{1,0:T(8,128)S(1)} %shard_map.58), channel_id=1, source_target_pairs={{0,31},{1,30},{2,29},{3,28},{4,27},{5,26},{6,25},{7,24},{8,23},{9,... | collective-permute-start | bytes 122888 | tf_op jit(solution)/shard_map/ppermute | solution.py:551
  14.4 4.7 %copy-start.6 = (s32[200]{0:T(256)S(1)}, s32[200]{0:T(256)}, u32[]{:S(2)}) copy-start(s32[200]{0:T(256)} %param.7) | copy-start | bytes 2404
  22.3 12.9 %collective-permute-start.4 = (f32[376,128]{1,0:T(8,128)S(1)}, f32[376,128]{1,0:T(8,128)S(1)}, u32[]{:S(2)}, u32[]{:S(2)}) collective-permute-start(f32[376,128]{1,0:T(8,128)S(1)} %get-tuple-element.45), channel_id=1, source_target_pairs={{0,31},{1,30},{2,29},{3,28},{4,27},{5,26},{6,25},{7,24},{8,23},{9,... | collective-permute-start | bytes 577544 | tf_op jit(solution)/shard_map/ppermute | solution.py:551
  36.7 5.9 %collective-permute-start.5 = (f32[200,128]{1,0:T(8,128)S(1)}, f32[200,128]{1,0:T(8,128)S(1)}, u32[]{:S(2)}, u32[]{:S(2)}) collective-permute-start(f32[200,128]{1,0:T(8,128)S(1)} %get-tuple-element.49), channel_id=1, source_target_pairs={{0,1},{1,0},{2,3},{3,2},{4,5},{5,4},{6,7},{7,6},{8,9},{9,8},{10,11... | collective-permute-start | bytes 307208 | tf_op jit(solution)/shard_map/ppermute | solution.py:551
  36.8 5.9 %collective-permute-start.6 = (f32[200,128]{1,0:T(8,128)S(1)}, f32[200,128]{1,0:T(8,128)S(1)}, u32[]{:S(2)}, u32[]{:S(2)}) collective-permute-start(f32[200,128]{1,0:T(8,128)S(1)} %get-tuple-element.50), channel_id=1, source_target_pairs={{0,31},{1,2},{2,1},{3,4},{4,3},{5,6},{6,5},{7,8},{8,7},{9,10},{10,... | collective-permute-start | bytes 307208 | tf_op jit(solution)/shard_map/ppermute | solution.py:551
  39.0 18.9 %collective-permute-start.7 = (f32[328,128]{1,0:T(8,128)S(1)}, f32[328,128]{1,0:T(8,128)S(1)}, u32[]{:S(2)}, u32[]{:S(2)}) collective-permute-start(f32[328,128]{1,0:T(8,128)S(1)} %get-tuple-element.51), channel_id=1, source_target_pairs={{0,31},{1,30},{2,29},{3,28},{4,27},{5,26},{6,25},{7,24},{8,23},{9,... | collective-permute-start | bytes 503816 | tf_op jit(solution)/shard_map/ppermute | solution.py:551
  40.4 21.1 %collective-permute-start.8 = (f32[328,128]{1,0:T(8,128)S(1)}, f32[328,128]{1,0:T(8,128)S(1)}, u32[]{:S(2)}, u32[]{:S(2)}) collective-permute-start(f32[328,128]{1,0:T(8,128)S(1)} %get-tuple-element.52), channel_id=1, source_target_pairs={{0,31},{1,30},{2,29},{3,28},{4,27},{5,26},{6,25},{7,24},{8,23},{9,... | collective-permute-start | bytes 503816 | tf_op jit(solution)/shard_map/ppermute | solution.py:551
  43.0 21.6 %collective-permute-start.9 = (f32[200,128]{1,0:T(8,128)S(1)}, f32[200,128]{1,0:T(8,128)S(1)}, u32[]{:S(2)}, u32[]{:S(2)}) collective-permute-start(f32[200,128]{1,0:T(8,128)S(1)} %shard_map.65), channel_id=1, source_target_pairs={{0,31},{1,30},{2,29},{3,28},{4,27},{5,26},{6,25},{7,24},{8,23},{9,... | collective-permute-start | bytes 307208 | tf_op jit(solution)/shard_map/ppermute | solution.py:551

commit v4 on v3

--- a/solution.py
+++ b/solution.py
@@ -204,16 +204,24 @@
     return jnp.concatenate(lanes_of(ref, row), axis=1)
 
 
-def k_first(par, field, south, main, ewi, ewc, top):
+def k_first(par, field, south, main, ewi, ewc, top, fedge, sedge, last, sems):
     cols, rows, channels = field.shape
     rem = channels - LANES - HALF
     even = par[0] == 0
+    sides = (pl.ds(0, HALO), pl.ds(cols - HALO, HALO))
+    copies = [pltpu.make_async_copy(field.at[at], fedge.at[i], sems.at[i]) for i, at in enumerate(sides)]
+    copies += [pltpu.make_async_copy(south.at[at], sedge.at[i], sems.at[2 + i]) for i, at in enumerate(sides)]
+    copies += [pltpu.make_async_copy(field.at[:, pl.ds(rows - 8, 8), :], last, sems.at[4])]
+    for copy in copies:
+        copy.start()
+    for copy in copies[:4]:
+        copy.wait()
 
     def edge(flip):
         def get(k, t):
             pick = []
-            for col in (k, cols - HALO + k):
-                tiles = [tile_at(field, col, 0, rows, t), tile_at(south, col, 0, south.shape[1], t)]
+            for i in range(2):
+                tiles = [tile_at(fedge.at[i], k, 0, rows, t), tile_at(sedge.at[i], k, 0, south.shape[1], t)]
                 pick.append(jnp.concatenate(tiles, axis=0))
             return jnp.where(even != flip, pick[1], pick[0])
 
@@ -222,9 +230,10 @@
     tall = rows + south.shape[1]
     pack(edge(False), putter(ewi, tall), HALO, tall, rem)
     pack(edge(True), putter(ewc, tall), HALO, tall, rem)
+    copies[4].wait()
     for col in range(cols):
         for t in range(2):
-            put_column(top, 0, col, t, tile_at(field, col, rows - 8, rows, t))
+            put_column(top, 0, col, t, tile_at(last, col, 0, 8, t))
     pack(lambda k, t: top[7 - k, t, 0:cols, :], putter(main, cols), 3, cols, rem)
 
 
@@ -517,7 +526,7 @@
 
 VM = pl.BlockSpec(memory_space=pltpu.VMEM)
 SM = pl.BlockSpec(memory_space=pltpu.SMEM)
-HB = pl.BlockSpec(memory_space=pl.ANY)
+HB = pl.BlockSpec(memory_space=pltpu.HBM)
 
 
 def lhs(rows):
@@ -525,6 +534,7 @@
 
 
 def call(kernel, outs, scratch, args, smem=0, flops=0, limit=16, hbm=(), alias=None):
+    args = [pltpu.with_memory_space_constraint(a, pltpu.HBM) if i in hbm else a for i, a in enumerate(args)]
     moved = sum(a.size * a.dtype.itemsize for a in args[smem:])
     outs = [o if isinstance(o, jax.ShapeDtypeStruct) else jax.ShapeDtypeStruct(o, F32) for o in outs]
     return pl.pallas_call(
@@ -563,7 +573,10 @@
     main, ewi, ewc = call(
         k_first,
         [(packed_rows(3, cols, rem), LANES), (ew_rows, LANES), (ew_rows, LANES)],
-        [pltpu.VMEM(state(8, 56), F32)], [par, field, south_rows], smem=1,
+        [pltpu.VMEM(state(8, 56), F32), pltpu.VMEM((2, HALO, rows, channels), F32),
+         pltpu.VMEM((2, HALO, south, channels), F32), pltpu.VMEM((cols, 8, channels), F32),
+         pltpu.SemaphoreType.DMA((5,))],
+        [par, field, south_rows], smem=1, hbm=(1, 2), limit=16,
     )
     ewi, ewc, main = send(ewi, intra), send(ewc, cross), send(main, mirror)
     split = call(
@@ -618,11 +631,6 @@
     )
     ewi, ewc = send(ewi, intra), send(ewc, cross)
     nb = send(nb, mirror)
-    (nc,) = call(
-        functools.partial(k_corner2, rows=rows, rem=rem),
-        [(packed_rows(8, 2 * HALO, rem), LANES)], [], [par, ewi, ewc], smem=1,
-    )
-    nc = send(nc, mirror)
     (acc,) = call(
         functools.partial(k_f, cols=cols),
         [(rows, MW, 2 * LANES)],
@@ -630,6 +638,12 @@
         [st3l, st3m, st3b, se, *split[6:8], biases],
         flops=(rows - 3) * row_flops,
     )
+    ewi, ewc, acc = lax.optimization_barrier((ewi, ewc, acc))
+    (nc,) = call(
+        functools.partial(k_corner2, rows=rows, rem=rem),
+        [(packed_rows(8, 2 * HALO, rem), LANES)], [], [par, ewi, ewc], smem=1,
+    )
+    nc = send(nc, mirror)
     out, acc = call(
         functools.partial(k_g, cols=cols, rem=rem),
         [(cols, rows, channels), (rows, MW, 2 * LANES)],

time: 66.1 us -> 59.8 us (0.905)
  the two profiles are of different devices: /device:TPU:8 before, /device:TPU:0 now
where the time goes in v4:
time: 59.8 us; the launch traced here: 59.7 us
  Pallas kernels  30.6 us (51%)
  starting transfers between devices  26.5 us (44%)
  waiting for transfers between devices  2.3 us (4%)
    pallas_call x12, Pallas kernels, call(): pl.pallas_call(kernel, out_shape=outs, in_specs=[SM if i < smem else HB i...  30.6 us
    ppermute x10, starting transfers between devices, layers_of(): send = lambda x, route: lax.ppermute(x, 'lon', route)  26.5 us
    ppermute x10, waiting for transfers between devices, layers_of(): send = lambda x, route: lax.ppermute(x, 'lon', route)  2.3 us
  transfers between devices with their start and end apart: 10, of which 2 were waited for; matrix products, arithmetic and copies ran while one was open for 0% of the time, Pallas kernels for 42%

profile of v4, /device:TPU:0, one launch (start us, length us, event | category | flops | bytes accessed | tf_op | source)
XLA Modules:
  0.0 59.7 jit_solution(17563178446517059677)
XLA Ops:
  0.0 1.4 %shard_map.55 = (f32[260,128]{1,0:T(8,128)S(1)}, f32[304,128]{1,0:T(8,128)S(1)}, f32[304,128]{1,0:T(8,128)S(1)}) custom-call(s32[1]{0:T(128)} %bitcast.par, f32[52,16,200]{2,1,0:T(8,128)} %bitcast.5, f32[52,8,200]{2,1,0:T(8,128)} %bitcast.7), custom_call_target="tpu_custom_call" | custom-call | bytes 998400 | tf_op jit(solution)/shard_map/pallas_call | solution.py:540
  1.4 0.6 collective-permute-start
  2.0 6.6 %collective-permute-start.1 = (f32[304,128]{1,0:T(8,128)S(1)}, f32[304,128]{1,0:T(8,128)S(1)}, u32[]{:S(2)}, u32[]{:S(2)}) collective-permute-start(f32[304,128]{1,0:T(8,128)S(1)} %get-tuple-element.34), channel_id=1, source_target_pairs={{0,31},{1,2},{2,1},{3,4},{4,3},{5,6},{6,5},{7,8},{8,7},{9,10},{10,... | collective-permute-start | bytes 466952 | tf_op jit(solution)/shard_map/ppermute | solution.py:561
  8.6 0.1 collective-permute-start.2
  8.6 3.6 %shard_map.56 = (bf16[3,768,256]{2,1,0:T(8,128)(2,1)S(1)}, bf16[3,768,256]{2,1,0:T(8,128)(2,1)S(1)}, bf16[3,768,256]{2,1,0:T(8,128)(2,1)S(1)}, bf16[3,768,256]{2...) custom-call(f32[4,9,200,200]{3,2,1,0:T(8,128)} %w.1), custom_call_target="tpu_custom_call" | custom-call | bytes 5760000 | tf_op jit(solution)/shard_map/pallas_call | solution.py:540
  12.3 0.5 collective-permute-done.1.ewc
  12.8 0.2 shard_map.58
  13.0 5.6 %collective-permute-start.3 = (f32[80,128]{1,0:T(8,128)S(1)}, f32[80,128]{1,0:T(8,128)S(1)}, u32[]{:S(2)}, u32[]{:S(2)}) collective-permute-start(f32[80,128]{1,0:T(8,128)S(1)} %shard_map.58), channel_id=1, source_target_pairs={{0,31},{1,30},{2,29},{3,28},{4,27},{5,26},{6,25},{7,24},{8,23},{9,... | collective-permute-start | bytes 122888 | tf_op jit(solution)/shard_map/ppermute | solution.py:561
  18.5 4.7 %shard_map.57 = (f32[15,2,72,128]{3,2,1,0:T(8,128)S(1)}, f32[8,2,80,128]{3,2,1,0:T(8,128)S(1)}, f32[16,2,72,128]{3,2,1,0:T(8,128)S(1)}) custom-call(s32[1]{0:T(128)} %bitcast.par, f32[52,16,200]{2,1,0:T(8,128)S(1)} %bitcast.6, f32[52,8,200]{2,1,0:T(8,128)S(1)} %bitcast.8, f32[304,128]{1,0:T(8,128)S(1)} %collective-permute-done.ewi, ...), custom_call_target="tpu_custom_call" | custom-call | flops 3397386240 | bytes 3672192 | tf_op jit(solution)/shard_map/pallas_call | solution.py:540
  23.2 3.2 %shard_map.59 = (f32[4,2,72,128]{3,2,1,0:T(8,128)S(1)}, f32[376,128]{1,0:T(8,128)S(1)}) custom-call(f32[16,2,72,128]{3,2,1,0:T(8,128)S(1)} %get-tuple-element.38.edge, f32[260,128]{1,0:T(8,128)S(1)} %collective-permute-done.2.main, f32[80,128]{1,0:T(8,128)S(1)} %collective-permute-done.3.corner, f32[15,2,72,128]{3,2,1,0:T(8,128)S(1)} %get-tuple-element.37.st1, ...), custom_call_target="tpu_custom_call" | custom-call | flops 1585446912 | bytes 7182240 | tf_op jit(solution)/shard_map/pallas_call | solution.py:540
  26.5 2.4 %collective-permute-start.4 = (f32[376,128]{1,0:T(8,128)S(1)}, f32[376,128]{1,0:T(8,128)S(1)}, u32[]{:S(2)}, u32[]{:S(2)}) collective-permute-start(f32[376,128]{1,0:T(8,128)S(1)} %get-tuple-element.46), channel_id=1, source_target_pairs={{0,31},{1,30},{2,29},{3,28},{4,27},{5,26},{6,25},{7,24},{8,23},{9,... | collective-permute-start | bytes 577544 | tf_op jit(solution)/shard_map/ppermute | solution.py:561
  28.8 4.7 %shard_map.60 = (f32[12,2,72,128]{3,2,1,0:T(8,128)S(1)}, f32[4,2,64,128]{3,2,1,0:T(8,128)S(1)}, f32[328,128]{1,0:T(8,128)S(1)}) custom-call(f32[15,2,72,128]{3,2,1,0:T(8,128)S(1)} %get-tuple-element.37.st1, f32[4,2,72,128]{3,2,1,0:T(8,128)S(1)} %get-tuple-element.42.st2b, bf16[3,768,256]{2,1,0:T(8,128)(2,1)S(1)} %get-tuple-element.40.wh1, ...), custom_call_target="tpu_custom_call" | custom-call | flops 2717908992 | bytes 6122624 | tf_op jit(solution)/shard_map/pallas_call | solution.py:540
  33.5 3.1 %collective-permute-start.7 = (f32[328,128]{1,0:T(8,128)S(1)}, f32[328,128]{1,0:T(8,128)S(1)}, u32[]{:S(2)}, u32[]{:S(2)}) collective-permute-start(f32[328,128]{1,0:T(8,128)S(1)} %get-tuple-element.57), channel_id=1, source_target_pairs={{0,31},{1,30},{2,29},{3,28},{4,27},{5,26},{6,25},{7,24},{8,23},{9,... | collective-permute-start | bytes 503816 | tf_op jit(solution)/shard_map/ppermute | solution.py:561
  36.6 3.6 %shard_map.61.st3l = f32[8,2,64,128]{3,2,1,0:T(8,128)S(1)} custom-call(f32[15,2,72,128]{3,2,1,0:T(8,128)S(1)} %get-tuple-element.37.st1, f32[12,2,72,128]{3,2,1,0:T(8,128)S(1)} %get-tuple-element.45.st2m.st2, f32[8,2,80,128]{3,2,1,0:T(8,128)S(1)} %get-tuple-element.47.se, bf16[3,768,256]{2,1,0:T(8,128)(2,1)S(1)} %get-tuple-element.40.wh1, ...), custom_call_target="tpu_custom_call" | custom-call | flops 2717908992 | bytes 7367808 | tf_op jit(solution)/shard_map/pallas_call | solution.py:540
  40.2 1.5 %shard_map.62 = (f32[4,2,64,128]{3,2,1,0:T(8,128)S(1)}, f32[328,128]{1,0:T(8,128)S(1)}, f32[200,128]{1,0:T(8,128)S(1)}, f32[200,128]{1,0:T(8,128)S(1)}) custom-call(s32[1]{0:T(128)} %bitcast.par, f32[12,2,72,128]{3,2,1,0:T(8,128)S(1)} %get-tuple-element.45.st2m.st2, f32[376,128]{1,0:T(8,128)S(1)} %collective-permute-done.4.north, ...), custom_call_target="tpu_custom_call" | custom-call | flops 905969664 | bytes 4226976 | tf_op jit(solution)/shard_map/pallas_call | solution.py:540
  41.7 0.1 collective-permute-start.5
  41.7 2.4 %collective-permute-start.6 = (f32[200,128]{1,0:T(8,128)S(1)}, f32[200,128]{1,0:T(8,128)S(1)}, u32[]{:S(2)}, u32[]{:S(2)}) collective-permute-start(f32[200,128]{1,0:T(8,128)S(1)} %get-tuple-element.50), channel_id=1, source_target_pairs={{0,31},{1,2},{2,1},{3,4},{4,3},{5,6},{6,5},{7,8},{8,7},{9,10},{10,... | collective-permute-start | bytes 307208 | tf_op jit(solution)/shard_map/ppermute | solution.py:561
  44.1 3.0 %collective-permute-start.8 = (f32[328,128]{1,0:T(8,128)S(1)}, f32[328,128]{1,0:T(8,128)S(1)}, u32[]{:S(2)}, u32[]{:S(2)}) collective-permute-start(f32[328,128]{1,0:T(8,128)S(1)} %get-tuple-element.58), channel_id=1, source_target_pairs={{0,31},{1,30},{2,29},{3,28},{4,27},{5,26},{6,25},{7,24},{8,23},{9,... | collective-permute-start | bytes 503816 | tf_op jit(solution)/shard_map/ppermute | solution.py:561
  47.1 3.3 %shard_map.63.acc = f32[16,64,256]{2,1,0:T(8,128)S(1)} custom-call(f32[8,2,64,128]{3,2,1,0:T(8,128)S(1)} %shard_map.61.st3l, f32[4,2,64,128]{3,2,1,0:T(8,128)S(1)} %get-tuple-element.48.st3m, f32[4,2,64,128]{3,2,1,0:T(8,128)S(1)} %get-tuple-element.51.st3b, f32[8,2,80,128]{3,2,1,0:T(8,128)S(1)} %get-tuple-element.47.se, ...), custom_call_target="tpu_custom_call" | custom-call | flops 2944401408 | bytes 4066432 | tf_op jit(solution)/shard_map/pallas_call | solution.py:540
  50.4 0.2 shard_map.65
  50.7 2.8 %collective-permute-start.9 = (f32[200,128]{1,0:T(8,128)S(1)}, f32[200,128]{1,0:T(8,128)S(1)}, u32[]{:S(2)}, u32[]{:S(2)}) collective-permute-start(f32[200,128]{1,0:T(8,128)S(1)} %shard_map.65), channel_id=1, source_target_pairs={{0,31},{1,30},{2,29},{3,28},{4,27},{5,26},{6,25},{7,24},{8,23},{9,... | collective-permute-start | bytes 307208 | tf_op jit(solution)/shard_map/ppermute | solution.py:561
  53.5 3.1 %shard_map.64 = (f32[52,16,200]{2,1,0:T(8,128)}, f32[16,64,256]{2,1,0:T(8,128)S(1)}) custom-call(s32[1]{0:T(128)} %bitcast.par, f32[16,64,256]{2,1,0:T(8,128)S(1)} %shard_map.63.acc, f32[8,2,64,128]{3,2,1,0:T(8,128)S(1)} %shard_map.61.st3l, f32[4,2,64,128]{3,2,1,0:T(8,128)S(1)} %get-tuple-element.48.st3m, f32[4,2,64,128]{3,2,1,0:T(8,128)S(1)} %get-tuple-element.51.st3b, ...), custom_call_target="tpu_custom_call" | custom-call | flops 905969664 | bytes 5653280 | tf_op jit(solution)/shard_map/pallas_call | solution.py:540
  56.6 1.8 %collective-permute-done.9.nc = f32[200,128]{1,0:T(8,128)S(1)} collective-permute-done((f32[200,128]{1,0:T(8,128)S(1)}, f32[200,128]{1,0:T(8,128)S(1)}, u32[]{:S(2)}, u32[]{:S(2)}) %collective-permute-start.9) | collective-permute-done | bytes 102432 | tf_op jit(solution)/shard_map/ppermute | solution.py:561
  58.4 1.1 %shard_map.66 = f32[52,16,200]{2,1,0:T(8,128)} custom-call(f32[52,16,200]{2,1,0:T(8,128)} %get-tuple-element.59.before, f32[16,64,256]{2,1,0:T(8,128)S(1)} %get-tuple-element.60.accn, f32[4,2,64,128]{3,2,1,0:T(8,128)S(1)} %get-tuple-element.48.st3m, f32[4,2,64,128]{3,2,1,0:T(8,128)S(1)} %get-tuple-element.51.st3b, ...), custom_call_target="tpu_custom_call", output_to_operand_aliasing={{}: (0, {})} | custom-call | flops 226492416 | bytes 4700960 | tf_op jit(solution)/shard_map/pallas_call | solution.py:540
  (16 shorter events, 0.0 us)
Async XLA Ops:
  1.4 10.8 %collective-permute-start = (f32[304,128]{1,0:T(8,128)S(1)}, f32[304,128]{1,0:T(8,128)S(1)}, u32[]{:S(2)}, u32[]{:S(2)}) collective-permute-start(f32[304,128]{1,0:T(8,128)S(1)} %get-tuple-element.33), channel_id=1, source_target_pairs={{0,1},{1,0},{2,3},{3,2},{4,5},{5,4},{6,7},{7,6},{8,9},{9,8},{10,11... | collective-permute-start | bytes 466952 | tf_op jit(solution)/shard_map/ppermute | solution.py:561
  2.0 10.8 %collective-permute-start.1 = (f32[304,128]{1,0:T(8,128)S(1)}, f32[304,128]{1,0:T(8,128)S(1)}, u32[]{:S(2)}, u32[]{:S(2)}) collective-permute-start(f32[304,128]{1,0:T(8,128)S(1)} %get-tuple-element.34), channel_id=1, source_target_pairs={{0,31},{1,2},{2,1},{3,4},{4,3},{5,6},{6,5},{7,8},{8,7},{9,10},{10,... | collective-permute-start | bytes 466952 | tf_op jit(solution)/shard_map/ppermute | solution.py:561
  8.6 10.0 %copy-start = (f32[16,52,200]{2,0,1:T(8,128)S(1)}, f32[16,52,200]{2,0,1:T(8,128)}, u32[]{:S(2)}) copy-start(f32[16,52,200]{2,0,1:T(8,128)} %param.5) | copy-start | bytes 1996804
  8.6 10.0 %copy-start.1 = (f32[8,52,200]{2,0,1:T(8,128)S(1)}, f32[8,52,200]{2,0,1:T(8,128)}, u32[]{:S(2)}) copy-start(f32[8,52,200]{2,0,1:T(8,128)} %param.6) | copy-start | bytes 998404
  8.6 10.0 %copy-start.2 = (f32[4,200]{1,0:T(4,128)S(1)}, f32[4,200]{1,0:T(4,128)}, u32[]{:S(2)}) copy-start(f32[4,200]{1,0:T(4,128)} %bias.11) | copy-start | bytes 9604
  8.6 14.6 %collective-permute-start.2 = (f32[260,128]{1,0:T(8,128)S(1)}, f32[260,128]{1,0:T(8,128)S(1)}, u32[]{:S(2)}, u32[]{:S(2)}) collective-permute-start(f32[260,128]{1,0:T(8,128)S(1)} %get-tuple-element.39), channel_id=1, source_target_pairs={{0,31},{1,30},{2,29},{3,28},{4,27},{5,26},{6,25},{7,24},{8,23},{9,... | collective-permute-start | bytes 399368 | tf_op jit(solution)/shard_map/ppermute | solution.py:561
  13.0 10.3 %collective-permute-start.3 = (f32[80,128]{1,0:T(8,128)S(1)}, f32[80,128]{1,0:T(8,128)S(1)}, u32[]{:S(2)}, u32[]{:S(2)}) collective-permute-start(f32[80,128]{1,0:T(8,128)S(1)} %shard_map.58), channel_id=1, source_target_pairs={{0,31},{1,30},{2,29},{3,28},{4,27},{5,26},{6,25},{7,24},{8,23},{9,... | collective-permute-start | bytes 122888 | tf_op jit(solution)/shard_map/ppermute | solution.py:561
  18.5 4.7 %copy-start.3 = (s32[200]{0:T(256)S(1)}, s32[200]{0:T(256)}, u32[]{:S(2)}) copy-start(s32[200]{0:T(256)} %param.7) | copy-start | bytes 2404
  26.5 13.7 %collective-permute-start.4 = (f32[376,128]{1,0:T(8,128)S(1)}, f32[376,128]{1,0:T(8,128)S(1)}, u32[]{:S(2)}, u32[]{:S(2)}) collective-permute-start(f32[376,128]{1,0:T(8,128)S(1)} %get-tuple-element.46), channel_id=1, source_target_pairs={{0,31},{1,30},{2,29},{3,28},{4,27},{5,26},{6,25},{7,24},{8,23},{9,... | collective-permute-start | bytes 577544 | tf_op jit(solution)/shard_map/ppermute | solution.py:561
  33.5 20.0 %collective-permute-start.7 = (f32[328,128]{1,0:T(8,128)S(1)}, f32[328,128]{1,0:T(8,128)S(1)}, u32[]{:S(2)}, u32[]{:S(2)}) collective-permute-start(f32[328,128]{1,0:T(8,128)S(1)} %get-tuple-element.57), channel_id=1, source_target_pairs={{0,31},{1,30},{2,29},{3,28},{4,27},{5,26},{6,25},{7,24},{8,23},{9,... | collective-permute-start | bytes 503816 | tf_op jit(solution)/shard_map/ppermute | solution.py:561
  41.7 8.8 %collective-permute-start.5 = (f32[200,128]{1,0:T(8,128)S(1)}, f32[200,128]{1,0:T(8,128)S(1)}, u32[]{:S(2)}, u32[]{:S(2)}) collective-permute-start(f32[200,128]{1,0:T(8,128)S(1)} %get-tuple-element.49), channel_id=1, source_target_pairs={{0,1},{1,0},{2,3},{3,2},{4,5},{5,4},{6,7},{7,6},{8,9},{9,8},{10,11... | collective-permute-start | bytes 307208 | tf_op jit(solution)/shard_map/ppermute | solution.py:561
  41.7 8.7 %collective-permute-start.6 = (f32[200,128]{1,0:T(8,128)S(1)}, f32[200,128]{1,0:T(8,128)S(1)}, u32[]{:S(2)}, u32[]{:S(2)}) collective-permute-start(f32[200,128]{1,0:T(8,128)S(1)} %get-tuple-element.50), channel_id=1, source_target_pairs={{0,31},{1,2},{2,1},{3,4},{4,3},{5,6},{6,5},{7,8},{8,7},{9,10},{10,... | collective-permute-start | bytes 307208 | tf_op jit(solution)/shard_map/ppermute | solution.py:561
  44.1 9.4 %collective-permute-start.8 = (f32[328,128]{1,0:T(8,128)S(1)}, f32[328,128]{1,0:T(8,128)S(1)}, u32[]{:S(2)}, u32[]{:S(2)}) collective-permute-start(f32[328,128]{1,0:T(8,128)S(1)} %get-tuple-element.58), channel_id=1, source_target_pairs={{0,31},{1,30},{2,29},{3,28},{4,27},{5,26},{6,25},{7,24},{8,23},{9,... | collective-permute-start | bytes 503816 | tf_op jit(solution)/shard_map/ppermute | solution.py:561
  50.7 7.7 %collective-permute-start.9 = (f32[200,128]{1,0:T(8,128)S(1)}, f32[200,128]{1,0:T(8,128)S(1)}, u32[]{:S(2)}, u32[]{:S(2)}) collective-permute-start(f32[200,128]{1,0:T(8,128)S(1)} %shard_map.65), channel_id=1, source_target_pairs={{0,31},{1,30},{2,29},{3,28},{4,27},{5,26},{6,25},{7,24},{8,23},{9,... | collective-permute-start | bytes 307208 | tf_op jit(solution)/shard_map/ppermute | solution.py:561

commit v5 on v4

--- a/solution.py
+++ b/solution.py
@@ -304,8 +304,10 @@
             for h in range(0, rows, 8):
                 put_column(x0, h, HALO + col, t, tile_at(field, col, h, h + 8, t))
             put_column(se, 0, HALO + col, t, tile_at(south, col, 0, 8, t))
-    sources = run(se, deep - 1, 1, (1, 2, 3)) + run(x0, 0, rows, (1, 2, 3))
-    conv(buffers, wh, wl, bias_of(bias, 0), 1, sources, rows - 1, 5, add_rows(st1, 0, x0, 0, 2, 5))
+    count = st1.shape[0]
+    first = rows - 1 - count
+    sources = run(x0, first - 1, count + 2, (1, 2, 3))
+    conv(buffers, wh, wl, bias_of(bias, 0), 1, sources, count, 5, add_rows(st1, 0, x0, first, 2, 5))
 
 
 def signed(tiles, sign):
@@ -327,7 +329,7 @@
         put_row(dst, dst_row + k, left + cols, [x[HALO:] for x in t])
 
 
-def k_b(edge, main, corner, st1, sign, wh0, wl0, wh1, wl1, bias, st2, out, x0, xr, x1, hi, lo, *buffers, cols, rem):
+def k_b(edge, se, main, corner, st1, sign, wh0, wl0, wh1, wl1, bias, st2, out, low, x0, xr, x1, hi, lo, h1, l1, *buffers, cols, rem):
     rows = edge.shape[0]
     sign = lanes_of(sign, 0)
     north_rows(xr, 1, main, None, 3, cols, HALO, rem)
@@ -336,7 +338,7 @@
     for t in range(2):
         x0[2, t] = xr[1, t] * sign[t]
         xr[0, t] = edge[rows - 1, t] * sign[t]
-    x1[0:5] = st1[rows - 6 : rows - 1]
+    x1[0:5] = st1[st1.shape[0] - 5 :]
     offs = (1, 2, 3)
     fill(hi, lo, 0, x0, 0, 3, offs)
     fill(hi, lo, 3, xr, 0, 4, offs[::-1])
@@ -354,25 +356,36 @@
                 x1[5, t, 0:MW, :] = x0[1, t, 2 : 2 + MW, :] + g
             else:
                 x1[5 + q, t, 0:MW, :] = sign[t] * (xr[q, t, 2 : 2 + MW, :] + g)
+    count = low.shape[0]
+    sources = run(se, se.shape[0] - 1, 1, offs) + run(edge, 0, count + 1, offs)
+    conv((h1, l1), wh0, wl0, bias_of(bias, 0), 1, sources, count, count, add_rows(low, 0, edge, 0, 2, count))
     conv(buffers, wh1, wl1, bias_of(bias, 1), 2, run(x1, 0, 8, (0, 2, 4)), 4, 4, add_rows(st2, 0, x1, 2, 2, 4))
     wide = cols + 8
     pack(lambda k, t: st2[3 - k, t, 0:wide, :], putter(out, wide), 4, wide, rem)
 
 
-def k_c1(st1, st2b, wh1, wl1, wh2, wl2, bias, st2, st3, out, h1, l1, h2, l2, *, cols, rem):
-    conv((h1, l1), wh1, wl1, bias_of(bias, 1), 2, run(st1, 2, 12, (0, 2, 4)), 8, 4, add_rows(st2, 0, st1, 4, 2, 4))
-    st2[8:12] = st2b[...]
-    conv((h2, l2), wh2, wl2, bias_of(bias, 2), 4, run(st2, 0, 12, (0, 4, 8)), 4, 4, add_rows(st3, 0, st2, 4, 4, 4))
-    pack(lambda k, t: st3[3 - k, t, 0:cols, :], putter(out, cols), 4, cols, rem)
-
-
-def k_c2(st1, st2m, se, wh1, wl1, wh2, wl2, bias, st3, x2, h1, l1, h2, l2):
+def k_c1(low, st1a, st2b, se, wh1, wl1, wh2, wl2, bias, st2, st3, st3l, out, st1, h0, l0, h1, l1, h2, l2, *, cols, rem):
     south = se.shape[0]
+    done = low.shape[0]
+    st1[0:done] = low[...]
+    st1[done:] = st1a[...]
+    bias1 = bias_of(bias, 1)
+    conv((h1, l1), wh1, wl1, bias1, 2, run(st1, 2, 12, (0, 2, 4)), 8, 4, add_rows(st2, 4, st1, 4, 2, 4))
     sources = run(se, south - 2, 2, (2, 4, 6)) + run(st1, 0, 6, (0, 2, 4))
-    conv((h1, l1), wh1, wl1, bias_of(bias, 1), 2, sources, 4, 4, add_rows(x2, 0, st1, 0, 2, 4))
-    x2[4:8] = st2m[0:4]
-    sources = run(se, south - 4, 4, (4, 8, 12)) + run(x2, 0, 4, (0, 4, 8)) + run(st2m, 0, 8, (0, 4, 8))
-    conv((h2, l2), wh2, wl2, bias_of(bias, 2), 4, sources, 8, 4, add_rows(st3, 0, x2, 0, 4, 4))
+    conv((h0, l0), wh1, wl1, bias1, 2, sources, 4, 4, add_rows(st2, 0, st1, 0, 2, 4))
+    st2[12:16] = st2b[...]
+    bias2 = bias_of(bias, 2)
+    sources = run(se, south - 4, 4, (4, 8, 12)) + run(st2, 0, 16, (0, 4, 8))
+    for i in range(8, 20):
+        fill_row(h2, l2, i, *sources[i])
+    for row in (8, 0, 4):
+        for i in range(8 if row == 0 else 0):
+            fill_row(h2, l2, i, *sources[i])
+        total = products(h2, l2, wh2, wl2, (0, 1, 2), row, 4, 4)
+        emit = add_rows(st3, -8, st2, 0, 4, 4) if row == 8 else add_rows(st3l, 0, st2, 0, 4, 4)
+        emit(row, jax.nn.gelu(total + bias2))
+        if row == 8:
+            pack(lambda k, t: st3[3 - k, t, 0:cols, :], putter(out, cols), 4, cols, rem)
 
 
 def row_of(parts, row):
@@ -385,8 +398,8 @@
 def k_d(par, st2, north, st3l, st3m, sign, wh, wl, bias, st3b, out, ewi, ewc, x2, hi, lo, *, cols, rem):
     wide = cols + 8
     north_rows(x2, 0, north, lanes_of(sign, 0), 4, wide, 0, rem)
-    sources = run(st2, 4, 8, (0, 4, 8)) + run(x2, 0, 4, (0, 4, 8))
-    conv((hi, lo), wh, wl, bias_of(bias, 2), 4, sources, 4, 4, add_rows(st3b, 0, st2, 8, 4, 4))
+    sources = run(st2, 8, 8, (0, 4, 8)) + run(x2, 0, 4, (0, 4, 8))
+    conv((hi, lo), wh, wl, bias_of(bias, 2), 4, sources, 4, 4, add_rows(st3b, 0, st2, 12, 4, 4))
     pack(lambda k, t: st3b[3 - k, t, 0:cols, :], putter(out, cols), 4, cols, rem)
     even = par[0] == 0
     parts = (st3l, st3m, st3b)
@@ -410,9 +423,9 @@
         out[col, first : first + 8, LANES:channels] = get_column(src, 0, col, 1)[:, 0 : channels - LANES]
 
 
-def k_f(st3l, st3m, st3b, se, wh, wl, bias, acc, x3, hi, lo, *, cols):
-    rows = acc.shape[0]
-    south = se.shape[0]
+def k_f(st3l, st3m, st3b, se, wh, wl, bias, acc, top, x3, hi, lo, *, cols):
+    low, south = acc.shape[0], se.shape[0]
+    rows = low + top.shape[0]
     zero = jnp.zeros((2, HALO, LANES), F32)
     for k in range(rows + south):
         ref, row = (se, k) if k < south else row_of((st3l, st3m, st3b), k - south)
@@ -423,12 +436,13 @@
     bias = bias_of(bias, 3)
     filled = 0
     for row in range(0, rows, 4):
-        taps = (0, 1, 2) if row < rows - 8 else (0, 1)
+        taps = (0, 1, 2) if row < low else (0, 1)
         while filled < row + 4 + 8 * taps[-1]:
             fill_row(hi, lo, filled, x3, filled, (0, 8, 16))
             filled += 1
         total = products(hi, lo, wh, wl, taps, row, 4, 8)
-        acc[row : row + 4] = (total + bias).reshape(4, MW, 2 * LANES)
+        ref, at = (acc, row) if row < low else (top, row - low)
+        ref[at : at + 4] = (total + bias).reshape(4, MW, 2 * LANES)
 
 
 def split_bf16(x):
@@ -451,8 +465,8 @@
     return lambda a: ref[a, at : at + 2 * LANES, :]
 
 
-def k_g(par, acc, st3l, st3m, st3b, se, ewi, ewc, na, nb, sign, wh, wl, out, accn, xn, halo, end, hi, lo, *, cols, rem):
-    rows = acc.shape[0]
+def k_g(par, acc1, acc, st3l, st3m, st3b, se, ewi, ewc, na, nb, sign, wh, wl, out, accn, xn, halo, end, hi, lo, *, cols, rem):
+    rows = accn.shape[0]
     channels = out.shape[-1]
     south = se.shape[0]
     sign = lanes_of(sign, 0)
@@ -462,12 +476,12 @@
     north_rows(xn, 0, nb, sign, 4, cols, HALO, rem)
     north_rows(xn, 4, na, sign, 4, cols, HALO, rem)
     fill(hi, lo, 0, xn, 0, 8, (0, 8, 16))
-    accn[0 : rows - 8] = acc[0 : rows - 8]
+    accn[0 : rows - 8] = acc1[...]
     for i in range(2):
         at = slice(4 * i, 4 * i + 4)
         lh = hi[at].reshape(4 * MW, hi.shape[-1])
         ll = lo[at].reshape(4 * MW, hi.shape[-1])
-        total = acc[rows - 8 + 4 * i : rows - 4 + 4 * i].reshape(4 * MW, 2 * LANES)
+        total = acc[4 * i : 4 * i + 4].reshape(4 * MW, 2 * LANES)
         for left, right in ((lh, wh), (ll, wh), (lh, wl)):
             total = total + jnp.dot(left, right[2], preferred_element_type=F32)
         accn[rows - 8 + 4 * i : rows - 4 + 4 * i] = total.reshape(4, MW, 2 * LANES)
@@ -593,34 +607,27 @@
     corner = send(corner, mirror)
     st1, se, x0 = call(
         k_a,
-        [state(rows - 1, 72), state(south, 80), state(rows, 72)],
-        lhs(rows + 1),
+        [state(rows - 6, 72), state(south, 80), state(rows, 72)],
+        lhs(rows - 4),
         [par, field, south_rows, ewi, ewc, *split[0:2], biases],
-        smem=1, flops=15 * row_flops,
-    )
-    st2b, north = call(
+        smem=1, flops=10 * row_flops,
+    )
+    st2b, north, low = call(
         functools.partial(k_b, cols=cols, rem=rem),
-        [state(4, 72), (packed_rows(4, cols + 8, rem), LANES)],
-        [pltpu.VMEM(state(3, 72), F32), pltpu.VMEM(state(4, 72), F32), pltpu.VMEM(state(8, 72), F32)] + lhs(7) + lhs(8),
-        [x0, main, corner, st1, sign, *split[0:4], biases],
-        flops=7 * row_flops,
+        [state(4, 72), (packed_rows(4, cols + 8, rem), LANES), state(5, 72)],
+        [pltpu.VMEM(state(3, 72), F32), pltpu.VMEM(state(4, 72), F32), pltpu.VMEM(state(8, 72), F32)] + lhs(7) + lhs(7) + lhs(8),
+        [x0, se, main, corner, st1, sign, *split[0:4], biases],
+        flops=12 * row_flops,
     )
     north = send(north, mirror)
-    st2m, st3m, na = call(
+    st2m, st3m, st3l, na = call(
         functools.partial(k_c1, cols=cols, rem=rem),
-        [state(12, 72), state(4, MW), (packed_rows(4, cols, rem), LANES)],
-        lhs(12) + lhs(12),
-        [st1, st2b, *split[2:6], biases],
-        flops=12 * row_flops,
+        [state(rows, 72), state(4, MW), state(8, MW), (packed_rows(4, cols, rem), LANES)],
+        [pltpu.VMEM(state(rows - 1, 72), F32)] + lhs(8) + lhs(12) + lhs(rows + 4),
+        [low, st1, st2b, se, *split[2:6], biases],
+        flops=24 * row_flops,
     )
     na = send(na, mirror)
-    (st3l,) = call(
-        k_c2,
-        [state(8, MW)],
-        [pltpu.VMEM(state(8, 72), F32)] + lhs(8) + lhs(16),
-        [st1, st2m, se, *split[2:6], biases],
-        flops=12 * row_flops,
-    )
     ew_rows = packed_rows(rows, HALO, rem)
     st3b, nb, ewi, ewc = call(
         functools.partial(k_d, cols=cols, rem=rem),
@@ -631,14 +638,14 @@
     )
     ewi, ewc = send(ewi, intra), send(ewc, cross)
     nb = send(nb, mirror)
-    (acc,) = call(
+    acc, acc2 = call(
         functools.partial(k_f, cols=cols),
-        [(rows, MW, 2 * LANES)],
+        [(rows - 8, MW, 2 * LANES), (8, MW, 2 * LANES)],
         [pltpu.VMEM(state(rows + south, 80), F32)] + lhs(rows + south),
         [st3l, st3m, st3b, se, *split[6:8], biases],
         flops=(rows - 3) * row_flops,
     )
-    ewi, ewc, acc = lax.optimization_barrier((ewi, ewc, acc))
+    ewi, ewc, acc, acc2 = lax.optimization_barrier((ewi, ewc, acc, acc2))
     (nc,) = call(
         functools.partial(k_corner2, rows=rows, rem=rem),
         [(packed_rows(8, 2 * HALO, rem), LANES)], [], [par, ewi, ewc], smem=1,
@@ -649,7 +656,7 @@
         [(cols, rows, channels), (rows, MW, 2 * LANES)],
         [pltpu.VMEM(state(8, 80), F32), pltpu.VMEM((2, (rows + south + 8) * HALO, 2 * LANES), F32),
          pltpu.VMEM((2,) + state(8, MW), F32)] + lhs(8),
-        [par, acc, st3l, st3m, st3b, se, ewi, ewc, na, nb, sign, *split[6:8]],
+        [par, acc, acc2, st3l, st3m, st3b, se, ewi, ewc, na, nb, sign, *split[6:8]],
         smem=1, flops=4 * row_flops,
     )
     (out,) = call(

time: 59.8 us -> 57.3 us (0.958)
  Pallas kernels: 30.6 us -> 28 us
  starting transfers between devices: 26.5 us -> 27.8 us
  waiting for transfers between devices: 2.3 us -> 1.08 us
    pallas_call x12 -> x11, Pallas kernels: 30.6 us -> 28 us  [call(): pl.pallas_call(kernel, out_shape=outs, in_specs=[SM if i < smem else HB i...]
    ppermute x10, starting transfers between devices: 26.5 us -> 27.8 us  [layers_of(): send = lambda x, route: lax.ppermute(x, 'lon', route)]
    ppermute x10, waiting for transfers between devices: 2.3 us -> 1.08 us  [layers_of(): send = lambda x, route: lax.ppermute(x, 'lon', route)]
  transfers between devices with their start and end apart: 10 -> 10, of which waited for: 2 -> 2; matrix products, arithmetic and copies ran while one was open for 0% -> 0% of each run, Pallas kernels for 42% -> 38%
where the time goes in v5:
time: 57.3 us; the launch traced here: 57.2 us
  Pallas kernels  28 us (49%)
  starting transfers between devices  27.8 us (49%)
  waiting for transfers between devices  1.08 us (2%)
    pallas_call x11, Pallas kernels, call(): pl.pallas_call(kernel, out_shape=outs, in_specs=[SM if i < smem else HB i...  28 us
    ppermute x10, starting transfers between devices, layers_of(): send = lambda x, route: lax.ppermute(x, 'lon', route)  27.8 us
  transfers between devices with their start and end apart: 10, of which 2 were waited for; matrix products, arithmetic and copies ran while one was open for 0% of the time, Pallas kernels for 38%

profile of v5, /device:TPU:0, one launch (start us, length us, event | category | flops | bytes accessed | tf_op | source)
XLA Modules:
  0.0 57.2 jit_solution(2119812585809387940)
XLA Ops:
  0.0 1.4 %shard_map.55 = (f32[260,128]{1,0:T(8,128)S(1)}, f32[304,128]{1,0:T(8,128)S(1)}, f32[304,128]{1,0:T(8,128)S(1)}) custom-call(s32[1]{0:T(128)} %bitcast.par, f32[52,16,200]{2,1,0:T(8,128)} %bitcast.5, f32[52,8,200]{2,1,0:T(8,128)} %bitcast.7), custom_call_target="tpu_custom_call" | custom-call | bytes 998400 | tf_op jit(solution)/shard_map/pallas_call | solution.py:554
  1.4 0.6 collective-permute-start
  2.0 6.6 %collective-permute-start.1 = (f32[304,128]{1,0:T(8,128)S(1)}, f32[304,128]{1,0:T(8,128)S(1)}, u32[]{:S(2)}, u32[]{:S(2)}) collective-permute-start(f32[304,128]{1,0:T(8,128)S(1)} %get-tuple-element.39), channel_id=1, source_target_pairs={{0,31},{1,2},{2,1},{3,4},{4,3},{5,6},{6,5},{7,8},{8,7},{9,10},{10,... | collective-permute-start | bytes 466952 | tf_op jit(solution)/shard_map/ppermute | solution.py:575
  8.6 0.1 collective-permute-start.2
  8.6 3.6 %shard_map.56 = (bf16[3,768,256]{2,1,0:T(8,128)(2,1)S(1)}, bf16[3,768,256]{2,1,0:T(8,128)(2,1)S(1)}, bf16[3,768,256]{2,1,0:T(8,128)(2,1)S(1)}, bf16[3,768,256]{2...) custom-call(f32[4,9,200,200]{3,2,1,0:T(8,128)} %w.1), custom_call_target="tpu_custom_call" | custom-call | bytes 5760000 | tf_op jit(solution)/shard_map/pallas_call | solution.py:554
  12.3 0.5 collective-permute-done.1.ewc
  12.8 0.2 shard_map.58
  13.0 5.6 %collective-permute-start.3 = (f32[80,128]{1,0:T(8,128)S(1)}, f32[80,128]{1,0:T(8,128)S(1)}, u32[]{:S(2)}, u32[]{:S(2)}) collective-permute-start(f32[80,128]{1,0:T(8,128)S(1)} %shard_map.58), channel_id=1, source_target_pairs={{0,31},{1,30},{2,29},{3,28},{4,27},{5,26},{6,25},{7,24},{8,23},{9,... | collective-permute-start | bytes 122888 | tf_op jit(solution)/shard_map/ppermute | solution.py:575
  18.5 3.4 %shard_map.57 = (f32[10,2,72,128]{3,2,1,0:T(8,128)S(1)}, f32[8,2,80,128]{3,2,1,0:T(8,128)S(1)}, f32[16,2,72,128]{3,2,1,0:T(8,128)S(1)}) custom-call(s32[1]{0:T(128)} %bitcast.par, f32[52,16,200]{2,1,0:T(8,128)S(1)} %bitcast.6, f32[52,8,200]{2,1,0:T(8,128)S(1)} %bitcast.8, f32[304,128]{1,0:T(8,128)S(1)} %collective-permute-done.ewi, ...), custom_call_target="tpu_custom_call" | custom-call | flops 2264924160 | bytes 3672192 | tf_op jit(solution)/shard_map/pallas_call | solution.py:554
  21.9 0.0 collective-permute-done.3.corner
  21.9 3.5 %shard_map.59 = (f32[4,2,72,128]{3,2,1,0:T(8,128)S(1)}, f32[376,128]{1,0:T(8,128)S(1)}, f32[5,2,72,128]{3,2,1,0:T(8,128)S(1)}) custom-call(f32[16,2,72,128]{3,2,1,0:T(8,128)S(1)} %get-tuple-element.42.edge, f32[8,2,80,128]{3,2,1,0:T(8,128)S(1)} %get-tuple-element.43.se, f32[260,128]{1,0:T(8,128)S(1)} %collective-permute-done.2.main, ...), custom_call_target="tpu_custom_call" | custom-call | flops 2717908992 | bytes 7468960 | tf_op jit(solution)/shard_map/pallas_call | solution.py:554
  25.4 3.7 %collective-permute-start.4 = (f32[376,128]{1,0:T(8,128)S(1)}, f32[376,128]{1,0:T(8,128)S(1)}, u32[]{:S(2)}, u32[]{:S(2)}) collective-permute-start(f32[376,128]{1,0:T(8,128)S(1)} %get-tuple-element.53), channel_id=1, source_target_pairs={{0,31},{1,30},{2,29},{3,28},{4,27},{5,26},{6,25},{7,24},{8,23},{9,... | collective-permute-start | bytes 577544 | tf_op jit(solution)/shard_map/ppermute | solution.py:575
  29.1 6.8 %shard_map.60 = (f32[16,2,72,128]{3,2,1,0:T(8,128)S(1)}, f32[4,2,64,128]{3,2,1,0:T(8,128)S(1)}, f32[8,2,64,128]{3,2,1,0:T(8,128)S(1)}, f32[328,128]{1,0:T(8,128)S(1)}) custom-call(f32[5,2,72,128]{3,2,1,0:T(8,128)S(1)} %get-tuple-element.48.low, f32[10,2,72,128]{3,2,1,0:T(8,128)S(1)} %get-tuple-element.45.st1.st1a, ...), custom_call_target="tpu_custom_call" | custom-call | flops 5435817984 | bytes 6777984 | tf_op jit(solution)/shard_map/pallas_call | solution.py:554
  35.9 1.8 %collective-permute-start.7 = (f32[328,128]{1,0:T(8,128)S(1)}, f32[328,128]{1,0:T(8,128)S(1)}, u32[]{:S(2)}, u32[]{:S(2)}) collective-permute-start(f32[328,128]{1,0:T(8,128)S(1)} %get-tuple-element.67), channel_id=1, source_target_pairs={{0,31},{1,30},{2,29},{3,28},{4,27},{5,26},{6,25},{7,24},{8,23},{9,... | collective-permute-start | bytes 503816 | tf_op jit(solution)/shard_map/ppermute | solution.py:575
  37.7 1.5 %shard_map.61 = (f32[4,2,64,128]{3,2,1,0:T(8,128)S(1)}, f32[328,128]{1,0:T(8,128)S(1)}, f32[200,128]{1,0:T(8,128)S(1)}, f32[200,128]{1,0:T(8,128)S(1)}) custom-call(s32[1]{0:T(128)} %bitcast.par, f32[16,2,72,128]{3,2,1,0:T(8,128)S(1)} %get-tuple-element.52.st2, f32[376,128]{1,0:T(8,128)S(1)} %collective-permute-done.4.north, ...), custom_call_target="tpu_custom_call" | custom-call | flops 905969664 | bytes 4521888 | tf_op jit(solution)/shard_map/pallas_call | solution.py:554
  39.1 0.1 collective-permute-start.5
  39.2 3.7 %collective-permute-start.6 = (f32[200,128]{1,0:T(8,128)S(1)}, f32[200,128]{1,0:T(8,128)S(1)}, u32[]{:S(2)}, u32[]{:S(2)}) collective-permute-start(f32[200,128]{1,0:T(8,128)S(1)} %get-tuple-element.57), channel_id=1, source_target_pairs={{0,31},{1,2},{2,1},{3,4},{4,3},{5,6},{6,5},{7,8},{8,7},{9,10},{10,... | collective-permute-start | bytes 307208 | tf_op jit(solution)/shard_map/ppermute | solution.py:575
  42.9 1.7 %collective-permute-start.8 = (f32[328,128]{1,0:T(8,128)S(1)}, f32[328,128]{1,0:T(8,128)S(1)}, u32[]{:S(2)}, u32[]{:S(2)}) collective-permute-start(f32[328,128]{1,0:T(8,128)S(1)} %get-tuple-element.68), channel_id=1, source_target_pairs={{0,31},{1,30},{2,29},{3,28},{4,27},{5,26},{6,25},{7,24},{8,23},{9,... | collective-permute-start | bytes 503816 | tf_op jit(solution)/shard_map/ppermute | solution.py:575
  44.6 3.3 %shard_map.62 = (f32[8,64,256]{2,1,0:T(8,128)S(1)}, f32[8,64,256]{2,1,0:T(8,128)S(1)}) custom-call(f32[8,2,64,128]{3,2,1,0:T(8,128)S(1)} %get-tuple-element.54.st3l, f32[4,2,64,128]{3,2,1,0:T(8,128)S(1)} %get-tuple-element.55.st3m, f32[4,2,64,128]{3,2,1,0:T(8,128)S(1)} %get-tuple-element.58.st3b, f32[8,2,80,128]{3,2,1,0:T(8,128)S(1)} %get-tuple-element.43.se, ...), custom_call_target="tpu_custom_call" | custom-call | flops 2944401408 | bytes 4066432 | tf_op jit(solution)/shard_map/pallas_call | solution.py:554
  47.9 0.2 shard_map.64
  48.1 4.1 %collective-permute-start.9 = (f32[200,128]{1,0:T(8,128)S(1)}, f32[200,128]{1,0:T(8,128)S(1)}, u32[]{:S(2)}, u32[]{:S(2)}) collective-permute-start(f32[200,128]{1,0:T(8,128)S(1)} %shard_map.64), channel_id=1, source_target_pairs={{0,31},{1,30},{2,29},{3,28},{4,27},{5,26},{6,25},{7,24},{8,23},{9,... | collective-permute-start | bytes 307208 | tf_op jit(solution)/shard_map/ppermute | solution.py:575
  52.2 3.1 %shard_map.63 = (f32[52,16,200]{2,1,0:T(8,128)}, f32[16,64,256]{2,1,0:T(8,128)S(1)}) custom-call(s32[1]{0:T(128)} %bitcast.par, f32[8,64,256]{2,1,0:T(8,128)S(1)} %get-tuple-element.63.acc1, f32[8,64,256]{2,1,0:T(8,128)S(1)} %get-tuple-element.64.acc, f32[8,2,64,128]{3,2,1,0:T(8,128)S(1)} %get-tuple-element.54.st3l, ...), custom_call_target="tpu_custom_call" | custom-call | flops 905969664 | bytes 5653280 | tf_op jit(solution)/shard_map/pallas_call | solution.py:554
  55.4 0.6 collective-permute-done.9.nc
  55.9 1.1 %shard_map.65 = f32[52,16,200]{2,1,0:T(8,128)} custom-call(f32[52,16,200]{2,1,0:T(8,128)} %get-tuple-element.69.before, f32[16,64,256]{2,1,0:T(8,128)S(1)} %get-tuple-element.70.accn, f32[4,2,64,128]{3,2,1,0:T(8,128)S(1)} %get-tuple-element.55.st3m, f32[4,2,64,128]{3,2,1,0:T(8,128)S(1)} %get-tuple-element.58.st3b, ...), custom_call_target="tpu_custom_call", output_to_operand_aliasing={{}: (0, {})} | custom-call | flops 226492416 | bytes 4700960 | tf_op jit(solution)/shard_map/pallas_call | solution.py:554
  (15 shorter events, 0.0 us)
Async XLA Ops:
  1.4 10.8 %collective-permute-start = (f32[304,128]{1,0:T(8,128)S(1)}, f32[304,128]{1,0:T(8,128)S(1)}, u32[]{:S(2)}, u32[]{:S(2)}) collective-permute-start(f32[304,128]{1,0:T(8,128)S(1)} %get-tuple-element.38), channel_id=1, source_target_pairs={{0,1},{1,0},{2,3},{3,2},{4,5},{5,4},{6,7},{7,6},{8,9},{9,8},{10,11... | collective-permute-start | bytes 466952 | tf_op jit(solution)/shard_map/ppermute | solution.py:575
  2.0 10.8 %collective-permute-start.1 = (f32[304,128]{1,0:T(8,128)S(1)}, f32[304,128]{1,0:T(8,128)S(1)}, u32[]{:S(2)}, u32[]{:S(2)}) collective-permute-start(f32[304,128]{1,0:T(8,128)S(1)} %get-tuple-element.39), channel_id=1, source_target_pairs={{0,31},{1,2},{2,1},{3,4},{4,3},{5,6},{6,5},{7,8},{8,7},{9,10},{10,... | collective-permute-start | bytes 466952 | tf_op jit(solution)/shard_map/ppermute | solution.py:575
  8.6 10.0 %copy-start = (f32[16,52,200]{2,0,1:T(8,128)S(1)}, f32[16,52,200]{2,0,1:T(8,128)}, u32[]{:S(2)}) copy-start(f32[16,52,200]{2,0,1:T(8,128)} %param.5) | copy-start | bytes 1996804
  8.6 10.0 %copy-start.1 = (f32[8,52,200]{2,0,1:T(8,128)S(1)}, f32[8,52,200]{2,0,1:T(8,128)}, u32[]{:S(2)}) copy-start(f32[8,52,200]{2,0,1:T(8,128)} %param.6) | copy-start | bytes 998404
  8.6 10.0 %copy-start.3 = (f32[4,200]{1,0:T(4,128)S(1)}, f32[4,200]{1,0:T(4,128)}, u32[]{:S(2)}) copy-start(f32[4,200]{1,0:T(4,128)} %bias.9) | copy-start | bytes 9604
  8.6 13.3 %collective-permute-start.2 = (f32[260,128]{1,0:T(8,128)S(1)}, f32[260,128]{1,0:T(8,128)S(1)}, u32[]{:S(2)}, u32[]{:S(2)}) collective-permute-start(f32[260,128]{1,0:T(8,128)S(1)} %get-tuple-element.44), channel_id=1, source_target_pairs={{0,31},{1,30},{2,29},{3,28},{4,27},{5,26},{6,25},{7,24},{8,23},{9,... | collective-permute-start | bytes 399368 | tf_op jit(solution)/shard_map/ppermute | solution.py:575
  13.0 9.0 %collective-permute-start.3 = (f32[80,128]{1,0:T(8,128)S(1)}, f32[80,128]{1,0:T(8,128)S(1)}, u32[]{:S(2)}, u32[]{:S(2)}) collective-permute-start(f32[80,128]{1,0:T(8,128)S(1)} %shard_map.58), channel_id=1, source_target_pairs={{0,31},{1,30},{2,29},{3,28},{4,27},{5,26},{6,25},{7,24},{8,23},{9,... | collective-permute-start | bytes 122888 | tf_op jit(solution)/shard_map/ppermute | solution.py:575
  18.5 3.4 %copy-start.2 = (s32[200]{0:T(256)S(1)}, s32[200]{0:T(256)}, u32[]{:S(2)}) copy-start(s32[200]{0:T(256)} %param.7) | copy-start | bytes 2404
  25.4 12.3 %collective-permute-start.4 = (f32[376,128]{1,0:T(8,128)S(1)}, f32[376,128]{1,0:T(8,128)S(1)}, u32[]{:S(2)}, u32[]{:S(2)}) collective-permute-start(f32[376,128]{1,0:T(8,128)S(1)} %get-tuple-element.53), channel_id=1, source_target_pairs={{0,31},{1,30},{2,29},{3,28},{4,27},{5,26},{6,25},{7,24},{8,23},{9,... | collective-permute-start | bytes 577544 | tf_op jit(solution)/shard_map/ppermute | solution.py:575
  35.9 16.4 %collective-permute-start.7 = (f32[328,128]{1,0:T(8,128)S(1)}, f32[328,128]{1,0:T(8,128)S(1)}, u32[]{:S(2)}, u32[]{:S(2)}) collective-permute-start(f32[328,128]{1,0:T(8,128)S(1)} %get-tuple-element.67), channel_id=1, source_target_pairs={{0,31},{1,30},{2,29},{3,28},{4,27},{5,26},{6,25},{7,24},{8,23},{9,... | collective-permute-start | bytes 503816 | tf_op jit(solution)/shard_map/ppermute | solution.py:575
  39.1 8.8 %collective-permute-start.5 = (f32[200,128]{1,0:T(8,128)S(1)}, f32[200,128]{1,0:T(8,128)S(1)}, u32[]{:S(2)}, u32[]{:S(2)}) collective-permute-start(f32[200,128]{1,0:T(8,128)S(1)} %get-tuple-element.56), channel_id=1, source_target_pairs={{0,1},{1,0},{2,3},{3,2},{4,5},{5,4},{6,7},{7,6},{8,9},{9,8},{10,11... | collective-permute-start | bytes 307208 | tf_op jit(solution)/shard_map/ppermute | solution.py:575
  39.2 8.7 %collective-permute-start.6 = (f32[200,128]{1,0:T(8,128)S(1)}, f32[200,128]{1,0:T(8,128)S(1)}, u32[]{:S(2)}, u32[]{:S(2)}) collective-permute-start(f32[200,128]{1,0:T(8,128)S(1)} %get-tuple-element.57), channel_id=1, source_target_pairs={{0,31},{1,2},{2,1},{3,4},{4,3},{5,6},{6,5},{7,8},{8,7},{9,10},{10,... | collective-permute-start | bytes 307208 | tf_op jit(solution)/shard_map/ppermute | solution.py:575
  42.9 9.4 %collective-permute-start.8 = (f32[328,128]{1,0:T(8,128)S(1)}, f32[328,128]{1,0:T(8,128)S(1)}, u32[]{:S(2)}, u32[]{:S(2)}) collective-permute-start(f32[328,128]{1,0:T(8,128)S(1)} %get-tuple-element.68), channel_id=1, source_target_pairs={{0,31},{1,30},{2,29},{3,28},{4,27},{5,26},{6,25},{7,24},{8,23},{9,... | collective-permute-start | bytes 503816 | tf_op jit(solution)/shard_map/ppermute | solution.py:575
  48.1 7.8 %collective-permute-start.9 = (f32[200,128]{1,0:T(8,128)S(1)}, f32[200,128]{1,0:T(8,128)S(1)}, u32[]{:S(2)}, u32[]{:S(2)}) collective-permute-start(f32[200,128]{1,0:T(8,128)S(1)} %shard_map.64), channel_id=1, source_target_pairs={{0,31},{1,30},{2,29},{3,28},{4,27},{5,26},{6,25},{7,24},{8,23},{9,... | collective-permute-start | bytes 307208 | tf_op jit(solution)/shard_map/ppermute | solution.py:575

commit v6 on v5

--- a/solution.py
+++ b/solution.py
@@ -12,6 +12,7 @@
 LANES = 128
 HALF = 64
 MW = 64
+NW = 56
 HALO = 8
 
 
@@ -123,6 +124,30 @@
             lo[dst, :, at : at + LANES] = (x - h.astype(F32)).astype(BF16)
 
 
+def fill_pair(hi, lo, dst, sources, at):
+    place = slice(dst * NW, (dst + 2) * NW)
+    for b in range(3):
+        for t in range(2):
+            x = jnp.concatenate(
+                [ref[row, t, offs[b] : offs[b] + NW, :] for ref, row, offs in sources[at : at + 2]], axis=0
+            )
+            h = x.astype(BF16)
+            to = b * 2 * LANES + t * LANES
+            hi[place, to : to + LANES] = h
+            lo[place, to : to + LANES] = (x - h.astype(F32)).astype(BF16)
+
+
+def narrow(hi, lo, wh, wl, taps, row, chunk, dilate):
+    total = None
+    for a in taps:
+        at = slice((row + a * dilate) * NW, (row + a * dilate + chunk) * NW)
+        lh, ll = hi[at], lo[at]
+        for left, right in ((lh, wh), (ll, wh), (lh, wl)):
+            term = jnp.dot(left, right[a], preferred_element_type=F32)
+            total = term if total is None else total + term
+    return total
+
+
 def fill(hi, lo, dst, ref, src, count, offs):
     for i in range(count):
         fill_row(hi, lo, dst + i, ref, src + i, offs)
@@ -155,13 +180,13 @@
         emit(row, jax.nn.gelu(total + bias))
 
 
-def add_rows(out, out_row, res, res_row, off, chunk):
+def add_rows(out, out_row, res, res_row, off, chunk, width=MW):
     def emit(row, grown):
         for q in range(chunk):
             for t in range(2):
-                out[out_row + row + q, t, 0:MW, :] = (
-                    res[res_row + row + q, t, off : off + MW, :]
-                    + grown[q * MW : (q + 1) * MW, t * LANES : (t + 1) * LANES]
+                out[out_row + row + q, t, 0:width, :] = (
+                    res[res_row + row + q, t, off : off + width, :]
+                    + grown[q * width : (q + 1) * width, t * LANES : (t + 1) * LANES]
                 )
 
     return emit
@@ -376,13 +401,13 @@
     st2[12:16] = st2b[...]
     bias2 = bias_of(bias, 2)
     sources = run(se, south - 4, 4, (4, 8, 12)) + run(st2, 0, 16, (0, 4, 8))
-    for i in range(8, 20):
-        fill_row(h2, l2, i, *sources[i])
+    for i in range(8, 20, 2):
+        fill_pair(h2, l2, i, sources, i)
     for row in (8, 0, 4):
-        for i in range(8 if row == 0 else 0):
-            fill_row(h2, l2, i, *sources[i])
-        total = products(h2, l2, wh2, wl2, (0, 1, 2), row, 4, 4)
-        emit = add_rows(st3, -8, st2, 0, 4, 4) if row == 8 else add_rows(st3l, 0, st2, 0, 4, 4)
+        for i in range(0, 8 if row == 0 else 0, 2):
+            fill_pair(h2, l2, i, sources, i)
+        total = narrow(h2, l2, wh2, wl2, (0, 1, 2), row, 4, 4)
+        emit = add_rows(st3, -8, st2, 0, 4, 4, NW) if row == 8 else add_rows(st3l, 0, st2, 0, 4, 4, NW)
         emit(row, jax.nn.gelu(total + bias2))
         if row == 8:
             pack(lambda k, t: st3[3 - k, t, 0:cols, :], putter(out, cols), 4, cols, rem)
@@ -399,7 +424,10 @@
     wide = cols + 8
     north_rows(x2, 0, north, lanes_of(sign, 0), 4, wide, 0, rem)
     sources = run(st2, 8, 8, (0, 4, 8)) + run(x2, 0, 4, (0, 4, 8))
-    conv((hi, lo), wh, wl, bias_of(bias, 2), 4, sources, 4, 4, add_rows(st3b, 0, st2, 12, 4, 4))
+    for i in range(0, 12, 2):
+        fill_pair(hi, lo, i, sources, i)
+    total = narrow(hi, lo, wh, wl, (0, 1, 2), 0, 4, 4)
+    add_rows(st3b, 0, st2, 12, 4, 4, NW)(0, jax.nn.gelu(total + bias_of(bias, 2)))
     pack(lambda k, t: st3b[3 - k, t, 0:cols, :], putter(out, cols), 4, cols, rem)
     even = par[0] == 0
     parts = (st3l, st3m, st3b)
@@ -438,11 +466,11 @@
     for row in range(0, rows, 4):
         taps = (0, 1, 2) if row < low else (0, 1)
         while filled < row + 4 + 8 * taps[-1]:
-            fill_row(hi, lo, filled, x3, filled, (0, 8, 16))
-            filled += 1
-        total = products(hi, lo, wh, wl, taps, row, 4, 8)
+            fill_pair(hi, lo, filled, run(x3, filled, 2, (0, 8, 16)), 0)
+            filled += 2
+        total = narrow(hi, lo, wh, wl, taps, row, 4, 8)
         ref, at = (acc, row) if row < low else (top, row - low)
-        ref[at : at + 4] = (total + bias).reshape(4, MW, 2 * LANES)
+        ref[at : at + 4] = (total + bias).reshape(4, NW, 2 * LANES)
 
 
 def split_bf16(x):
@@ -475,16 +503,15 @@
     xn[:, :, HALO + cols : 2 * HALO + cols, :] = zero
     north_rows(xn, 0, nb, sign, 4, cols, HALO, rem)
     north_rows(xn, 4, na, sign, 4, cols, HALO, rem)
-    fill(hi, lo, 0, xn, 0, 8, (0, 8, 16))
+    for i in range(0, 8, 2):
+        fill_pair(hi, lo, i, run(xn, i, 2, (0, 8, 16)), 0)
     accn[0 : rows - 8] = acc1[...]
-    for i in range(2):
-        at = slice(4 * i, 4 * i + 4)
-        lh = hi[at].reshape(4 * MW, hi.shape[-1])
-        ll = lo[at].reshape(4 * MW, hi.shape[-1])
-        total = acc[4 * i : 4 * i + 4].reshape(4 * MW, 2 * LANES)
-        for left, right in ((lh, wh), (ll, wh), (lh, wl)):
+    for i in range(0, 8, 4):
+        at = slice(i * NW, (i + 4) * NW)
+        total = acc[i : i + 4].reshape(4 * NW, 2 * LANES)
+        for left, right in ((hi[at], wh), (lo[at], wh), (hi[at], wl)):
             total = total + jnp.dot(left, right[2], preferred_element_type=F32)
-        accn[rows - 8 + 4 * i : rows - 4 + 4 * i] = total.reshape(4, MW, 2 * LANES)
+        accn[rows - 8 + i : rows - 4 + i] = total.reshape(4, NW, 2 * LANES)
     for side, slot in enumerate(sided(par, ewi, ewc, rows, HALO, rem)):
         b, to = ((0, 0), (2, cols - HALO))[side]
         at = side * (HALO + cols)
@@ -547,6 +574,10 @@
     return [pltpu.VMEM((rows, MW, 6 * LANES), BF16)] * 2
 
 
+def flat(rows):
+    return [pltpu.VMEM((rows * NW, 6 * LANES), BF16)] * 2
+
+
 def call(kernel, outs, scratch, args, smem=0, flops=0, limit=16, hbm=(), alias=None):
     args = [pltpu.with_memory_space_constraint(a, pltpu.HBM) if i in hbm else a for i, a in enumerate(args)]
     moved = sum(a.size * a.dtype.itemsize for a in args[smem:])
@@ -622,8 +653,8 @@
     north = send(north, mirror)
     st2m, st3m, st3l, na = call(
         functools.partial(k_c1, cols=cols, rem=rem),
-        [state(rows, 72), state(4, MW), state(8, MW), (packed_rows(4, cols, rem), LANES)],
-        [pltpu.VMEM(state(rows - 1, 72), F32)] + lhs(8) + lhs(12) + lhs(rows + 4),
+        [state(rows, 72), state(4, NW), state(8, NW), (packed_rows(4, cols, rem), LANES)],
+        [pltpu.VMEM(state(rows - 1, 72), F32)] + lhs(8) + lhs(12) + flat(rows + 4),
         [low, st1, st2b, se, *split[2:6], biases],
         flops=24 * row_flops,
     )
@@ -631,8 +662,8 @@
     ew_rows = packed_rows(rows, HALO, rem)
     st3b, nb, ewi, ewc = call(
         functools.partial(k_d, cols=cols, rem=rem),
-        [state(4, MW), (packed_rows(4, cols, rem), LANES), (ew_rows, LANES), (ew_rows, LANES)],
-        [pltpu.VMEM(state(4, 72), F32)] + lhs(12),
+        [state(4, NW), (packed_rows(4, cols, rem), LANES), (ew_rows, LANES), (ew_rows, LANES)],
+        [pltpu.VMEM(state(4, 72), F32)] + flat(12),
         [par, st2m, north, st3l, st3m, sign, *split[4:6], biases],
         smem=1, flops=4 * row_flops,
     )
@@ -640,8 +671,8 @@
     nb = send(nb, mirror)
     acc, acc2 = call(
         functools.partial(k_f, cols=cols),
-        [(rows - 8, MW, 2 * LANES), (8, MW, 2 * LANES)],
-        [pltpu.VMEM(state(rows + south, 80), F32)] + lhs(rows + south),
+        [(rows - 8, NW, 2 * LANES), (8, NW, 2 * LANES)],
+        [pltpu.VMEM(state(rows + south, 80), F32)] + flat(rows + south),
         [st3l, st3m, st3b, se, *split[6:8], biases],
         flops=(rows - 3) * row_flops,
     )
@@ -653,9 +684,9 @@
     nc = send(nc, mirror)
     out, acc = call(
         functools.partial(k_g, cols=cols, rem=rem),
-        [(cols, rows, channels), (rows, MW, 2 * LANES)],
+        [(cols, rows, channels), (rows, NW, 2 * LANES)],
         [pltpu.VMEM(state(8, 80), F32), pltpu.VMEM((2, (rows + south + 8) * HALO, 2 * LANES), F32),
-         pltpu.VMEM((2,) + state(8, MW), F32)] + lhs(8),
+         pltpu.VMEM((2,) + state(8, NW), F32)] + flat(8),
         [par, acc, acc2, st3l, st3m, st3b, se, ewi, ewc, na, nb, sign, *split[6:8]],
         smem=1, flops=4 * row_flops,
     )

time: 57.3 us -> 57.2 us (level); the launches traced: 57.2 us -> 56.3 us
  Pallas kernels: 28 us -> 26.7 us
    pallas_call x11, Pallas kernels: 28 us -> 26.7 us  [call(): pl.pallas_call(kernel, out_shape=outs, in_specs=[SM if i < smem else HB i...]
  transfers between devices with their start and end apart: 10 -> 10, of which waited for: 2 -> 2; matrix products, arithmetic and copies ran while one was open for 0% -> 0% of each run, Pallas kernels for 38% -> 37%
where the time goes in v6:
time: 57.2 us; the launch traced here: 56.3 us
  starting transfers between devices  28.2 us (49%)
  Pallas kernels  26.7 us (47%)
  waiting for transfers between devices  1.16 us (2%)
    ppermute x10, starting transfers between devices, layers_of(): send = lambda x, route: lax.ppermute(x, 'lon', route)  28.2 us
    pallas_call x11, Pallas kernels, call(): pl.pallas_call(kernel, out_shape=outs, in_specs=[SM if i < smem else HB i...  26.7 us
    ppermute x10, waiting for transfers between devices, layers_of(): send = lambda x, route: lax.ppermute(x, 'lon', route)  1.16 us
  transfers between devices with their start and end apart: 10, of which 2 were waited for; matrix products, arithmetic and copies ran while one was open for 0% of the time, Pallas kernels for 37%

profile of v6, /device:TPU:0, one launch (start us, length us, event | category | flops | bytes accessed | tf_op | source)
XLA Modules:
  0.0 56.3 jit_solution(12286216479330377369)
XLA Ops:
  0.0 1.4 %shard_map.55 = (f32[260,128]{1,0:T(8,128)S(1)}, f32[304,128]{1,0:T(8,128)S(1)}, f32[304,128]{1,0:T(8,128)S(1)}) custom-call(s32[1]{0:T(128)} %bitcast.par, f32[52,16,200]{2,1,0:T(8,128)} %bitcast.5, f32[52,8,200]{2,1,0:T(8,128)} %bitcast.7), custom_call_target="tpu_custom_call" | custom-call | bytes 998400 | tf_op jit(solution)/shard_map/pallas_call | solution.py:585
  1.4 0.6 collective-permute-start
  2.0 6.6 %collective-permute-start.1 = (f32[304,128]{1,0:T(8,128)S(1)}, f32[304,128]{1,0:T(8,128)S(1)}, u32[]{:S(2)}, u32[]{:S(2)}) collective-permute-start(f32[304,128]{1,0:T(8,128)S(1)} %get-tuple-element.39), channel_id=1, source_target_pairs={{0,31},{1,2},{2,1},{3,4},{4,3},{5,6},{6,5},{7,8},{8,7},{9,10},{10,... | collective-permute-start | bytes 466952 | tf_op jit(solution)/shard_map/ppermute | solution.py:606
  8.6 0.1 collective-permute-start.2
  8.6 3.6 %shard_map.56 = (bf16[3,768,256]{2,1,0:T(8,128)(2,1)S(1)}, bf16[3,768,256]{2,1,0:T(8,128)(2,1)S(1)}, bf16[3,768,256]{2,1,0:T(8,128)(2,1)S(1)}, bf16[3,768,256]{2...) custom-call(f32[4,9,200,200]{3,2,1,0:T(8,128)} %w.1), custom_call_target="tpu_custom_call" | custom-call | bytes 5760000 | tf_op jit(solution)/shard_map/pallas_call | solution.py:585
  12.3 0.5 collective-permute-done.1.ewc
  12.8 0.2 shard_map.58
  13.0 5.6 %collective-permute-start.3 = (f32[80,128]{1,0:T(8,128)S(1)}, f32[80,128]{1,0:T(8,128)S(1)}, u32[]{:S(2)}, u32[]{:S(2)}) collective-permute-start(f32[80,128]{1,0:T(8,128)S(1)} %shard_map.58), channel_id=1, source_target_pairs={{0,31},{1,30},{2,29},{3,28},{4,27},{5,26},{6,25},{7,24},{8,23},{9,... | collective-permute-start | bytes 122888 | tf_op jit(solution)/shard_map/ppermute | solution.py:606
  18.5 3.4 %shard_map.57 = (f32[10,2,72,128]{3,2,1,0:T(8,128)S(1)}, f32[8,2,80,128]{3,2,1,0:T(8,128)S(1)}, f32[16,2,72,128]{3,2,1,0:T(8,128)S(1)}) custom-call(s32[1]{0:T(128)} %bitcast.par, f32[52,16,200]{2,1,0:T(8,128)S(1)} %bitcast.6, f32[52,8,200]{2,1,0:T(8,128)S(1)} %bitcast.8, f32[304,128]{1,0:T(8,128)S(1)} %collective-permute-done.ewi, ...), custom_call_target="tpu_custom_call" | custom-call | flops 2264924160 | bytes 3672192 | tf_op jit(solution)/shard_map/pallas_call | solution.py:585
  21.9 0.0 collective-permute-done.3.corner
  21.9 3.5 %shard_map.59 = (f32[4,2,72,128]{3,2,1,0:T(8,128)S(1)}, f32[376,128]{1,0:T(8,128)S(1)}, f32[5,2,72,128]{3,2,1,0:T(8,128)S(1)}) custom-call(f32[16,2,72,128]{3,2,1,0:T(8,128)S(1)} %get-tuple-element.42.edge, f32[8,2,80,128]{3,2,1,0:T(8,128)S(1)} %get-tuple-element.43.se, f32[260,128]{1,0:T(8,128)S(1)} %collective-permute-done.2.main, ...), custom_call_target="tpu_custom_call" | custom-call | flops 2717908992 | bytes 7468960 | tf_op jit(solution)/shard_map/pallas_call | solution.py:585
  25.4 3.7 %collective-permute-start.4 = (f32[376,128]{1,0:T(8,128)S(1)}, f32[376,128]{1,0:T(8,128)S(1)}, u32[]{:S(2)}, u32[]{:S(2)}) collective-permute-start(f32[376,128]{1,0:T(8,128)S(1)} %get-tuple-element.53), channel_id=1, source_target_pairs={{0,31},{1,30},{2,29},{3,28},{4,27},{5,26},{6,25},{7,24},{8,23},{9,... | collective-permute-start | bytes 577544 | tf_op jit(solution)/shard_map/ppermute | solution.py:606
  29.1 6.3 %shard_map.60 = (f32[16,2,72,128]{3,2,1,0:T(8,128)S(1)}, f32[4,2,56,128]{3,2,1,0:T(8,128)S(1)}, f32[8,2,56,128]{3,2,1,0:T(8,128)S(1)}, f32[328,128]{1,0:T(8,128)S(1)}) custom-call(f32[5,2,72,128]{3,2,1,0:T(8,128)S(1)} %get-tuple-element.48.low, f32[10,2,72,128]{3,2,1,0:T(8,128)S(1)} %get-tuple-element.45.st1.st1a, ...), custom_call_target="tpu_custom_call" | custom-call | flops 5435817984 | bytes 6777984 | tf_op jit(solution)/shard_map/pallas_call | solution.py:585
  35.4 1.8 %collective-permute-start.7 = (f32[328,128]{1,0:T(8,128)S(1)}, f32[328,128]{1,0:T(8,128)S(1)}, u32[]{:S(2)}, u32[]{:S(2)}) collective-permute-start(f32[328,128]{1,0:T(8,128)S(1)} %get-tuple-element.67), channel_id=1, source_target_pairs={{0,31},{1,30},{2,29},{3,28},{4,27},{5,26},{6,25},{7,24},{8,23},{9,... | collective-permute-start | bytes 503816 | tf_op jit(solution)/shard_map/ppermute | solution.py:606
  37.2 1.4 %shard_map.61 = (f32[4,2,56,128]{3,2,1,0:T(8,128)S(1)}, f32[328,128]{1,0:T(8,128)S(1)}, f32[200,128]{1,0:T(8,128)S(1)}, f32[200,128]{1,0:T(8,128)S(1)}) custom-call(s32[1]{0:T(128)} %bitcast.par, f32[16,2,72,128]{3,2,1,0:T(8,128)S(1)} %get-tuple-element.52.st2, f32[376,128]{1,0:T(8,128)S(1)} %collective-permute-done.4.north, ...), custom_call_target="tpu_custom_call" | custom-call | flops 905969664 | bytes 4423584 | tf_op jit(solution)/shard_map/pallas_call | solution.py:585
  38.6 0.0 collective-permute-start.5
  38.6 3.7 %collective-permute-start.6 = (f32[200,128]{1,0:T(8,128)S(1)}, f32[200,128]{1,0:T(8,128)S(1)}, u32[]{:S(2)}, u32[]{:S(2)}) collective-permute-start(f32[200,128]{1,0:T(8,128)S(1)} %get-tuple-element.57), channel_id=1, source_target_pairs={{0,31},{1,2},{2,1},{3,4},{4,3},{5,6},{6,5},{7,8},{8,7},{9,10},{10,... | collective-permute-start | bytes 307208 | tf_op jit(solution)/shard_map/ppermute | solution.py:606
  42.3 1.7 %collective-permute-start.8 = (f32[328,128]{1,0:T(8,128)S(1)}, f32[328,128]{1,0:T(8,128)S(1)}, u32[]{:S(2)}, u32[]{:S(2)}) collective-permute-start(f32[328,128]{1,0:T(8,128)S(1)} %get-tuple-element.68), channel_id=1, source_target_pairs={{0,31},{1,30},{2,29},{3,28},{4,27},{5,26},{6,25},{7,24},{8,23},{9,... | collective-permute-start | bytes 503816 | tf_op jit(solution)/shard_map/ppermute | solution.py:606
  44.1 2.9 %shard_map.62 = (f32[8,56,256]{2,1,0:T(8,128)S(1)}, f32[8,56,256]{2,1,0:T(8,128)S(1)}) custom-call(f32[8,2,56,128]{3,2,1,0:T(8,128)S(1)} %get-tuple-element.54.st3l, f32[4,2,56,128]{3,2,1,0:T(8,128)S(1)} %get-tuple-element.55.st3m, f32[4,2,56,128]{3,2,1,0:T(8,128)S(1)} %get-tuple-element.58.st3b, f32[8,2,80,128]{3,2,1,0:T(8,128)S(1)} %get-tuple-element.43.se, ...), custom_call_target="tpu_custom_call" | custom-call | flops 2944401408 | bytes 3935360 | tf_op jit(solution)/shard_map/pallas_call | solution.py:585
  47.0 0.2 shard_map.64
  47.2 4.5 %collective-permute-start.9 = (f32[200,128]{1,0:T(8,128)S(1)}, f32[200,128]{1,0:T(8,128)S(1)}, u32[]{:S(2)}, u32[]{:S(2)}) collective-permute-start(f32[200,128]{1,0:T(8,128)S(1)} %shard_map.64), channel_id=1, source_target_pairs={{0,31},{1,30},{2,29},{3,28},{4,27},{5,26},{6,25},{7,24},{8,23},{9,... | collective-permute-start | bytes 307208 | tf_op jit(solution)/shard_map/ppermute | solution.py:606
  51.7 2.7 %shard_map.63 = (f32[52,16,200]{2,1,0:T(8,128)}, f32[16,56,256]{2,1,0:T(8,128)S(1)}) custom-call(s32[1]{0:T(128)} %bitcast.par, f32[8,56,256]{2,1,0:T(8,128)S(1)} %get-tuple-element.63.acc1, f32[8,56,256]{2,1,0:T(8,128)S(1)} %get-tuple-element.64.acc, f32[8,2,56,128]{3,2,1,0:T(8,128)S(1)} %get-tuple-element.54.st3l, ...), custom_call_target="tpu_custom_call" | custom-call | flops 905969664 | bytes 5391136 | tf_op jit(solution)/shard_map/pallas_call | solution.py:585
  54.4 0.6 %collective-permute-done.9.nc = f32[200,128]{1,0:T(8,128)S(1)} collective-permute-done((f32[200,128]{1,0:T(8,128)S(1)}, f32[200,128]{1,0:T(8,128)S(1)}, u32[]{:S(2)}, u32[]{:S(2)}) %collective-permute-start.9) | collective-permute-done | bytes 102432 | tf_op jit(solution)/shard_map/ppermute | solution.py:606
  55.0 1.1 %shard_map.65 = f32[52,16,200]{2,1,0:T(8,128)} custom-call(f32[52,16,200]{2,1,0:T(8,128)} %get-tuple-element.69.before, f32[16,56,256]{2,1,0:T(8,128)S(1)} %get-tuple-element.70.accn, f32[4,2,56,128]{3,2,1,0:T(8,128)S(1)} %get-tuple-element.55.st3m, f32[4,2,56,128]{3,2,1,0:T(8,128)S(1)} %get-tuple-element.58.st3b, ...), custom_call_target="tpu_custom_call", output_to_operand_aliasing={{}: (0, {})} | custom-call | flops 226492416 | bytes 4504352 | tf_op jit(solution)/shard_map/pallas_call | solution.py:585
  (15 shorter events, 0.0 us)
Async XLA Ops:
  1.4 10.8 %collective-permute-start = (f32[304,128]{1,0:T(8,128)S(1)}, f32[304,128]{1,0:T(8,128)S(1)}, u32[]{:S(2)}, u32[]{:S(2)}) collective-permute-start(f32[304,128]{1,0:T(8,128)S(1)} %get-tuple-element.38), channel_id=1, source_target_pairs={{0,1},{1,0},{2,3},{3,2},{4,5},{5,4},{6,7},{7,6},{8,9},{9,8},{10,11... | collective-permute-start | bytes 466952 | tf_op jit(solution)/shard_map/ppermute | solution.py:606
  2.0 10.8 %collective-permute-start.1 = (f32[304,128]{1,0:T(8,128)S(1)}, f32[304,128]{1,0:T(8,128)S(1)}, u32[]{:S(2)}, u32[]{:S(2)}) collective-permute-start(f32[304,128]{1,0:T(8,128)S(1)} %get-tuple-element.39), channel_id=1, source_target_pairs={{0,31},{1,2},{2,1},{3,4},{4,3},{5,6},{6,5},{7,8},{8,7},{9,10},{10,... | collective-permute-start | bytes 466952 | tf_op jit(solution)/shard_map/ppermute | solution.py:606
  8.6 10.0 %copy-start = (f32[16,52,200]{2,0,1:T(8,128)S(1)}, f32[16,52,200]{2,0,1:T(8,128)}, u32[]{:S(2)}) copy-start(f32[16,52,200]{2,0,1:T(8,128)} %param.5) | copy-start | bytes 1996804
  8.6 10.0 %copy-start.1 = (f32[8,52,200]{2,0,1:T(8,128)S(1)}, f32[8,52,200]{2,0,1:T(8,128)}, u32[]{:S(2)}) copy-start(f32[8,52,200]{2,0,1:T(8,128)} %param.6) | copy-start | bytes 998404
  8.6 10.0 %copy-start.3 = (f32[4,200]{1,0:T(4,128)S(1)}, f32[4,200]{1,0:T(4,128)}, u32[]{:S(2)}) copy-start(f32[4,200]{1,0:T(4,128)} %bias.9) | copy-start | bytes 9604
  8.6 13.3 %collective-permute-start.2 = (f32[260,128]{1,0:T(8,128)S(1)}, f32[260,128]{1,0:T(8,128)S(1)}, u32[]{:S(2)}, u32[]{:S(2)}) collective-permute-start(f32[260,128]{1,0:T(8,128)S(1)} %get-tuple-element.44), channel_id=1, source_target_pairs={{0,31},{1,30},{2,29},{3,28},{4,27},{5,26},{6,25},{7,24},{8,23},{9,... | collective-permute-start | bytes 399368 | tf_op jit(solution)/shard_map/ppermute | solution.py:606
  13.0 9.0 %collective-permute-start.3 = (f32[80,128]{1,0:T(8,128)S(1)}, f32[80,128]{1,0:T(8,128)S(1)}, u32[]{:S(2)}, u32[]{:S(2)}) collective-permute-start(f32[80,128]{1,0:T(8,128)S(1)} %shard_map.58), channel_id=1, source_target_pairs={{0,31},{1,30},{2,29},{3,28},{4,27},{5,26},{6,25},{7,24},{8,23},{9,... | collective-permute-start | bytes 122888 | tf_op jit(solution)/shard_map/ppermute | solution.py:606
  18.5 3.4 %copy-start.2 = (s32[200]{0:T(256)S(1)}, s32[200]{0:T(256)}, u32[]{:S(2)}) copy-start(s32[200]{0:T(256)} %param.7) | copy-start | bytes 2404
  25.4 11.8 %collective-permute-start.4 = (f32[376,128]{1,0:T(8,128)S(1)}, f32[376,128]{1,0:T(8,128)S(1)}, u32[]{:S(2)}, u32[]{:S(2)}) collective-permute-start(f32[376,128]{1,0:T(8,128)S(1)} %get-tuple-element.53), channel_id=1, source_target_pairs={{0,31},{1,30},{2,29},{3,28},{4,27},{5,26},{6,25},{7,24},{8,23},{9,... | collective-permute-start | bytes 577544 | tf_op jit(solution)/shard_map/ppermute | solution.py:606
  35.4 16.3 %collective-permute-start.7 = (f32[328,128]{1,0:T(8,128)S(1)}, f32[328,128]{1,0:T(8,128)S(1)}, u32[]{:S(2)}, u32[]{:S(2)}) collective-permute-start(f32[328,128]{1,0:T(8,128)S(1)} %get-tuple-element.67), channel_id=1, source_target_pairs={{0,31},{1,30},{2,29},{3,28},{4,27},{5,26},{6,25},{7,24},{8,23},{9,... | collective-permute-start | bytes 503816 | tf_op jit(solution)/shard_map/ppermute | solution.py:606
  38.6 8.4 %collective-permute-start.5 = (f32[200,128]{1,0:T(8,128)S(1)}, f32[200,128]{1,0:T(8,128)S(1)}, u32[]{:S(2)}, u32[]{:S(2)}) collective-permute-start(f32[200,128]{1,0:T(8,128)S(1)} %get-tuple-element.56), channel_id=1, source_target_pairs={{0,1},{1,0},{2,3},{3,2},{4,5},{5,4},{6,7},{7,6},{8,9},{9,8},{10,11... | collective-permute-start | bytes 307208 | tf_op jit(solution)/shard_map/ppermute | solution.py:606
  38.6 8.3 %collective-permute-start.6 = (f32[200,128]{1,0:T(8,128)S(1)}, f32[200,128]{1,0:T(8,128)S(1)}, u32[]{:S(2)}, u32[]{:S(2)}) collective-permute-start(f32[200,128]{1,0:T(8,128)S(1)} %get-tuple-element.57), channel_id=1, source_target_pairs={{0,31},{1,2},{2,1},{3,4},{4,3},{5,6},{6,5},{7,8},{8,7},{9,10},{10,... | collective-permute-start | bytes 307208 | tf_op jit(solution)/shard_map/ppermute | solution.py:606
  42.3 9.4 %collective-permute-start.8 = (f32[328,128]{1,0:T(8,128)S(1)}, f32[328,128]{1,0:T(8,128)S(1)}, u32[]{:S(2)}, u32[]{:S(2)}) collective-permute-start(f32[328,128]{1,0:T(8,128)S(1)} %get-tuple-element.68), channel_id=1, source_target_pairs={{0,31},{1,30},{2,29},{3,28},{4,27},{5,26},{6,25},{7,24},{8,23},{9,... | collective-permute-start | bytes 503816 | tf_op jit(solution)/shard_map/ppermute | solution.py:606
  47.2 7.8 %collective-permute-start.9 = (f32[200,128]{1,0:T(8,128)S(1)}, f32[200,128]{1,0:T(8,128)S(1)}, u32[]{:S(2)}, u32[]{:S(2)}) collective-permute-start(f32[200,128]{1,0:T(8,128)S(1)} %shard_map.64), channel_id=1, source_target_pairs={{0,31},{1,30},{2,29},{3,28},{4,27},{5,26},{6,25},{7,24},{8,23},{9,... | collective-permute-start | bytes 307208 | tf_op jit(solution)/shard_map/ppermute | solution.py:606

commit v7 on v6

--- a/solution.py
+++ b/solution.py
@@ -542,8 +542,9 @@
     rows = accn.shape[0]
     channels = out.shape[-1]
     slot = turned(slots_of(nc, 8, 2 * HALO, rem)).__getitem__
+    sign = lanes_of(sign, 0)
     for k in range(8):
-        tiles = signed(unpack(slot, k, 8, 2 * HALO, rem), lanes_of(sign, 0))
+        tiles = signed(unpack(slot, k, 8, 2 * HALO, rem), sign)
         for t in range(2):
             for side in range(2):
                 xc[side, k * HALO : (k + 1) * HALO, t * LANES : (t + 1) * LANES] = tiles[t][side * HALO : (side + 1) * HALO]
@@ -623,7 +624,9 @@
          pltpu.SemaphoreType.DMA((5,))],
         [par, field, south_rows], smem=1, hbm=(1, 2), limit=16,
     )
-    ewi, ewc, main = send(ewi, intra), send(ewc, cross), send(main, mirror)
+    ewc = send(ewc, cross)
+    ewi = send(ewi, intra)
+    main = send(main, mirror)
     split = call(
         k_weights,
         [jax.ShapeDtypeStruct((3, 6 * LANES, 2 * LANES), BF16)] * (2 * layers),

time: 57.2 us -> 57.2 us (level)
  no operation moved by 1% of the time
where the time goes in v7:
time: 57.2 us; the launch traced here: 56.3 us
  starting transfers between devices  28.2 us (49%)
  Pallas kernels  26.7 us (47%)
  waiting for transfers between devices  1.16 us (2%)
    ppermute x10, starting transfers between devices, layers_of(): send = lambda x, route: lax.ppermute(x, 'lon', route)  28.2 us
    pallas_call x11, Pallas kernels, call(): pl.pallas_call(kernel, out_shape=outs, in_specs=[SM if i < smem else HB i...  26.7 us
    ppermute x10, waiting for transfers between devices, layers_of(): send = lambda x, route: lax.ppermute(x, 'lon', route)  1.16 us
  transfers between devices with their start and end apart: 10, of which 2 were waited for; matrix products, arithmetic and copies ran while one was open for 0% of the time, Pallas kernels for 37%

profile of v7, /device:TPU:0, one launch (start us, length us, event | category | flops | bytes accessed | tf_op | source)
XLA Modules:
  0.0 56.3 jit_solution(12286216479330377369)
XLA Ops:
  0.0 1.4 %shard_map.55 = (f32[260,128]{1,0:T(8,128)S(1)}, f32[304,128]{1,0:T(8,128)S(1)}, f32[304,128]{1,0:T(8,128)S(1)}) custom-call(s32[1]{0:T(128)} %bitcast.par, f32[52,16,200]{2,1,0:T(8,128)} %bitcast.5, f32[52,8,200]{2,1,0:T(8,128)} %bitcast.7), custom_call_target="tpu_custom_call" | custom-call | bytes 998400 | tf_op jit(solution)/shard_map/pallas_call | solution.py:586
  1.4 0.6 collective-permute-start
  2.0 6.6 %collective-permute-start.1 = (f32[304,128]{1,0:T(8,128)S(1)}, f32[304,128]{1,0:T(8,128)S(1)}, u32[]{:S(2)}, u32[]{:S(2)}) collective-permute-start(f32[304,128]{1,0:T(8,128)S(1)} %get-tuple-element.39), channel_id=1, source_target_pairs={{0,31},{1,2},{2,1},{3,4},{4,3},{5,6},{6,5},{7,8},{8,7},{9,10},{10,... | collective-permute-start | bytes 466952 | tf_op jit(solution)/shard_map/ppermute | solution.py:607
  8.6 0.1 collective-permute-start.2
  8.6 3.6 %shard_map.56 = (bf16[3,768,256]{2,1,0:T(8,128)(2,1)S(1)}, bf16[3,768,256]{2,1,0:T(8,128)(2,1)S(1)}, bf16[3,768,256]{2,1,0:T(8,128)(2,1)S(1)}, bf16[3,768,256]{2...) custom-call(f32[4,9,200,200]{3,2,1,0:T(8,128)} %w.1), custom_call_target="tpu_custom_call" | custom-call | bytes 5760000 | tf_op jit(solution)/shard_map/pallas_call | solution.py:586
  12.3 0.5 collective-permute-done.1.ewc
  12.8 0.2 shard_map.58
  13.0 5.6 %collective-permute-start.3 = (f32[80,128]{1,0:T(8,128)S(1)}, f32[80,128]{1,0:T(8,128)S(1)}, u32[]{:S(2)}, u32[]{:S(2)}) collective-permute-start(f32[80,128]{1,0:T(8,128)S(1)} %shard_map.58), channel_id=1, source_target_pairs={{0,31},{1,30},{2,29},{3,28},{4,27},{5,26},{6,25},{7,24},{8,23},{9,... | collective-permute-start | bytes 122888 | tf_op jit(solution)/shard_map/ppermute | solution.py:607
  18.5 3.4 %shard_map.57 = (f32[10,2,72,128]{3,2,1,0:T(8,128)S(1)}, f32[8,2,80,128]{3,2,1,0:T(8,128)S(1)}, f32[16,2,72,128]{3,2,1,0:T(8,128)S(1)}) custom-call(s32[1]{0:T(128)} %bitcast.par, f32[52,16,200]{2,1,0:T(8,128)S(1)} %bitcast.6, f32[52,8,200]{2,1,0:T(8,128)S(1)} %bitcast.8, f32[304,128]{1,0:T(8,128)S(1)} %collective-permute-done.ewi, ...), custom_call_target="tpu_custom_call" | custom-call | flops 2264924160 | bytes 3672192 | tf_op jit(solution)/shard_map/pallas_call | solution.py:586
  21.9 0.0 collective-permute-done.3.corner
  21.9 3.5 %shard_map.59 = (f32[4,2,72,128]{3,2,1,0:T(8,128)S(1)}, f32[376,128]{1,0:T(8,128)S(1)}, f32[5,2,72,128]{3,2,1,0:T(8,128)S(1)}) custom-call(f32[16,2,72,128]{3,2,1,0:T(8,128)S(1)} %get-tuple-element.42.edge, f32[8,2,80,128]{3,2,1,0:T(8,128)S(1)} %get-tuple-element.43.se, f32[260,128]{1,0:T(8,128)S(1)} %collective-permute-done.2.main, ...), custom_call_target="tpu_custom_call" | custom-call | flops 2717908992 | bytes 7468960 | tf_op jit(solution)/shard_map/pallas_call | solution.py:586
  25.4 3.7 %collective-permute-start.4 = (f32[376,128]{1,0:T(8,128)S(1)}, f32[376,128]{1,0:T(8,128)S(1)}, u32[]{:S(2)}, u32[]{:S(2)}) collective-permute-start(f32[376,128]{1,0:T(8,128)S(1)} %get-tuple-element.53), channel_id=1, source_target_pairs={{0,31},{1,30},{2,29},{3,28},{4,27},{5,26},{6,25},{7,24},{8,23},{9,... | collective-permute-start | bytes 577544 | tf_op jit(solution)/shard_map/ppermute | solution.py:607
  29.1 6.3 %shard_map.60 = (f32[16,2,72,128]{3,2,1,0:T(8,128)S(1)}, f32[4,2,56,128]{3,2,1,0:T(8,128)S(1)}, f32[8,2,56,128]{3,2,1,0:T(8,128)S(1)}, f32[328,128]{1,0:T(8,128)S(1)}) custom-call(f32[5,2,72,128]{3,2,1,0:T(8,128)S(1)} %get-tuple-element.48.low, f32[10,2,72,128]{3,2,1,0:T(8,128)S(1)} %get-tuple-element.45.st1.st1a, ...), custom_call_target="tpu_custom_call" | custom-call | flops 5435817984 | bytes 6777984 | tf_op jit(solution)/shard_map/pallas_call | solution.py:586
  35.4 1.8 %collective-permute-start.7 = (f32[328,128]{1,0:T(8,128)S(1)}, f32[328,128]{1,0:T(8,128)S(1)}, u32[]{:S(2)}, u32[]{:S(2)}) collective-permute-start(f32[328,128]{1,0:T(8,128)S(1)} %get-tuple-element.67), channel_id=1, source_target_pairs={{0,31},{1,30},{2,29},{3,28},{4,27},{5,26},{6,25},{7,24},{8,23},{9,... | collective-permute-start | bytes 503816 | tf_op jit(solution)/shard_map/ppermute | solution.py:607
  37.2 1.4 %shard_map.61 = (f32[4,2,56,128]{3,2,1,0:T(8,128)S(1)}, f32[328,128]{1,0:T(8,128)S(1)}, f32[200,128]{1,0:T(8,128)S(1)}, f32[200,128]{1,0:T(8,128)S(1)}) custom-call(s32[1]{0:T(128)} %bitcast.par, f32[16,2,72,128]{3,2,1,0:T(8,128)S(1)} %get-tuple-element.52.st2, f32[376,128]{1,0:T(8,128)S(1)} %collective-permute-done.4.north, ...), custom_call_target="tpu_custom_call" | custom-call | flops 905969664 | bytes 4423584 | tf_op jit(solution)/shard_map/pallas_call | solution.py:586
  38.6 0.0 collective-permute-start.5
  38.6 3.7 %collective-permute-start.6 = (f32[200,128]{1,0:T(8,128)S(1)}, f32[200,128]{1,0:T(8,128)S(1)}, u32[]{:S(2)}, u32[]{:S(2)}) collective-permute-start(f32[200,128]{1,0:T(8,128)S(1)} %get-tuple-element.57), channel_id=1, source_target_pairs={{0,31},{1,2},{2,1},{3,4},{4,3},{5,6},{6,5},{7,8},{8,7},{9,10},{10,... | collective-permute-start | bytes 307208 | tf_op jit(solution)/shard_map/ppermute | solution.py:607
  42.3 1.7 %collective-permute-start.8 = (f32[328,128]{1,0:T(8,128)S(1)}, f32[328,128]{1,0:T(8,128)S(1)}, u32[]{:S(2)}, u32[]{:S(2)}) collective-permute-start(f32[328,128]{1,0:T(8,128)S(1)} %get-tuple-element.68), channel_id=1, source_target_pairs={{0,31},{1,30},{2,29},{3,28},{4,27},{5,26},{6,25},{7,24},{8,23},{9,... | collective-permute-start | bytes 503816 | tf_op jit(solution)/shard_map/ppermute | solution.py:607
  44.1 2.9 %shard_map.62 = (f32[8,56,256]{2,1,0:T(8,128)S(1)}, f32[8,56,256]{2,1,0:T(8,128)S(1)}) custom-call(f32[8,2,56,128]{3,2,1,0:T(8,128)S(1)} %get-tuple-element.54.st3l, f32[4,2,56,128]{3,2,1,0:T(8,128)S(1)} %get-tuple-element.55.st3m, f32[4,2,56,128]{3,2,1,0:T(8,128)S(1)} %get-tuple-element.58.st3b, f32[8,2,80,128]{3,2,1,0:T(8,128)S(1)} %get-tuple-element.43.se, ...), custom_call_target="tpu_custom_call" | custom-call | flops 2944401408 | bytes 3935360 | tf_op jit(solution)/shard_map/pallas_call | solution.py:586
  47.0 0.2 shard_map.64
  47.2 4.5 %collective-permute-start.9 = (f32[200,128]{1,0:T(8,128)S(1)}, f32[200,128]{1,0:T(8,128)S(1)}, u32[]{:S(2)}, u32[]{:S(2)}) collective-permute-start(f32[200,128]{1,0:T(8,128)S(1)} %shard_map.64), channel_id=1, source_target_pairs={{0,31},{1,30},{2,29},{3,28},{4,27},{5,26},{6,25},{7,24},{8,23},{9,... | collective-permute-start | bytes 307208 | tf_op jit(solution)/shard_map/ppermute | solution.py:607
  51.7 2.7 %shard_map.63 = (f32[52,16,200]{2,1,0:T(8,128)}, f32[16,56,256]{2,1,0:T(8,128)S(1)}) custom-call(s32[1]{0:T(128)} %bitcast.par, f32[8,56,256]{2,1,0:T(8,128)S(1)} %get-tuple-element.63.acc1, f32[8,56,256]{2,1,0:T(8,128)S(1)} %get-tuple-element.64.acc, f32[8,2,56,128]{3,2,1,0:T(8,128)S(1)} %get-tuple-element.54.st3l, ...), custom_call_target="tpu_custom_call" | custom-call | flops 905969664 | bytes 5391136 | tf_op jit(solution)/shard_map/pallas_call | solution.py:586
  54.4 0.6 %collective-permute-done.9.nc = f32[200,128]{1,0:T(8,128)S(1)} collective-permute-done((f32[200,128]{1,0:T(8,128)S(1)}, f32[200,128]{1,0:T(8,128)S(1)}, u32[]{:S(2)}, u32[]{:S(2)}) %collective-permute-start.9) | collective-permute-done | bytes 102432 | tf_op jit(solution)/shard_map/ppermute | solution.py:607
  55.0 1.1 %shard_map.65 = f32[52,16,200]{2,1,0:T(8,128)} custom-call(f32[52,16,200]{2,1,0:T(8,128)} %get-tuple-element.69.before, f32[16,56,256]{2,1,0:T(8,128)S(1)} %get-tuple-element.70.accn, f32[4,2,56,128]{3,2,1,0:T(8,128)S(1)} %get-tuple-element.55.st3m, f32[4,2,56,128]{3,2,1,0:T(8,128)S(1)} %get-tuple-element.58.st3b, ...), custom_call_target="tpu_custom_call", output_to_operand_aliasing={{}: (0, {})} | custom-call | flops 226492416 | bytes 4504352 | tf_op jit(solution)/shard_map/pallas_call | solution.py:586
  (15 shorter events, 0.0 us)
Async XLA Ops:
  1.4 10.8 %collective-permute-start = (f32[304,128]{1,0:T(8,128)S(1)}, f32[304,128]{1,0:T(8,128)S(1)}, u32[]{:S(2)}, u32[]{:S(2)}) collective-permute-start(f32[304,128]{1,0:T(8,128)S(1)} %get-tuple-element.38), channel_id=1, source_target_pairs={{0,1},{1,0},{2,3},{3,2},{4,5},{5,4},{6,7},{7,6},{8,9},{9,8},{10,11... | collective-permute-start | bytes 466952 | tf_op jit(solution)/shard_map/ppermute | solution.py:607
  2.0 10.8 %collective-permute-start.1 = (f32[304,128]{1,0:T(8,128)S(1)}, f32[304,128]{1,0:T(8,128)S(1)}, u32[]{:S(2)}, u32[]{:S(2)}) collective-permute-start(f32[304,128]{1,0:T(8,128)S(1)} %get-tuple-element.39), channel_id=1, source_target_pairs={{0,31},{1,2},{2,1},{3,4},{4,3},{5,6},{6,5},{7,8},{8,7},{9,10},{10,... | collective-permute-start | bytes 466952 | tf_op jit(solution)/shard_map/ppermute | solution.py:607
  8.6 10.0 %copy-start = (f32[16,52,200]{2,0,1:T(8,128)S(1)}, f32[16,52,200]{2,0,1:T(8,128)}, u32[]{:S(2)}) copy-start(f32[16,52,200]{2,0,1:T(8,128)} %param.5) | copy-start | bytes 1996804
  8.6 10.0 %copy-start.1 = (f32[8,52,200]{2,0,1:T(8,128)S(1)}, f32[8,52,200]{2,0,1:T(8,128)}, u32[]{:S(2)}) copy-start(f32[8,52,200]{2,0,1:T(8,128)} %param.6) | copy-start | bytes 998404
  8.6 10.0 %copy-start.3 = (f32[4,200]{1,0:T(4,128)S(1)}, f32[4,200]{1,0:T(4,128)}, u32[]{:S(2)}) copy-start(f32[4,200]{1,0:T(4,128)} %bias.9) | copy-start | bytes 9604
  8.6 13.3 %collective-permute-start.2 = (f32[260,128]{1,0:T(8,128)S(1)}, f32[260,128]{1,0:T(8,128)S(1)}, u32[]{:S(2)}, u32[]{:S(2)}) collective-permute-start(f32[260,128]{1,0:T(8,128)S(1)} %get-tuple-element.44), channel_id=1, source_target_pairs={{0,31},{1,30},{2,29},{3,28},{4,27},{5,26},{6,25},{7,24},{8,23},{9,... | collective-permute-start | bytes 399368 | tf_op jit(solution)/shard_map/ppermute | solution.py:607
  13.0 9.0 %collective-permute-start.3 = (f32[80,128]{1,0:T(8,128)S(1)}, f32[80,128]{1,0:T(8,128)S(1)}, u32[]{:S(2)}, u32[]{:S(2)}) collective-permute-start(f32[80,128]{1,0:T(8,128)S(1)} %shard_map.58), channel_id=1, source_target_pairs={{0,31},{1,30},{2,29},{3,28},{4,27},{5,26},{6,25},{7,24},{8,23},{9,... | collective-permute-start | bytes 122888 | tf_op jit(solution)/shard_map/ppermute | solution.py:607
  18.5 3.4 %copy-start.2 = (s32[200]{0:T(256)S(1)}, s32[200]{0:T(256)}, u32[]{:S(2)}) copy-start(s32[200]{0:T(256)} %param.7) | copy-start | bytes 2404
  25.4 11.8 %collective-permute-start.4 = (f32[376,128]{1,0:T(8,128)S(1)}, f32[376,128]{1,0:T(8,128)S(1)}, u32[]{:S(2)}, u32[]{:S(2)}) collective-permute-start(f32[376,128]{1,0:T(8,128)S(1)} %get-tuple-element.53), channel_id=1, source_target_pairs={{0,31},{1,30},{2,29},{3,28},{4,27},{5,26},{6,25},{7,24},{8,23},{9,... | collective-permute-start | bytes 577544 | tf_op jit(solution)/shard_map/ppermute | solution.py:607
  35.4 16.3 %collective-permute-start.7 = (f32[328,128]{1,0:T(8,128)S(1)}, f32[328,128]{1,0:T(8,128)S(1)}, u32[]{:S(2)}, u32[]{:S(2)}) collective-permute-start(f32[328,128]{1,0:T(8,128)S(1)} %get-tuple-element.67), channel_id=1, source_target_pairs={{0,31},{1,30},{2,29},{3,28},{4,27},{5,26},{6,25},{7,24},{8,23},{9,... | collective-permute-start | bytes 503816 | tf_op jit(solution)/shard_map/ppermute | solution.py:607
  38.6 8.4 %collective-permute-start.5 = (f32[200,128]{1,0:T(8,128)S(1)}, f32[200,128]{1,0:T(8,128)S(1)}, u32[]{:S(2)}, u32[]{:S(2)}) collective-permute-start(f32[200,128]{1,0:T(8,128)S(1)} %get-tuple-element.56), channel_id=1, source_target_pairs={{0,1},{1,0},{2,3},{3,2},{4,5},{5,4},{6,7},{7,6},{8,9},{9,8},{10,11... | collective-permute-start | bytes 307208 | tf_op jit(solution)/shard_map/ppermute | solution.py:607
  38.6 8.3 %collective-permute-start.6 = (f32[200,128]{1,0:T(8,128)S(1)}, f32[200,128]{1,0:T(8,128)S(1)}, u32[]{:S(2)}, u32[]{:S(2)}) collective-permute-start(f32[200,128]{1,0:T(8,128)S(1)} %get-tuple-element.57), channel_id=1, source_target_pairs={{0,31},{1,2},{2,1},{3,4},{4,3},{5,6},{6,5},{7,8},{8,7},{9,10},{10,... | collective-permute-start | bytes 307208 | tf_op jit(solution)/shard_map/ppermute | solution.py:607
  42.3 9.4 %collective-permute-start.8 = (f32[328,128]{1,0:T(8,128)S(1)}, f32[328,128]{1,0:T(8,128)S(1)}, u32[]{:S(2)}, u32[]{:S(2)}) collective-permute-start(f32[328,128]{1,0:T(8,128)S(1)} %get-tuple-element.68), channel_id=1, source_target_pairs={{0,31},{1,30},{2,29},{3,28},{4,27},{5,26},{6,25},{7,24},{8,23},{9,... | collective-permute-start | bytes 503816 | tf_op jit(solution)/shard_map/ppermute | solution.py:607
  47.2 7.8 %collective-permute-start.9 = (f32[200,128]{1,0:T(8,128)S(1)}, f32[200,128]{1,0:T(8,128)S(1)}, u32[]{:S(2)}, u32[]{:S(2)}) collective-permute-start(f32[200,128]{1,0:T(8,128)S(1)} %shard_map.64), channel_id=1, source_target_pairs={{0,31},{1,30},{2,29},{3,28},{4,27},{5,26},{6,25},{7,24},{8,23},{9,... | collective-permute-start | bytes 307208 | tf_op jit(solution)/shard_map/ppermute | solution.py:607
